TPU v7x, 32 devices: a whole 2x2x4 slice. The times are simulated.
32 devices in a mesh: gx: 4 (over z), gy: 2 (over x), gz: 4 (over y, core).
Axes of the slice: x: 2, y: 2, z: 4, core: 2. Of those that a mesh axis runs over, the one named last changes fastest.
Arguments:
- final_adjoint: float32 [9, 56, 4096], P(None, None, ('gx', 'gy', 'gz')), may hold values from -6 to 6
- star_mats: float32 [3, 9, 9, 4096], P(None, None, None, ('gx', 'gy', 'gz')), may hold values from -6 to 6
- deriv_stiff: float32 [3, 56, 56], replicated, may hold values from -6 to 6
- volume_stiffness: float32 [3, 56, 56], replicated, may hold values from -0.21875 to 0.21875
- face_projection: float32 [4, 21, 56], replicated, may hold values from -0.75 to 0.75
- flux_local: float32 [4, 9, 9, 4096], P(None, None, None, ('gx', 'gy', 'gz')), may hold values from -0.875 to 0.875
- flux_across: float32 [4, 9, 9, 4096], P(None, None, None, ('gx', 'gy', 'gz')), may hold values from -0.875 to 0.875
- cluster: int32 [4096], P(('gx', 'gy', 'gz')), may hold values from 0 to 1, as said below
- partner: int32 [4, 4096], P(None, ('gx', 'gy', 'gz')), may hold values from 0 to 703, as said below
- send_slots: int32 [6, 1024], P(None, ('gx', 'gy', 'gz')), may hold values from 0 to 511, as said below
Outputs:
- initial_adjoint: float32 [9, 56, 4096], P(None, None, ('gx', 'gy', 'gz'))
Inputs may be any that keep to these rules, and one draw needn't show every extreme that they name: At most 64 of a partition's elements have cluster 0, some partition has exactly 64, and every partition has at least three sixteenths of 128. `send_slots`: row d of a partition lists 32 distinct face slots c * 128 + e lying on its boundary toward direction d; no slot is in two rows. At most 16 slots of a row belong to cluster-0 elements, and some row of some partition has exactly 16. partner[c, e] = 512 + d * 32 + j exactly when send_slots[d, j] of the partition is c * 128 + e; every other slot's partner is another slot of the same partition below 512 whose partner is it.
All inputs are finite; a program needn't handle non-finite values.
Results may differ from a plain program's by a relative error of at most 0.0003.
Values sent between devices are 32-bit elements; how exact they have to be, the bound alone decides.
No kernel may reach another device: no remote copies, remote signals or barrier semaphores. Data moves between devices by JAX's collectives and lax.ppermute only.
A program may use at most 64 MiB of HBM per device.

v0:
```python
import functools
import math

import jax
import jax.numpy as jnp
from jax import lax
from jax.experimental import pallas as pl
from jax.experimental.pallas import tpu as pltpu
from jax.sharding import PartitionSpec as P

TERMS = 6
FINE_STEPS = 4
BF = jnp.bfloat16
F32 = jnp.float32


def up(n, unit):
    return -(-n // unit) * unit


AXES = ("gx", "gy", "gz")


def matchings():
    plan = []
    for axis in AXES:
        size = lax.axis_size(axis)
        for first in (0, 1):
            links = [(i, i + 1) for i in range(first, size - 1, 2)]
            if not links:
                continue
            if first == 1 and size % 2 == 0:
                links.append((size - 1, 0))
            plan.append((axis, [q for i, j in links for q in ((i, j), (j, i))], first))
    return plan


def bearings(plan):
    upward, block = [], [jnp.int32(-1)] * 6
    for number, (axis, _, first) in enumerate(plan):
        a, place, size = AXES.index(axis), lax.axis_index(axis), lax.axis_size(axis)
        rises = lax.rem(place, 2) == first
        upward.append((a, rises))
        for side in (0, 1):
            inside = (place > 0) if side == 0 else (place < size - 1)
            used = jnp.logical_and(rises if side == 1 else jnp.logical_not(rises), inside)
            block[2 * a + side] = jnp.where(used, number, block[2 * a + side])
    return upward, block


def coefficients(lower, upper):
    return [(upper ** (k + 1) - lower ** (k + 1)) / math.factorial(k + 1) for k in range(TERMS)]


def halves(x):
    hi = x.astype(BF)
    return hi, (x - hi.astype(F32)).astype(BF)


def dot(a, b):
    return jnp.dot(a, b, preferred_element_type=F32)


class Sizes:
    def __init__(self, fields, modes, faces, bases, members, width, messages):
        self.F, self.M, self.C, self.B, self.E = fields, modes, faces, bases, members
        self.W, self.K = width, messages
        self.H = members // 2
        self.FP = up(fields, 2) // 2
        self.MP = up(modes, 64)
        self.BP = up(bases, 8)
        self.BQ = up(bases, 16)
        self.R = fields * self.BP
        self.RP = up(self.R, 16)
        self.Q = members // width
        self.QR = up(up(self.R, 8 * self.Q) // self.Q, 8)
        self.KW = up(messages * width, 128)
        self.S = faces * members


def filled(x, rows):
    if x.shape[0] == rows:
        return x
    return jnp.concatenate([x, jnp.zeros((rows - x.shape[0], x.shape[1]), x.dtype)], axis=0)


def put_field(z, y3, f, x):
    hi, lo = halves(filled(x, z.MP))
    lanes = slice(f * z.E, (f + 1) * z.E)
    y3[0:z.MP, lanes] = hi
    y3[z.MP:2 * z.MP, lanes] = lo
    y3[2 * z.MP:3 * z.MP, lanes] = hi


def put_face(z, u, c, lanes, hi, lo):
    for part, value in enumerate((hi, lo, hi)):
        at = (part * z.C + c) * z.BQ
        u[at:at + z.BQ, lanes] = value


def lane(z, i):
    return slice(i * z.E, (i + 1) * z.E)


def take(x, row):
    return jnp.take_along_axis(x, jnp.broadcast_to(row, x.shape), axis=1)


def low_lanes(z, rows):
    return lax.broadcasted_iota(jnp.int32, (rows, z.E), 1) < z.H


def fold(z, first, second):
    low = low_lanes(z, first.shape[0])
    second = jnp.zeros_like(first) if second is None else second
    return jnp.where(low, first, second) + pltpu.roll(jnp.where(low, second, first), z.H, 1)


def compact(z, pick, field):
    low = low_lanes(z, z.M)
    out = []
    for p in range(z.FP):
        a = take(field(2 * p), pick)
        b = take(field(2 * p + 1), pick) if 2 * p + 1 < z.F else jnp.zeros_like(a)
        out.append(jnp.where(low, a, b))
    return out


def expand(z, rank, pairs, f):
    return take(pairs(f // 2), rank + z.H * (f % 2))


def star_sum(z, start, group, turned, star, count):
    total = list(start)
    for f in range(count):
        for d in range(3):
            t = turned[d * z.M:(d + 1) * z.M, lane(z, f)]
            for i, g in enumerate(group):
                term = star[g, f, d:d + 1, :] * t
                total[i] = term if total[i] is None else total[i] + term
    return total


def star_pair(z, p, turned, star):
    group = [g for g in (2 * p, 2 * p + 1) if g < z.F]
    total = star_sum(z, [None] * len(group), group, turned, star, z.FP)
    return fold(z, total[0], total[1] if len(group) == 2 else None)


def face_sum(z, flux, g, c, t):
    total = flux[g, 0, c:c + 1, :] * t[0]
    for f in range(1, len(t)):
        total = total + flux[g, f, c:c + 1, :] * t[f]
    return total


def face_rows(z, traces, c, count):
    return [traces[c * z.BP:(c + 1) * z.BP, lane(z, f)] for f in range(count)]


def groups_of(n, size):
    return [list(range(i, min(n, i + size))) for i in range(0, n, size)]


def pack_messages(z, sent, ohs, sx, messages, picked):
    hi, lo = halves(sent[...])
    sx[0:z.R, :] = hi
    sx[z.RP:z.RP + z.R, :] = lo
    both = dot(sx[...], ohs[...])
    picked[...] = both[0:z.R, :] + both[z.RP:z.RP + z.R, :]
    for m, message in enumerate(messages):
        for q in range(z.Q):
            rows = min(z.R, (q + 1) * z.QR) - q * z.QR
            lanes = slice(q * z.W, (q + 1) * z.W)
            message[0:rows, lanes] = picked[q * z.QR:q * z.QR + rows, m * z.W:(m + 1) * z.W]
            if rows < z.QR:
                message[rows:z.QR, lanes] = jnp.zeros((z.QR - rows, z.W), F32)


def triple(rows, cols, target, wide, matrix):
    hi = matrix.astype(BF).astype(F32)
    wide[rows, 0:cols] = hi
    wide[rows, cols:2 * cols] = hi
    wide[rows, 2 * cols:3 * cols] = matrix - hi
    target[rows, :] = wide[rows, 0:3 * cols].astype(BF)


def first_kernel(z, plan, *refs):
    n = 10
    hbm, refs = refs[:n], refs[n:]
    (y, star, local, across, deriv, volume, partner, cluster, p3, square, ohs, y3, traces, sx), refs = refs[:14], refs[14:]
    messages, refs = refs[:z.K], refs[z.K:]
    projection, slots, sent, picked, picks, wide, sem = refs
    targets = (y, projection, slots, across, star, local, deriv, volume, partner, cluster)
    copies = [pltpu.make_async_copy(a, b, sem.at[i]) for i, (a, b) in enumerate(zip(hbm, targets))]
    for copy in copies:
        copy.start()
    square[...] = jnp.zeros_like(square)
    wide[...] = jnp.zeros_like(wide)
    picks[...] = jnp.full_like(picks, -1)
    upward, _ = bearings(plan)
    copies[2].wait()
    for m, (a, rises) in enumerate(upward):
        picks[0:1, m * z.W:(m + 1) * z.W] = jnp.where(rises, slots[2 * a + 1:2 * a + 2, :], slots[2 * a:2 * a + 1, :])
    ids = lax.broadcasted_iota(jnp.int32, (z.S, z.KW), 0)
    ohs[...] = jnp.where(ids == picks[0:1, :], 1.0, 0.0).astype(BF)
    copies[1].wait()
    for c in range(z.C):
        for b in range(z.B):
            square[c * z.BQ + b:c * z.BQ + b + 1, 0:z.M] = projection[b, c:c + 1, :]
    for c in range(z.C):
        rows = slice(c * z.BP, (c + 1) * z.BP)
        triple(rows, z.MP, p3, wide, square[c * z.BQ:c * z.BQ + z.BP, 0:z.MP])
    copies[0].wait()
    for f in range(z.F):
        put_field(z, y3, f, y[f * z.M:(f + 1) * z.M, :])
    traces[...] = dot(p3[...], y3[...])
    copies[3].wait()
    for c in range(z.C):
        t = face_rows(z, traces, c, z.F)
        for g in range(z.F):
            sent[g * z.BP:(g + 1) * z.BP, lane(z, c)] = face_sum(z, across, g, c, t)
    pack_messages(z, sent, ohs, sx, messages, picked)
    for copy in copies[4:]:
        copy.wait()


def set_up(z, plan, deriv, volume, square, partner, cluster, ohs, star, across, local, outs, scratch):
    s3, v3, pt, ohr, ohl, ohs_half, ohl_half, index, star_pairs, across_pairs, local_pairs = outs
    wide, block, picks = scratch
    wide[...] = jnp.zeros_like(wide)
    block[...] = jnp.zeros_like(block)
    for source, target in ((deriv, s3), (volume, v3)):
        for d in range(3):
            block[0:z.M, 0:z.M] = source[d]
            turned = jnp.transpose(block[...])
            triple(slice(d * z.M, (d + 1) * z.M), z.MP, target, wide, turned[0:z.M, 0:z.MP])
    triple(slice(0, z.M), z.C * z.BQ, pt, wide, jnp.transpose(square[...])[0:z.M, 0:z.C * z.BQ])
    _, arrival = bearings(plan)
    far = partner[...] - z.S
    moved = jnp.full_like(far, -1)
    for i in range(6):
        here = jnp.logical_and(far >= i * z.W, far < (i + 1) * z.W)
        here = jnp.logical_and(here, arrival[i] >= 0)
        moved = jnp.where(here, arrival[i] * z.W + far - i * z.W, moved)
    slots = partner[...]
    for c in range(z.C):
        ids = lax.broadcasted_iota(jnp.int32, (z.S, z.E), 0)
        ohl[:, lane(z, c)] = jnp.where(ids == slots[c:c + 1, :], 1.0, 0.0).astype(BF)
        ids = lax.broadcasted_iota(jnp.int32, (z.KW, z.E), 0)
        ohr[:, lane(z, c)] = jnp.where(ids == moved[c:c + 1, :], 1.0, 0.0).astype(BF)
    fast = cluster[...] == 0
    flags = jnp.broadcast_to(jnp.where(fast, 1.0, 0.0), (8, z.E))
    a = lax.broadcasted_iota(jnp.int32, (z.E, z.E), 0)
    b = lax.broadcasted_iota(jnp.int32, (z.E, z.E), 1)
    below = jnp.where(a <= b, 1.0, 0.0).astype(BF)
    running = dot(flags.astype(BF), below)
    count = dot(flags.astype(BF), jnp.ones((z.E, z.E), BF))
    rank = running[0:1, :].astype(jnp.int32) - 1
    held = jnp.where(fast, rank, -1)
    chosen = jnp.where(lax.broadcasted_iota(jnp.int32, (z.H, z.E), 0) == held, 1.0, 0.0).astype(BF)
    numbers = lax.broadcasted_iota(jnp.int32, (8, z.E), 1).astype(F32).astype(BF)
    listed = lax.dot_general(numbers, chosen, (((1,), (1,)), ((), ())), preferred_element_type=F32)
    picks[:, 0:z.H] = listed
    picks[:, z.H:2 * z.H] = listed
    pick = picks[0:1, :].astype(jnp.int32)
    place = lax.broadcasted_iota(jnp.int32, (1, z.E), 1)
    place = jnp.where(place < z.H, place, place - z.H)
    live = place < count[0:1, :].astype(jnp.int32)
    index[...] = jnp.zeros_like(index)
    index[0:1, :] = pick
    index[1:2, :] = jnp.maximum(rank, 0)
    index[2:3, :] = jnp.where(fast, 1, 0)
    for c in range(z.C):
        rows = slice(c * z.H, (c + 1) * z.H)
        ohs_half[rows, :] = dot(chosen, ohs[lane(z, c), :]).astype(BF)
        ohl_half[rows, :] = dot(chosen, ohl[lane(z, c), :]).astype(BF)
    for source, target in ((star, star_pairs), (across, across_pairs), (local, local_pairs)):
        low = jnp.logical_and(low_lanes(z, 1), live)
        high = jnp.logical_and(jnp.logical_not(low_lanes(z, 1)), live)
        for g in range(z.F):
            for p in range(z.FP):
                value = jnp.where(low, take(source[g, 2 * p], pick), 0.0)
                if 2 * p + 1 < z.F:
                    value = jnp.where(high, take(source[g, 2 * p + 1], pick), value)
                target[g, p] = value


def first_local_kernel(z, plan, *refs):
    deriv, volume, square, partner, cluster, ohs, star, across, local, y3, traces, sx = refs[:12]
    outs, src, refs = refs[12:23], refs[23], refs[24:]
    turned, u, gathered, *scratch = refs
    set_up(z, plan, deriv, volume, square, partner, cluster, ohs, star, across, local, outs, scratch)
    v3, pt, ohl = outs[1], outs[2], outs[4]
    turned[...] = dot(v3[...], y3[...])
    gathered[...] = dot(sx[...], ohl[...])
    for c in range(z.C):
        t = face_rows(z, traces, c, z.F)
        for g in range(z.F):
            total = gathered[g * z.BP:(g + 1) * z.BP, lane(z, c)] + gathered[z.RP + g * z.BP:z.RP + (g + 1) * z.BP, lane(z, c)]
            hi, lo = halves(filled(total + face_sum(z, local, g, c, t), z.BQ))
            put_face(z, u, c, lane(z, g), hi, lo)
    lifted = dot(pt[...], u[...])
    for group in groups_of(z.F, 3):
        start = [lifted[:, lane(z, g)] for g in group]
        for g, total in zip(group, star_sum(z, start, group, turned, star, z.F)):
            src[g * z.M:(g + 1) * z.M, :] = total


def lift_gathered(z, gathered, u, pt):
    for c in range(z.C):
        for g in range(z.F):
            hi = filled(gathered[g * z.BP:(g + 1) * z.BP, lane(z, c)], z.BQ).astype(BF)
            lo = filled(gathered[z.RP + g * z.BP:z.RP + (g + 1) * z.BP, lane(z, c)], z.BQ).astype(BF)
            put_face(z, u, c, lane(z, g), hi, lo)
    return dot(pt[...], u[...])


def local_kernel(z, last, *refs):
    y3, traces, sx, v3, pt, star, local, ohl, index, src_in, half_in = refs[:11]
    refs = refs[11:]
    if last:
        older, start, moved, refs = refs[0:2], refs[2], refs[3], refs[4:]
        src_out, weights, base, refs = refs[0], refs[1], refs[2], refs[3:]
        half_out = refs[0]
        refs = refs[1:]
    else:
        src_out, half_out, refs = refs[0], refs[1], refs[2:]
    turned, u, gathered, u_half, lifted = refs
    turned[...] = dot(v3[...], y3[...])
    gathered[...] = dot(sx[...], ohl[...])
    for c in range(z.C):
        t = face_rows(z, traces, c, z.FP)
        for p in range(z.FP):
            first = face_sum(z, local, 2 * p, c, t)
            second = face_sum(z, local, 2 * p + 1, c, t) if 2 * p + 1 < z.F else None
            hi, lo = halves(filled(fold(z, first, second), z.BQ))
            put_face(z, u_half, c, lane(z, p), hi, lo)
    lifted_half = dot(pt[...], u_half[...])
    lifted[...] = lift_gathered(z, gathered, u, pt)
    pick, rank = index[0:1, :], index[1:2, :]
    gained = compact(z, pick, lambda f: lifted[:, lane(z, f)])
    for p in range(z.FP):
        rows = slice(p * z.M, (p + 1) * z.M)
        half_out[rows, :] = half_in[rows, :] + gained[p] + lifted_half[:, lane(z, p)] + star_pair(z, p, turned, star)
    fast = index[2:3, :] > 0
    for g in range(z.F):
        rows = slice(g * z.M, (g + 1) * z.M)
        value = src_in[rows, :] + lifted[:, lane(z, g)]
        if last:
            pairs = lambda p: half_out[p * z.M:(p + 1) * z.M, :]
            src_out[rows, :] = jnp.where(fast, expand(z, rank, pairs, g), value)
            pairs = lambda p: moved[p * z.M:(p + 1) * z.M, :]
            base[rows, :] = start[rows, :] + jnp.where(fast, expand(z, rank, pairs, g), 0.0)
            sources = [x[rows, :] for x in older] + [src_in[rows, :]]
            sources = [jnp.where(fast, 0.0, x) for x in sources]
            for k in range(TERMS):
                total = None
                for step, x in zip(range(FINE_STEPS - 1, 0, -1), sources):
                    c = coefficients(step / FINE_STEPS, (step + 1) / FINE_STEPS)[k]
                    total = c * x if total is None else total + c * x
                weights[k, rows, :] = total
        else:
            src_out[rows, :] = value


def arrive(z, arrived, ohr, pt, landed, stacked, gathered, u):
    used = z.K * z.W // 128 * 128
    if used < z.KW:
        landed[:, used:z.KW] = jnp.zeros((z.R, z.KW - used), F32)
    for m in range(z.K):
        for q in range(z.Q):
            rows = min(z.R, (q + 1) * z.QR) - q * z.QR
            landed[q * z.QR:q * z.QR + rows, m * z.W:(m + 1) * z.W] = arrived[m][0:rows, q * z.W:(q + 1) * z.W]
    hi, lo = halves(landed[...])
    stacked[0:z.R, :] = hi
    stacked[z.RP:z.RP + z.R, :] = lo
    gathered[...] = dot(stacked[...], ohr[...])
    return lift_gathered(z, gathered, u, pt)


def step_kernel(z, first, *refs):
    arrived, refs = refs[:z.K], refs[z.K:]
    src_in, half_in, moved_in, s3, p3, pt, star, across, ohr, ohs, index = refs[:11]
    src_out, half, moved, y3, traces, sx = refs[11:17]
    messages, refs = refs[17:17 + z.K], refs[17 + z.K:]
    landed, stacked, gathered, u, lifted, turned, change, sent, picked = refs
    lifted[...] = arrive(z, arrived, ohr, pt, landed, stacked, gathered, u)
    for g in range(z.F):
        rows = slice(g * z.M, (g + 1) * z.M)
        src_out[rows, :] = src_in[rows, :] + lifted[:, lane(z, g)]
    if first:
        gained = compact(z, index[0:1, :], lambda f: src_out[f * z.M:(f + 1) * z.M, :])
    else:
        gained = compact(z, index[0:1, :], lambda f: lifted[:, lane(z, f)])
    row = coefficients(0.0, 1.0 / FINE_STEPS)
    for p in range(z.FP):
        rows = slice(p * z.M, (p + 1) * z.M)
        value = gained[p] if first else half_in[rows, :] + gained[p]
        half[rows, :] = value
        put_field(z, y3, p, row[TERMS - 1] * value)

    def term(i, carry):
        c = F32(row[TERMS - 2])
        for k in range(TERMS - 2):
            c = jnp.where(i == TERMS - 2 - k, F32(row[k]), c)
        turned[...] = dot(s3[...], y3[...])
        for p in range(z.FP):
            rows = slice(p * z.M, (p + 1) * z.M)
            total = c * half[rows, :] + star_pair(z, p, turned, star)
            put_field(z, y3, p, total)
            change[rows, :] = total
        return carry

    lax.fori_loop(0, TERMS - 1, term, 0)
    moved[...] = change[...] if first else moved_in[...] + change[...]
    traces[...] = dot(p3[...], y3[...])
    for pair in groups_of(z.C, 2):
        t = [face_rows(z, traces, c, z.FP) for c in pair]
        for g in range(z.F):
            total = fold(z, *[face_sum(z, across, g, c, t[i]) for i, c in enumerate(pair)])
            sent[g * z.BP:(g + 1) * z.BP, lane(z, pair[0] // 2)] = total
    pack_messages(z, sent, ohs, sx, messages, picked)


def last_kernel(z, *refs):
    arrived, refs = refs[:z.K], refs[z.K:]
    src_in, weights, base, s3, pt, star, ohr, out = refs[:8]
    landed, stacked, gathered, u, lifted, turned, y3, src = refs[8:]
    lifted[...] = arrive(z, arrived, ohr, pt, landed, stacked, gathered, u)
    row = coefficients(0.0, 1.0 / FINE_STEPS)
    for g in range(z.F):
        rows = slice(g * z.M, (g + 1) * z.M)
        value = src_in[rows, :] + lifted[:, lane(z, g)]
        src[rows, :] = value
        put_field(z, y3, g, weights[TERMS - 1, rows, :] + row[TERMS - 1] * value)

    def term(i, carry):
        c = F32(row[TERMS - 2])
        for k in range(TERMS - 2):
            c = jnp.where(i == TERMS - 2 - k, F32(row[k]), c)
        turned[...] = dot(s3[...], y3[...])
        for group in groups_of(z.F, 3):
            start = [weights[TERMS - 2 - i, g * z.M:(g + 1) * z.M, :] + c * src[g * z.M:(g + 1) * z.M, :] for g in group]
            for g, total in zip(group, star_sum(z, start, group, turned, star, z.F)):
                put_field(z, y3, g, total)
                out[g * z.M:(g + 1) * z.M, :] = total
        return carry

    lax.fori_loop(0, TERMS - 1, term, 0)
    out[...] = out[...] + base[...]


def call(kernel, outs, scratch, *args, remote=False):
    place = pl.BlockSpec(memory_space=pltpu.HBM if remote else pltpu.VMEM)
    if remote:
        args = [pltpu.with_memory_space_constraint(x, pltpu.HBM) for x in args]
    vmem = pl.BlockSpec(memory_space=pltpu.VMEM)
    return pl.pallas_call(
        kernel,
        out_shape=[jax.ShapeDtypeStruct(*o) for o in outs],
        in_specs=[place] * len(args),
        out_specs=[vmem] * len(outs),
        scratch_shapes=[pltpu.VMEM(*o) if isinstance(o, tuple) else o for o in scratch],
        compiler_params=pltpu.CompilerParams(vmem_limit_bytes=24 << 20),
        cost_estimate=pl.CostEstimate(flops=1 << 30, bytes_accessed=2 << 20, transcendentals=0),
    )(*args)


def body(
    final_adjoint,
    star_mats,
    deriv_stiff,
    volume_stiffness,
    face_projection,
    flux_local,
    flux_across,
    cluster,
    partner,
    send_slots,
):
    fields, modes, members = final_adjoint.shape
    faces, bases, _ = face_projection.shape
    plan = matchings()
    width = send_slots.shape[1]
    z = Sizes(fields, modes, faces, bases, members, width, len(plan))

    full, half = ((fields * modes, members), F32), ((z.FP * modes, members), F32)
    y3, y3_half = ((3 * z.MP, fields * members), BF), ((3 * z.MP, z.FP * members), BF)
    traces, traces_half = ((faces * z.BP, fields * members), F32), ((faces * z.BP, z.FP * members), F32)
    turned, turned_half = ((3 * modes, fields * members), F32), ((3 * modes, z.FP * members), F32)
    u, u_half = ((3 * faces * z.BQ, fields * members), BF), ((3 * faces * z.BQ, z.FP * members), BF)
    gathered, lifted = ((2 * z.RP, z.S), F32), ((modes, fields * members), F32)
    landed, stacked = ((z.R, z.KW), F32), ((2 * z.RP, z.KW), BF)
    sx, sx_half = ((2 * z.RP, z.S), BF), ((2 * z.RP, z.S // 2), BF)
    sent, sent_half, picked = ((z.R, z.S), F32), ((z.R, z.S // 2), F32), ((z.R, z.KW), F32)
    messages_out = [((z.QR, members), F32)] * z.K
    wide = ((3 * modes, up(3 * max(z.MP, faces * z.BQ), 128)), F32)
    pairs = lambda n: ((fields, z.FP, n, members), F32)

    def trade(messages):
        return [lax.ppermute(m, axis, links) for m, (axis, links, _) in zip(messages, plan)]

    star = jnp.transpose(star_mats, (1, 2, 0, 3))
    local = jnp.transpose(flux_local, (1, 2, 0, 3))
    across = jnp.transpose(flux_across, (1, 2, 0, 3))
    args = [
        final_adjoint.reshape(fields * modes, members), jnp.transpose(face_projection, (1, 0, 2)), send_slots, across,
        star, local, deriv_stiff, volume_stiffness, partner, cluster.reshape(1, members),
    ]
    like = lambda x: (x.shape, x.dtype)
    (start, star, local, across, deriv, volume, partner, cluster, p3, square, ohs, y3v, tr, sxv, *messages) = call(
        functools.partial(first_kernel, z, plan),
        [like(args[i]) for i in (0, 4, 5, 3, 6, 7, 8, 9)]
        + [((faces * z.BP, 3 * z.MP), BF), ((128, 128), F32), ((z.S, z.KW), BF), y3, traces, sx] + messages_out,
        [like(args[1]), like(args[2]), sent, picked, ((8, z.KW), jnp.int32), wide, pltpu.SemaphoreType.DMA((len(args),))],
        *args, remote=True,
    )
    arrived = trade(messages)
    s3, v3, pt, ohr, ohl, ohs_half, ohl_half, index, star_pairs, across_pairs, local_pairs, src = call(
        functools.partial(first_local_kernel, z, plan),
        [((3 * modes, 3 * z.MP), BF), ((3 * modes, 3 * z.MP), BF), ((modes, 3 * faces * z.BQ), BF), ((z.KW, z.S), BF),
         ((z.S, z.S), BF), ((z.S // 2, z.KW), BF), ((z.S // 2, z.S), BF), ((8, members), jnp.int32),
         pairs(3), pairs(faces), pairs(faces), full],
        [turned, u, gathered, wide, ((128, 128), F32), ((8, members), F32)],
        deriv, volume, square, partner, cluster, ohs, star, across, local, y3v, tr, sxv,
    )
    half_src = moved = jnp.zeros((8, members), F32)
    sources = []
    for step in range(FINE_STEPS - 1, 0, -1):
        src, half_src, moved, y3v, tr, sxv, *messages = call(
            functools.partial(step_kernel, z, step == FINE_STEPS - 1),
            [full, half, half, y3_half, traces_half, sx_half] + messages_out,
            [landed, stacked, gathered, u, lifted, turned_half, half, sent_half, picked],
            *arrived, src, half_src, moved, s3, p3, pt, star_pairs, across_pairs, ohr, ohs_half, index,
        )
        arrived = trade(messages)
        sources.append(src)
        last = step == 1
        local_args = [y3v, tr, sxv, v3, pt, star_pairs, local_pairs, ohl_half, index, src, half_src]
        local_scratch = [turned_half, u, gathered, u_half, lifted]
        if last:
            src, weights, base, _ = call(
                functools.partial(local_kernel, z, True), [full, ((TERMS,) + full[0], F32), full, half], local_scratch,
                *local_args, *sources[:2], start, moved,
            )
        else:
            src, half_src = call(functools.partial(local_kernel, z, False), [full, half], local_scratch, *local_args)
    (out,) = call(
        functools.partial(last_kernel, z), [full],
        [landed, stacked, gathered, u, lifted, turned, y3, full],
        *arrived, src, weights, base, s3, pt, star, ohr,
    )
    return out.reshape(fields, modes, members)


def solution(mesh):
    in_specs = (
        P(None, None, ("gx", "gy", "gz")),
        P(None, None, None, ("gx", "gy", "gz")),
        P(),
        P(),
        P(),
        P(None, None, None, ("gx", "gy", "gz")),
        P(None, None, None, ("gx", "gy", "gz")),
        P(("gx", "gy", "gz")),
        P(None, ("gx", "gy", "gz")),
        P(None, ("gx", "gy", "gz")),
    )
    out_specs = P(None, None, ("gx", "gy", "gz"))
    return jax.shard_map(body, mesh=mesh, in_specs=in_specs, out_specs=out_specs, check_vma=False)
```

profile of v0, /device:TPU:1, one launch (start us, length us, event | category | flops | bytes accessed | tf_op | source)
XLA Modules:
  0.0 51.2 jit_solution(5329200768350012778)
XLA Ops:
  0.0 2.2 %shard_map.100 = (f32[504,128]{1,0:T(8,128)S(1)}, f32[9,9,3,128]{3,2,1,0:T(4,128)S(1)}, f32[9,9,4,128]{3,2,1,0:T(4,128)S(1)}, f32[9,9,4,128]{3,2,1,0:T(4,128)S(1...) custom-call(f32[504,128]{1,0:T(8,128)} %bitcast.7, ...), custom_call_target="tpu_custom_call" | custom-call | flops 1073741824 | bytes 2097152 | tf_op jit(solution)/shard_map/pallas_call | solution.py:459
  2.2 2.2 %collective-permute-start = (f32[56,128]{1,0:T(8,128)S(1)}, f32[56,128]{1,0:T(8,128)S(1)}, u32[]{:S(2)}, u32[]{:S(2)}) collective-permute-start(f32[56,128]{1,0:T(8,128)S(1)} %get-tuple-element.75), channel_id=1, source_target_pairs={{0,8},{8,0},{16,24},{24,16},{1,9},{9,1},{17,25},{25,17},{2,10},{10... | collective-permute-start | bytes 86024 | tf_op jit(solution)/shard_map/ppermute | solution.py:502
  4.4 2.2 %collective-permute-start.1 = (f32[56,128]{1,0:T(8,128)S(1)}, f32[56,128]{1,0:T(8,128)S(1)}, u32[]{:S(2)}, u32[]{:S(2)}) collective-permute-start(f32[56,128]{1,0:T(8,128)S(1)} %get-tuple-element.76), channel_id=1, source_target_pairs={{8,16},{16,8},{24,0},{0,24},{9,17},{17,9},{25,1},{1,25},{10,18},{1... | collective-permute-start | bytes 86024 | tf_op jit(solution)/shard_map/ppermute | solution.py:502
  6.6 1.2 %collective-permute-start.2 = (f32[56,128]{1,0:T(8,128)S(1)}, f32[56,128]{1,0:T(8,128)S(1)}, u32[]{:S(2)}, u32[]{:S(2)}) collective-permute-start(f32[56,128]{1,0:T(8,128)S(1)} %get-tuple-element.77), channel_id=1, source_target_pairs={{0,4},{4,0},{1,5},{5,1},{2,6},{6,2},{3,7},{7,3},{8,12},{12,8},{9,1... | collective-permute-start | bytes 86024 | tf_op jit(solution)/shard_map/ppermute | solution.py:502
  7.8 1.5 %collective-permute-start.3 = (f32[56,128]{1,0:T(8,128)S(1)}, f32[56,128]{1,0:T(8,128)S(1)}, u32[]{:S(2)}, u32[]{:S(2)}) collective-permute-start(f32[56,128]{1,0:T(8,128)S(1)} %get-tuple-element.78), channel_id=1, source_target_pairs={{0,1},{1,0},{2,3},{3,2},{4,5},{5,4},{6,7},{7,6},{8,9},{9,8},{10,11... | collective-permute-start | bytes 86024 | tf_op jit(solution)/shard_map/ppermute | solution.py:502
  9.3 1.1 %collective-permute-start.4 = (f32[56,128]{1,0:T(8,128)S(1)}, f32[56,128]{1,0:T(8,128)S(1)}, u32[]{:S(2)}, u32[]{:S(2)}) collective-permute-start(f32[56,128]{1,0:T(8,128)S(1)} %get-tuple-element.79), channel_id=1, source_target_pairs={{1,2},{2,1},{3,0},{0,3},{5,6},{6,5},{7,4},{4,7},{9,10},{10,9},{11,... | collective-permute-start | bytes 86024 | tf_op jit(solution)/shard_map/ppermute | solution.py:502
  10.4 1.9 %shard_map.101 = (bf16[168,192]{1,0:T(8,128)(2,1)S(1)}, bf16[168,192]{1,0:T(8,128)(2,1)S(1)}, bf16[56,384]{1,0:T(8,128)(2,1)S(1)}, bf16[256,512]{1,0:T(8,128)(2,...) custom-call(f32[3,56,56]{2,1,0:T(8,128)S(1)} %get-tuple-element.80.r, ...), custom_call_target="tpu_custom_call" | custom-call | flops 1073741824 | bytes 2097152 | tf_op jit(solution)/shard_map/pallas_call | solution.py:459
  12.6 4.3 %shard_map.102 = (f32[504,128]{1,0:T(8,128)S(1)}, f32[280,128]{1,0:T(8,128)S(1)}, f32[280,128]{1,0:T(8,128)S(1)}, bf16[192,640]{1,0:T(8,128)(2,1)S(1)}, f32[96,6...) custom-call(f32[56,128]{1,0:T(8,128)S(1)} %collective-permute-done.r, ...), custom_call_target="tpu_custom_call" | custom-call | flops 1073741824 | bytes 2097152 | tf_op jit(solution)/shard_map/pallas_call | solution.py:459
  16.9 0.5 collective-permute-start.5
  17.3 0.8 %collective-permute-start.6 = (f32[56,128]{1,0:T(8,128)S(1)}, f32[56,128]{1,0:T(8,128)S(1)}, u32[]{:S(2)}, u32[]{:S(2)}) collective-permute-start(f32[56,128]{1,0:T(8,128)S(1)} %get-tuple-element.102), channel_id=1, source_target_pairs={{8,16},{16,8},{24,0},{0,24},{9,17},{17,9},{25,1},{1,25},{10,18},{1... | collective-permute-start | bytes 86024 | tf_op jit(solution)/shard_map/ppermute | solution.py:502
  18.1 0.4 collective-permute-start.7
  18.4 1.0 %collective-permute-start.8 = (f32[56,128]{1,0:T(8,128)S(1)}, f32[56,128]{1,0:T(8,128)S(1)}, u32[]{:S(2)}, u32[]{:S(2)}) collective-permute-start(f32[56,128]{1,0:T(8,128)S(1)} %get-tuple-element.104), channel_id=1, source_target_pairs={{0,1},{1,0},{2,3},{3,2},{4,5},{5,4},{6,7},{7,6},{8,9},{9,8},{10,11... | collective-permute-start | bytes 86024 | tf_op jit(solution)/shard_map/ppermute | solution.py:502
  19.4 1.1 %collective-permute-start.9 = (f32[56,128]{1,0:T(8,128)S(1)}, f32[56,128]{1,0:T(8,128)S(1)}, u32[]{:S(2)}, u32[]{:S(2)}) collective-permute-start(f32[56,128]{1,0:T(8,128)S(1)} %get-tuple-element.105), channel_id=1, source_target_pairs={{1,2},{2,1},{3,0},{0,3},{5,6},{6,5},{7,4},{4,7},{9,10},{10,9},{11,... | collective-permute-start | bytes 86024 | tf_op jit(solution)/shard_map/ppermute | solution.py:502
  20.6 1.1 %shard_map.103 = (f32[504,128]{1,0:T(8,128)S(1)}, f32[280,128]{1,0:T(8,128)S(1)}) custom-call(bf16[192,640]{1,0:T(8,128)(2,1)S(1)} %get-tuple-element.106.refs_0_, f32[96,640]{1,0:T(8,128)S(1)} %get-tuple-element.107.refs_1_, bf16[448,256]{1,0:T(8,128)(2,1)S(1)} %get-tuple-element.108.refs_2_, bf16[168,192]{1,0:T(8,128)(2,1)S(1)} %get-tuple-element.109.refs_3_, ...), custom_call_target="tpu_custom_call" | custom-call | flops 1073741824 | bytes 2097152 | tf_op jit(solution)/shard_map/pallas_call | solution.py:459
  21.9 1.1 %collective-permute-done.9.refs_4_ = f32[56,128]{1,0:T(8,128)S(1)} collective-permute-done((f32[56,128]{1,0:T(8,128)S(1)}, f32[56,128]{1,0:T(8,128)S(1)}, u32[]{:S(2)}, u32[]{:S(2)}) %collective-permute-start.9) | collective-permute-done | bytes 28704 | tf_op jit(solution)/shard_map/ppermute | solution.py:502
  23.0 4.1 %shard_map.104 = (f32[504,128]{1,0:T(8,128)S(1)}, f32[280,128]{1,0:T(8,128)S(1)}, f32[280,128]{1,0:T(8,128)S(1)}, bf16[192,640]{1,0:T(8,128)(2,1)S(1)}, f32[96,6...) custom-call(f32[56,128]{1,0:T(8,128)S(1)} %collective-permute-done.5, ...), custom_call_target="tpu_custom_call" | custom-call | flops 1073741824 | bytes 2097152 | tf_op jit(solution)/shard_map/pallas_call | solution.py:459
  27.1 0.5 %collective-permute-start.10 = (f32[56,128]{1,0:T(8,128)S(1)}, f32[56,128]{1,0:T(8,128)S(1)}, u32[]{:S(2)}, u32[]{:S(2)}) collective-permute-start(f32[56,128]{1,0:T(8,128)S(1)} %get-tuple-element.117), channel_id=1, source_target_pairs={{0,8},{8,0},{16,24},{24,16},{1,9},{9,1},{17,25},{25,17},{2,10},{10... | collective-permute-start | bytes 86024 | tf_op jit(solution)/shard_map/ppermute | solution.py:502
  27.7 2.0 %collective-permute-start.11 = (f32[56,128]{1,0:T(8,128)S(1)}, f32[56,128]{1,0:T(8,128)S(1)}, u32[]{:S(2)}, u32[]{:S(2)}) collective-permute-start(f32[56,128]{1,0:T(8,128)S(1)} %get-tuple-element.118), channel_id=1, source_target_pairs={{8,16},{16,8},{24,0},{0,24},{9,17},{17,9},{25,1},{1,25},{10,18},{1... | collective-permute-start | bytes 86024 | tf_op jit(solution)/shard_map/ppermute | solution.py:502
  29.7 1.2 %collective-permute-start.12 = (f32[56,128]{1,0:T(8,128)S(1)}, f32[56,128]{1,0:T(8,128)S(1)}, u32[]{:S(2)}, u32[]{:S(2)}) collective-permute-start(f32[56,128]{1,0:T(8,128)S(1)} %get-tuple-element.119), channel_id=1, source_target_pairs={{0,4},{4,0},{1,5},{5,1},{2,6},{6,2},{3,7},{7,3},{8,12},{12,8},{9,1... | collective-permute-start | bytes 86024 | tf_op jit(solution)/shard_map/ppermute | solution.py:502
  30.9 0.8 %collective-permute-start.13 = (f32[56,128]{1,0:T(8,128)S(1)}, f32[56,128]{1,0:T(8,128)S(1)}, u32[]{:S(2)}, u32[]{:S(2)}) collective-permute-start(f32[56,128]{1,0:T(8,128)S(1)} %get-tuple-element.120), channel_id=1, source_target_pairs={{0,1},{1,0},{2,3},{3,2},{4,5},{5,4},{6,7},{7,6},{8,9},{9,8},{10,11... | collective-permute-start | bytes 86024 | tf_op jit(solution)/shard_map/ppermute | solution.py:502
  31.7 0.8 %collective-permute-start.14 = (f32[56,128]{1,0:T(8,128)S(1)}, f32[56,128]{1,0:T(8,128)S(1)}, u32[]{:S(2)}, u32[]{:S(2)}) collective-permute-start(f32[56,128]{1,0:T(8,128)S(1)} %get-tuple-element.121), channel_id=1, source_target_pairs={{1,2},{2,1},{3,0},{0,3},{5,6},{6,5},{7,4},{4,7},{9,10},{10,9},{11,... | collective-permute-start | bytes 86024 | tf_op jit(solution)/shard_map/ppermute | solution.py:502
  32.5 1.0 %shard_map.105 = (f32[504,128]{1,0:T(8,128)S(1)}, f32[280,128]{1,0:T(8,128)S(1)}) custom-call(bf16[192,640]{1,0:T(8,128)(2,1)S(1)} %get-tuple-element.122.refs_0_, f32[96,640]{1,0:T(8,128)S(1)} %get-tuple-element.123.refs_1_, bf16[448,256]{1,0:T(8,128)(2,1)S(1)} %get-tuple-element.124.refs_2_, bf16[168,192]{1,0:T(8,128)(2,1)S(1)} %get-tuple-element.109.refs_3_, ...), custom_call_target="tpu_custom_call" | custom-call | flops 1073741824 | bytes 2097152 | tf_op jit(solution)/shard_map/pallas_call | solution.py:459
  33.6 1.4 %collective-permute-done.14.refs_4_ = f32[56,128]{1,0:T(8,128)S(1)} collective-permute-done((f32[56,128]{1,0:T(8,128)S(1)}, f32[56,128]{1,0:T(8,128)S(1)}, u32[]{:S(2)}, u32[]{:S(2)}) %collective-permute-start.14) | collective-permute-done | bytes 28704 | tf_op jit(solution)/shard_map/ppermute | solution.py:502
  35.0 4.1 %shard_map.106 = (f32[504,128]{1,0:T(8,128)S(1)}, f32[280,128]{1,0:T(8,128)S(1)}, f32[280,128]{1,0:T(8,128)S(1)}, bf16[192,640]{1,0:T(8,128)(2,1)S(1)}, f32[96,6...) custom-call(f32[56,128]{1,0:T(8,128)S(1)} %collective-permute-done.1, ...), custom_call_target="tpu_custom_call" | custom-call | flops 1073741824 | bytes 2097152 | tf_op jit(solution)/shard_map/pallas_call | solution.py:459
  39.1 0.5 collective-permute-start.15
  39.6 0.8 %collective-permute-start.16 = (f32[56,128]{1,0:T(8,128)S(1)}, f32[56,128]{1,0:T(8,128)S(1)}, u32[]{:S(2)}, u32[]{:S(2)}) collective-permute-start(f32[56,128]{1,0:T(8,128)S(1)} %get-tuple-element.131), channel_id=1, source_target_pairs={{8,16},{16,8},{24,0},{0,24},{9,17},{17,9},{25,1},{1,25},{10,18},{1... | collective-permute-start | bytes 86024 | tf_op jit(solution)/shard_map/ppermute | solution.py:502
  40.3 1.1 %collective-permute-start.17 = (f32[56,128]{1,0:T(8,128)S(1)}, f32[56,128]{1,0:T(8,128)S(1)}, u32[]{:S(2)}, u32[]{:S(2)}) collective-permute-start(f32[56,128]{1,0:T(8,128)S(1)} %get-tuple-element.132), channel_id=1, source_target_pairs={{0,4},{4,0},{1,5},{5,1},{2,6},{6,2},{3,7},{7,3},{8,12},{12,8},{9,1... | collective-permute-start | bytes 86024 | tf_op jit(solution)/shard_map/ppermute | solution.py:502
  41.4 0.8 %collective-permute-start.18 = (f32[56,128]{1,0:T(8,128)S(1)}, f32[56,128]{1,0:T(8,128)S(1)}, u32[]{:S(2)}, u32[]{:S(2)}) collective-permute-start(f32[56,128]{1,0:T(8,128)S(1)} %get-tuple-element.133), channel_id=1, source_target_pairs={{0,1},{1,0},{2,3},{3,2},{4,5},{5,4},{6,7},{7,6},{8,9},{9,8},{10,11... | collective-permute-start | bytes 86024 | tf_op jit(solution)/shard_map/ppermute | solution.py:502
  42.2 0.8 %collective-permute-start.19 = (f32[56,128]{1,0:T(8,128)S(1)}, f32[56,128]{1,0:T(8,128)S(1)}, u32[]{:S(2)}, u32[]{:S(2)}) collective-permute-start(f32[56,128]{1,0:T(8,128)S(1)} %get-tuple-element.134), channel_id=1, source_target_pairs={{1,2},{2,1},{3,0},{0,3},{5,6},{6,5},{7,4},{4,7},{9,10},{10,9},{11,... | collective-permute-start | bytes 86024 | tf_op jit(solution)/shard_map/ppermute | solution.py:502
  43.0 1.8 %shard_map.107 = (f32[504,128]{1,0:T(8,128)S(1)}, f32[6,504,128]{2,1,0:T(8,128)S(1)}, f32[504,128]{1,0:T(8,128)S(1)}, f32[280,128]{1,0:T(8,128)}) custom-call(bf16[192,640]{1,0:T(8,128)(2,1)S(1)} %get-tuple-element.135.refs_0_, f32[96,640]{1,0:T(8,128)S(1)} %get-tuple-element.136.refs_1_, bf16[448,256]{1,0:T(8,128)(2,1)S(1)} %get-tuple-element.137.refs_2_, ...), custom_call_target="tpu_custom_call" | custom-call | flops 1073741824 | bytes 2097152 | tf_op jit(solution)/shard_map/pallas_call | solution.py:459
  44.9 0.6 %collective-permute-done.19.refs_4_ = f32[56,128]{1,0:T(8,128)S(1)} collective-permute-done((f32[56,128]{1,0:T(8,128)S(1)}, f32[56,128]{1,0:T(8,128)S(1)}, u32[]{:S(2)}, u32[]{:S(2)}) %collective-permute-start.19) | collective-permute-done | bytes 28704 | tf_op jit(solution)/shard_map/ppermute | solution.py:502
  45.5 5.7 %shard_map.108 = f32[504,128]{1,0:T(8,128)} custom-call(f32[56,128]{1,0:T(8,128)S(1)} %collective-permute-done.15.refs_0_, f32[56,128]{1,0:T(8,128)S(1)} %collective-permute-done.16.refs_1_, f32[56,128]{1,0:T(8,128)S(1)} %collective-permute-done.17.refs_2_, f32[56,128]{1,0:T(8,128)S(1)} %collective-permute-done.18.refs_3_, ...), custom_call_target="tpu_custom_call" | custom-call | flops 1073741824 | bytes 2097152 | tf_op jit(solution)/shard_map/pallas_call | solution.py:459
  (18 shorter events, 0.5 us)
Async XLA Ops:
  2.2 10.2 %collective-permute-start = (f32[56,128]{1,0:T(8,128)S(1)}, f32[56,128]{1,0:T(8,128)S(1)}, u32[]{:S(2)}, u32[]{:S(2)}) collective-permute-start(f32[56,128]{1,0:T(8,128)S(1)} %get-tuple-element.75), channel_id=1, source_target_pairs={{0,8},{8,0},{16,24},{24,16},{1,9},{9,1},{17,25},{25,17},{2,10},{10... | collective-permute-start | bytes 86024 | tf_op jit(solution)/shard_map/ppermute | solution.py:502
  4.4 8.0 %collective-permute-start.1 = (f32[56,128]{1,0:T(8,128)S(1)}, f32[56,128]{1,0:T(8,128)S(1)}, u32[]{:S(2)}, u32[]{:S(2)}) collective-permute-start(f32[56,128]{1,0:T(8,128)S(1)} %get-tuple-element.76), channel_id=1, source_target_pairs={{8,16},{16,8},{24,0},{0,24},{9,17},{17,9},{25,1},{1,25},{10,18},{1... | collective-permute-start | bytes 86024 | tf_op jit(solution)/shard_map/ppermute | solution.py:502
  6.6 5.8 %collective-permute-start.2 = (f32[56,128]{1,0:T(8,128)S(1)}, f32[56,128]{1,0:T(8,128)S(1)}, u32[]{:S(2)}, u32[]{:S(2)}) collective-permute-start(f32[56,128]{1,0:T(8,128)S(1)} %get-tuple-element.77), channel_id=1, source_target_pairs={{0,4},{4,0},{1,5},{5,1},{2,6},{6,2},{3,7},{7,3},{8,12},{12,8},{9,1... | collective-permute-start | bytes 86024 | tf_op jit(solution)/shard_map/ppermute | solution.py:502
  7.8 4.6 %collective-permute-start.3 = (f32[56,128]{1,0:T(8,128)S(1)}, f32[56,128]{1,0:T(8,128)S(1)}, u32[]{:S(2)}, u32[]{:S(2)}) collective-permute-start(f32[56,128]{1,0:T(8,128)S(1)} %get-tuple-element.78), channel_id=1, source_target_pairs={{0,1},{1,0},{2,3},{3,2},{4,5},{5,4},{6,7},{7,6},{8,9},{9,8},{10,11... | collective-permute-start | bytes 86024 | tf_op jit(solution)/shard_map/ppermute | solution.py:502
  9.3 3.3 %collective-permute-start.4 = (f32[56,128]{1,0:T(8,128)S(1)}, f32[56,128]{1,0:T(8,128)S(1)}, u32[]{:S(2)}, u32[]{:S(2)}) collective-permute-start(f32[56,128]{1,0:T(8,128)S(1)} %get-tuple-element.79), channel_id=1, source_target_pairs={{1,2},{2,1},{3,0},{0,3},{5,6},{6,5},{7,4},{4,7},{9,10},{10,9},{11,... | collective-permute-start | bytes 86024 | tf_op jit(solution)/shard_map/ppermute | solution.py:502
  16.9 4.7 %collective-permute-start.5 = (f32[56,128]{1,0:T(8,128)S(1)}, f32[56,128]{1,0:T(8,128)S(1)}, u32[]{:S(2)}, u32[]{:S(2)}) collective-permute-start(f32[56,128]{1,0:T(8,128)S(1)} %get-tuple-element.101), channel_id=1, source_target_pairs={{0,8},{8,0},{16,24},{24,16},{1,9},{9,1},{17,25},{25,17},{2,10},{10... | collective-permute-start | bytes 86024 | tf_op jit(solution)/shard_map/ppermute | solution.py:502
  17.3 4.5 %collective-permute-start.6 = (f32[56,128]{1,0:T(8,128)S(1)}, f32[56,128]{1,0:T(8,128)S(1)}, u32[]{:S(2)}, u32[]{:S(2)}) collective-permute-start(f32[56,128]{1,0:T(8,128)S(1)} %get-tuple-element.102), channel_id=1, source_target_pairs={{8,16},{16,8},{24,0},{0,24},{9,17},{17,9},{25,1},{1,25},{10,18},{1... | collective-permute-start | bytes 86024 | tf_op jit(solution)/shard_map/ppermute | solution.py:502
  18.1 3.8 %collective-permute-start.7 = (f32[56,128]{1,0:T(8,128)S(1)}, f32[56,128]{1,0:T(8,128)S(1)}, u32[]{:S(2)}, u32[]{:S(2)}) collective-permute-start(f32[56,128]{1,0:T(8,128)S(1)} %get-tuple-element.103), channel_id=1, source_target_pairs={{0,4},{4,0},{1,5},{5,1},{2,6},{6,2},{3,7},{7,3},{8,12},{12,8},{9,1... | collective-permute-start | bytes 86024 | tf_op jit(solution)/shard_map/ppermute | solution.py:502
  18.4 3.4 %collective-permute-start.8 = (f32[56,128]{1,0:T(8,128)S(1)}, f32[56,128]{1,0:T(8,128)S(1)}, u32[]{:S(2)}, u32[]{:S(2)}) collective-permute-start(f32[56,128]{1,0:T(8,128)S(1)} %get-tuple-element.104), channel_id=1, source_target_pairs={{0,1},{1,0},{2,3},{3,2},{4,5},{5,4},{6,7},{7,6},{8,9},{9,8},{10,11... | collective-permute-start | bytes 86024 | tf_op jit(solution)/shard_map/ppermute | solution.py:502
  19.4 3.6 %collective-permute-start.9 = (f32[56,128]{1,0:T(8,128)S(1)}, f32[56,128]{1,0:T(8,128)S(1)}, u32[]{:S(2)}, u32[]{:S(2)}) collective-permute-start(f32[56,128]{1,0:T(8,128)S(1)} %get-tuple-element.105), channel_id=1, source_target_pairs={{1,2},{2,1},{3,0},{0,3},{5,6},{6,5},{7,4},{4,7},{9,10},{10,9},{11,... | collective-permute-start | bytes 86024 | tf_op jit(solution)/shard_map/ppermute | solution.py:502
  27.1 6.5 %collective-permute-start.10 = (f32[56,128]{1,0:T(8,128)S(1)}, f32[56,128]{1,0:T(8,128)S(1)}, u32[]{:S(2)}, u32[]{:S(2)}) collective-permute-start(f32[56,128]{1,0:T(8,128)S(1)} %get-tuple-element.117), channel_id=1, source_target_pairs={{0,8},{8,0},{16,24},{24,16},{1,9},{9,1},{17,25},{25,17},{2,10},{10... | collective-permute-start | bytes 86024 | tf_op jit(solution)/shard_map/ppermute | solution.py:502
  27.7 5.9 %collective-permute-start.11 = (f32[56,128]{1,0:T(8,128)S(1)}, f32[56,128]{1,0:T(8,128)S(1)}, u32[]{:S(2)}, u32[]{:S(2)}) collective-permute-start(f32[56,128]{1,0:T(8,128)S(1)} %get-tuple-element.118), channel_id=1, source_target_pairs={{8,16},{16,8},{24,0},{0,24},{9,17},{17,9},{25,1},{1,25},{10,18},{1... | collective-permute-start | bytes 86024 | tf_op jit(solution)/shard_map/ppermute | solution.py:502
  29.7 3.9 %collective-permute-start.12 = (f32[56,128]{1,0:T(8,128)S(1)}, f32[56,128]{1,0:T(8,128)S(1)}, u32[]{:S(2)}, u32[]{:S(2)}) collective-permute-start(f32[56,128]{1,0:T(8,128)S(1)} %get-tuple-element.119), channel_id=1, source_target_pairs={{0,4},{4,0},{1,5},{5,1},{2,6},{6,2},{3,7},{7,3},{8,12},{12,8},{9,1... | collective-permute-start | bytes 86024 | tf_op jit(solution)/shard_map/ppermute | solution.py:502
  30.9 2.7 %collective-permute-start.13 = (f32[56,128]{1,0:T(8,128)S(1)}, f32[56,128]{1,0:T(8,128)S(1)}, u32[]{:S(2)}, u32[]{:S(2)}) collective-permute-start(f32[56,128]{1,0:T(8,128)S(1)} %get-tuple-element.120), channel_id=1, source_target_pairs={{0,1},{1,0},{2,3},{3,2},{4,5},{5,4},{6,7},{7,6},{8,9},{9,8},{10,11... | collective-permute-start | bytes 86024 | tf_op jit(solution)/shard_map/ppermute | solution.py:502
  31.7 3.3 %collective-permute-start.14 = (f32[56,128]{1,0:T(8,128)S(1)}, f32[56,128]{1,0:T(8,128)S(1)}, u32[]{:S(2)}, u32[]{:S(2)}) collective-permute-start(f32[56,128]{1,0:T(8,128)S(1)} %get-tuple-element.121), channel_id=1, source_target_pairs={{1,2},{2,1},{3,0},{0,3},{5,6},{6,5},{7,4},{4,7},{9,10},{10,9},{11,... | collective-permute-start | bytes 86024 | tf_op jit(solution)/shard_map/ppermute | solution.py:502
  39.1 5.8 %collective-permute-start.15 = (f32[56,128]{1,0:T(8,128)S(1)}, f32[56,128]{1,0:T(8,128)S(1)}, u32[]{:S(2)}, u32[]{:S(2)}) collective-permute-start(f32[56,128]{1,0:T(8,128)S(1)} %get-tuple-element.130), channel_id=1, source_target_pairs={{0,8},{8,0},{16,24},{24,16},{1,9},{9,1},{17,25},{25,17},{2,10},{10... | collective-permute-start | bytes 86024 | tf_op jit(solution)/shard_map/ppermute | solution.py:502
  39.6 5.3 %collective-permute-start.16 = (f32[56,128]{1,0:T(8,128)S(1)}, f32[56,128]{1,0:T(8,128)S(1)}, u32[]{:S(2)}, u32[]{:S(2)}) collective-permute-start(f32[56,128]{1,0:T(8,128)S(1)} %get-tuple-element.131), channel_id=1, source_target_pairs={{8,16},{16,8},{24,0},{0,24},{9,17},{17,9},{25,1},{1,25},{10,18},{1... | collective-permute-start | bytes 86024 | tf_op jit(solution)/shard_map/ppermute | solution.py:502
  40.3 4.6 %collective-permute-start.17 = (f32[56,128]{1,0:T(8,128)S(1)}, f32[56,128]{1,0:T(8,128)S(1)}, u32[]{:S(2)}, u32[]{:S(2)}) collective-permute-start(f32[56,128]{1,0:T(8,128)S(1)} %get-tuple-element.132), channel_id=1, source_target_pairs={{0,4},{4,0},{1,5},{5,1},{2,6},{6,2},{3,7},{7,3},{8,12},{12,8},{9,1... | collective-permute-start | bytes 86024 | tf_op jit(solution)/shard_map/ppermute | solution.py:502
  41.4 3.5 %collective-permute-start.18 = (f32[56,128]{1,0:T(8,128)S(1)}, f32[56,128]{1,0:T(8,128)S(1)}, u32[]{:S(2)}, u32[]{:S(2)}) collective-permute-start(f32[56,128]{1,0:T(8,128)S(1)} %get-tuple-element.133), channel_id=1, source_target_pairs={{0,1},{1,0},{2,3},{3,2},{4,5},{5,4},{6,7},{7,6},{8,9},{9,8},{10,11... | collective-permute-start | bytes 86024 | tf_op jit(solution)/shard_map/ppermute | solution.py:502
  42.2 3.3 %collective-permute-start.19 = (f32[56,128]{1,0:T(8,128)S(1)}, f32[56,128]{1,0:T(8,128)S(1)}, u32[]{:S(2)}, u32[]{:S(2)}) collective-permute-start(f32[56,128]{1,0:T(8,128)S(1)} %get-tuple-element.134), channel_id=1, source_target_pairs={{1,2},{2,1},{3,0},{0,3},{5,6},{6,5},{7,4},{4,7},{9,10},{10,9},{11,... | collective-permute-start | bytes 86024 | tf_op jit(solution)/shard_map/ppermute | solution.py:502
where the time goes:
time: 51.3 us; the launch traced here: 51.2 us
  Pallas kernels  26.2 us (51%)
  starting transfers between devices  21.2 us (41%)
  waiting for transfers between devices  3.66 us (7%)
    pallas_call x9, Pallas kernels, call(): pl.pallas_call(kernel, out_shape=[jax.ShapeDtypeStruct(*o) for o in outs]...  26.2 us
    ppermute x20, starting transfers between devices, trade(): lax.ppermute(m, axis, links)  21.2 us
    ppermute x20, waiting for transfers between devices, trade(): lax.ppermute(m, axis, links)  3.66 us
  transfers between devices with their start and end apart: 20, of which 5 were waited for; matrix products, arithmetic and copies ran while one was open for 0% of the time, Pallas kernels for 11%

commit v1 on v0

--- a/solution.py
+++ b/solution.py
@@ -98,6 +98,10 @@
         u[at:at + z.BQ, lanes] = value
 
 
+def lift(z, pt, u):
+    return dot(pt[...], u[...])
+
+
 def lane(z, i):
     return slice(i * z.E, (i + 1) * z.E)
 
@@ -108,6 +112,16 @@
 
 def low_lanes(z, rows):
     return lax.broadcasted_iota(jnp.int32, (rows, z.E), 1) < z.H
+
+
+def balanced(z, out, matrix, y3):
+    rows, lanes = matrix.shape[0], out.shape[1]
+    even = lanes // (2 * z.E) * 2 * z.E
+    out[0:rows, 0:even] = dot(matrix[...], y3[:, 0:even])
+    if even < lanes:
+        cut = up(rows // 2, 16)
+        out[0:cut, even:lanes] = dot(matrix[0:cut, :], y3[:, even:lanes])
+        out[cut:rows, even:lanes] = dot(matrix[cut:rows, :], y3[:, even:lanes])
 
 
 def fold(z, first, second):
@@ -141,6 +155,11 @@
     return total
 
 
+def mark(ref, at, parts):
+    for i, x in enumerate(parts):
+        ref[pl.ds(pl.multiple_of(at, 8), 8), i * x.shape[1]:(i + 1) * x.shape[1]] = x[0:8, :]
+
+
 def star_pair(z, p, turned, star):
     group = [g for g in (2 * p, 2 * p + 1) if g < z.F]
     total = star_sum(z, [None] * len(group), group, turned, star, z.FP)
@@ -160,6 +179,30 @@
 
 def groups_of(n, size):
     return [list(range(i, min(n, i + size))) for i in range(0, n, size)]
+
+
+def regroup(z, base, part):
+    group = lax.broadcasted_iota(jnp.int32, (z.QR, z.E), 1)
+    out = None
+    for q in range(z.Q):
+        shift = (q - base) % z.Q * z.W
+        x = part(q)
+        x = pltpu.roll(x, shift, 1) if shift else x
+        out = x if out is None else jnp.where(group >= q * z.W, x, out)
+    return out
+
+
+def ungroup(z, messages, q):
+    group = lax.broadcasted_iota(jnp.int32, (z.QR, z.E), 1)
+    out = None
+    for m, message in enumerate(messages):
+        shift = (m - q) % z.Q * z.W
+        x = message[...]
+        x = pltpu.roll(x, shift, 1) if shift else x
+        out = x if out is None else jnp.where(group >= m * z.W, x, out)
+    if len(messages) < z.Q:
+        out = jnp.where(group < len(messages) * z.W, out, 0.0)
+    return out
 
 
 def pack_messages(z, sent, ohs, sx, messages, picked):
@@ -169,12 +212,8 @@
     both = dot(sx[...], ohs[...])
     picked[...] = both[0:z.R, :] + both[z.RP:z.RP + z.R, :]
     for m, message in enumerate(messages):
-        for q in range(z.Q):
-            rows = min(z.R, (q + 1) * z.QR) - q * z.QR
-            lanes = slice(q * z.W, (q + 1) * z.W)
-            message[0:rows, lanes] = picked[q * z.QR:q * z.QR + rows, m * z.W:(m + 1) * z.W]
-            if rows < z.QR:
-                message[rows:z.QR, lanes] = jnp.zeros((z.QR - rows, z.W), F32)
+        home = lane(z, m // z.Q)
+        message[...] = regroup(z, m % z.Q, lambda q: filled(picked[q * z.QR:min(z.R, (q + 1) * z.QR), home], z.QR))
 
 
 def triple(rows, cols, target, wide, matrix):
@@ -193,8 +232,8 @@
     projection, slots, sent, picked, picks, wide, sem = refs
     targets = (y, projection, slots, across, star, local, deriv, volume, partner, cluster)
     copies = [pltpu.make_async_copy(a, b, sem.at[i]) for i, (a, b) in enumerate(zip(hbm, targets))]
-    for copy in copies:
-        copy.start()
+    for i in (2, 1, 0, 3, *range(4, n)):
+        copies[i].start()
     square[...] = jnp.zeros_like(square)
     wide[...] = jnp.zeros_like(wide)
     picks[...] = jnp.full_like(picks, -1)
@@ -300,7 +339,7 @@
             total = gathered[g * z.BP:(g + 1) * z.BP, lane(z, c)] + gathered[z.RP + g * z.BP:z.RP + (g + 1) * z.BP, lane(z, c)]
             hi, lo = halves(filled(total + face_sum(z, local, g, c, t), z.BQ))
             put_face(z, u, c, lane(z, g), hi, lo)
-    lifted = dot(pt[...], u[...])
+    lifted = lift(z, pt, u)
     for group in groups_of(z.F, 3):
         start = [lifted[:, lane(z, g)] for g in group]
         for g, total in zip(group, star_sum(z, start, group, turned, star, z.F)):
@@ -313,7 +352,7 @@
             hi = filled(gathered[g * z.BP:(g + 1) * z.BP, lane(z, c)], z.BQ).astype(BF)
             lo = filled(gathered[z.RP + g * z.BP:z.RP + (g + 1) * z.BP, lane(z, c)], z.BQ).astype(BF)
             put_face(z, u, c, lane(z, g), hi, lo)
-    return dot(pt[...], u[...])
+    return lift(z, pt, u)
 
 
 def local_kernel(z, last, *refs):
@@ -336,7 +375,7 @@
             second = face_sum(z, local, 2 * p + 1, c, t) if 2 * p + 1 < z.F else None
             hi, lo = halves(filled(fold(z, first, second), z.BQ))
             put_face(z, u_half, c, lane(z, p), hi, lo)
-    lifted_half = dot(pt[...], u_half[...])
+    lifted_half = lift(z, pt, u_half)
     lifted[...] = lift_gathered(z, gathered, u, pt)
     pick, rank = index[0:1, :], index[1:2, :]
     gained = compact(z, pick, lambda f: lifted[:, lane(z, f)])
@@ -365,13 +404,10 @@
 
 
 def arrive(z, arrived, ohr, pt, landed, stacked, gathered, u):
-    used = z.K * z.W // 128 * 128
-    if used < z.KW:
-        landed[:, used:z.KW] = jnp.zeros((z.R, z.KW - used), F32)
-    for m in range(z.K):
+    for i, group in enumerate(groups_of(z.K, z.Q)):
         for q in range(z.Q):
             rows = min(z.R, (q + 1) * z.QR) - q * z.QR
-            landed[q * z.QR:q * z.QR + rows, m * z.W:(m + 1) * z.W] = arrived[m][0:rows, q * z.W:(q + 1) * z.W]
+            landed[q * z.QR:q * z.QR + rows, lane(z, i)] = ungroup(z, [arrived[m] for m in group], q)[0:rows, :]
     hi, lo = halves(landed[...])
     stacked[0:z.R, :] = hi
     stacked[z.RP:z.RP + z.R, :] = lo
@@ -404,7 +440,7 @@
         c = F32(row[TERMS - 2])
         for k in range(TERMS - 2):
             c = jnp.where(i == TERMS - 2 - k, F32(row[k]), c)
-        turned[...] = dot(s3[...], y3[...])
+        balanced(z, turned, s3, y3)
         for p in range(z.FP):
             rows = slice(p * z.M, (p + 1) * z.M)
             total = c * half[rows, :] + star_pair(z, p, turned, star)
@@ -439,10 +475,12 @@
         c = F32(row[TERMS - 2])
         for k in range(TERMS - 2):
             c = jnp.where(i == TERMS - 2 - k, F32(row[k]), c)
-        turned[...] = dot(s3[...], y3[...])
-        for group in groups_of(z.F, 3):
+        turned[0:3 * z.M, :] = dot(s3[...], y3[...])
+        for group in groups_of(z.F, 2):
             start = [weights[TERMS - 2 - i, g * z.M:(g + 1) * z.M, :] + c * src[g * z.M:(g + 1) * z.M, :] for g in group]
-            for g, total in zip(group, star_sum(z, start, group, turned, star, z.F)):
+            sums = star_sum(z, start, group, turned, star, z.F)
+            mark(turned, 3 * z.M + 8 * i, sums)
+            for g, total in zip(group, sums):
                 put_field(z, y3, g, total)
                 out[g * z.M:(g + 1) * z.M, :] = total
         return carry
@@ -489,6 +527,7 @@
     y3, y3_half = ((3 * z.MP, fields * members), BF), ((3 * z.MP, z.FP * members), BF)
     traces, traces_half = ((faces * z.BP, fields * members), F32), ((faces * z.BP, z.FP * members), F32)
     turned, turned_half = ((3 * modes, fields * members), F32), ((3 * modes, z.FP * members), F32)
+    marked = lambda o: ((o[0][0] + 8 * (TERMS - 1), o[0][1]), o[1])
     u, u_half = ((3 * faces * z.BQ, fields * members), BF), ((3 * faces * z.BQ, z.FP * members), BF)
     gathered, lifted = ((2 * z.RP, z.S), F32), ((modes, fields * members), F32)
     landed, stacked = ((z.R, z.KW), F32), ((2 * z.RP, z.KW), BF)
@@ -548,7 +587,7 @@
             src, half_src = call(functools.partial(local_kernel, z, False), [full, half], local_scratch, *local_args)
     (out,) = call(
         functools.partial(last_kernel, z), [full],
-        [landed, stacked, gathered, u, lifted, turned, y3, full],
+        [landed, stacked, gathered, u, lifted, marked(turned), y3, full],
         *arrived, src, weights, base, s3, pt, star, ohr,
     )
     return out.reshape(fields, modes, members)

time: 51.3 us -> 50.1 us (0.977)
  Pallas kernels: 26.2 us -> 24.9 us
    pallas_call x9, Pallas kernels: 26.2 us -> 24.9 us  [call(): pl.pallas_call(kernel, out_shape=[jax.ShapeDtypeStruct(*o) for o in outs]...]
  transfers between devices with their start and end apart: 20 -> 20, of which waited for: 5 -> 5; matrix products, arithmetic and copies ran while one was open for 0% -> 0% of each run, Pallas kernels for 11% -> 12%
where the time goes in v1:
time: 50.1 us; the launch traced here: 50 us
  Pallas kernels  24.9 us (50%)
  starting transfers between devices  21.2 us (42%)
  waiting for transfers between devices  3.64 us (7%)
    pallas_call x9, Pallas kernels, call(): pl.pallas_call(kernel, out_shape=[jax.ShapeDtypeStruct(*o) for o in outs]...  24.9 us
    ppermute x20, starting transfers between devices, trade(): lax.ppermute(m, axis, links)  21.2 us
    ppermute x20, waiting for transfers between devices, trade(): lax.ppermute(m, axis, links)  3.64 us
  transfers between devices with their start and end apart: 20, of which 5 were waited for; matrix products, arithmetic and copies ran while one was open for 0% of the time, Pallas kernels for 12%

profile of v1, /device:TPU:1, one launch (start us, length us, event | category | flops | bytes accessed | tf_op | source)
XLA Modules:
  0.0 50.0 jit_solution(8673029484081912043)
XLA Ops:
  0.0 2.1 %shard_map.100 = (f32[504,128]{1,0:T(8,128)S(1)}, f32[9,9,3,128]{3,2,1,0:T(4,128)S(1)}, f32[9,9,4,128]{3,2,1,0:T(4,128)S(1)}, f32[9,9,4,128]{3,2,1,0:T(4,128)S(1...) custom-call(f32[504,128]{1,0:T(8,128)} %bitcast.7, ...), custom_call_target="tpu_custom_call" | custom-call | flops 1073741824 | bytes 2097152 | tf_op jit(solution)/shard_map/pallas_call | solution.py:497
  2.1 2.2 %collective-permute-start = (f32[56,128]{1,0:T(8,128)S(1)}, f32[56,128]{1,0:T(8,128)S(1)}, u32[]{:S(2)}, u32[]{:S(2)}) collective-permute-start(f32[56,128]{1,0:T(8,128)S(1)} %get-tuple-element.75), channel_id=1, source_target_pairs={{0,8},{8,0},{16,24},{24,16},{1,9},{9,1},{17,25},{25,17},{2,10},{10... | collective-permute-start | bytes 86024 | tf_op jit(solution)/shard_map/ppermute | solution.py:541
  4.3 2.2 %collective-permute-start.1 = (f32[56,128]{1,0:T(8,128)S(1)}, f32[56,128]{1,0:T(8,128)S(1)}, u32[]{:S(2)}, u32[]{:S(2)}) collective-permute-start(f32[56,128]{1,0:T(8,128)S(1)} %get-tuple-element.76), channel_id=1, source_target_pairs={{8,16},{16,8},{24,0},{0,24},{9,17},{17,9},{25,1},{1,25},{10,18},{1... | collective-permute-start | bytes 86024 | tf_op jit(solution)/shard_map/ppermute | solution.py:541
  6.5 1.2 %collective-permute-start.2 = (f32[56,128]{1,0:T(8,128)S(1)}, f32[56,128]{1,0:T(8,128)S(1)}, u32[]{:S(2)}, u32[]{:S(2)}) collective-permute-start(f32[56,128]{1,0:T(8,128)S(1)} %get-tuple-element.77), channel_id=1, source_target_pairs={{0,4},{4,0},{1,5},{5,1},{2,6},{6,2},{3,7},{7,3},{8,12},{12,8},{9,1... | collective-permute-start | bytes 86024 | tf_op jit(solution)/shard_map/ppermute | solution.py:541
  7.7 1.5 %collective-permute-start.3 = (f32[56,128]{1,0:T(8,128)S(1)}, f32[56,128]{1,0:T(8,128)S(1)}, u32[]{:S(2)}, u32[]{:S(2)}) collective-permute-start(f32[56,128]{1,0:T(8,128)S(1)} %get-tuple-element.78), channel_id=1, source_target_pairs={{0,1},{1,0},{2,3},{3,2},{4,5},{5,4},{6,7},{7,6},{8,9},{9,8},{10,11... | collective-permute-start | bytes 86024 | tf_op jit(solution)/shard_map/ppermute | solution.py:541
  9.2 1.1 %collective-permute-start.4 = (f32[56,128]{1,0:T(8,128)S(1)}, f32[56,128]{1,0:T(8,128)S(1)}, u32[]{:S(2)}, u32[]{:S(2)}) collective-permute-start(f32[56,128]{1,0:T(8,128)S(1)} %get-tuple-element.79), channel_id=1, source_target_pairs={{1,2},{2,1},{3,0},{0,3},{5,6},{6,5},{7,4},{4,7},{9,10},{10,9},{11,... | collective-permute-start | bytes 86024 | tf_op jit(solution)/shard_map/ppermute | solution.py:541
  10.3 1.9 %shard_map.101 = (bf16[168,192]{1,0:T(8,128)(2,1)S(1)}, bf16[168,192]{1,0:T(8,128)(2,1)S(1)}, bf16[56,384]{1,0:T(8,128)(2,1)S(1)}, bf16[256,512]{1,0:T(8,128)(2,...) custom-call(f32[3,56,56]{2,1,0:T(8,128)S(1)} %get-tuple-element.80.r, ...), custom_call_target="tpu_custom_call" | custom-call | flops 1073741824 | bytes 2097152 | tf_op jit(solution)/shard_map/pallas_call | solution.py:497
  12.5 4.1 %shard_map.102 = (f32[504,128]{1,0:T(8,128)S(1)}, f32[280,128]{1,0:T(8,128)S(1)}, f32[280,128]{1,0:T(8,128)S(1)}, bf16[192,640]{1,0:T(8,128)(2,1)S(1)}, f32[96,6...) custom-call(f32[56,128]{1,0:T(8,128)S(1)} %collective-permute-done.r, ...), custom_call_target="tpu_custom_call" | custom-call | flops 1073741824 | bytes 2097152 | tf_op jit(solution)/shard_map/pallas_call | solution.py:497
  16.6 0.5 collective-permute-start.5
  17.1 0.7 %collective-permute-start.6 = (f32[56,128]{1,0:T(8,128)S(1)}, f32[56,128]{1,0:T(8,128)S(1)}, u32[]{:S(2)}, u32[]{:S(2)}) collective-permute-start(f32[56,128]{1,0:T(8,128)S(1)} %get-tuple-element.102), channel_id=1, source_target_pairs={{8,16},{16,8},{24,0},{0,24},{9,17},{17,9},{25,1},{1,25},{10,18},{1... | collective-permute-start | bytes 86024 | tf_op jit(solution)/shard_map/ppermute | solution.py:541
  17.8 0.3 collective-permute-start.7
  18.2 1.0 %collective-permute-start.8 = (f32[56,128]{1,0:T(8,128)S(1)}, f32[56,128]{1,0:T(8,128)S(1)}, u32[]{:S(2)}, u32[]{:S(2)}) collective-permute-start(f32[56,128]{1,0:T(8,128)S(1)} %get-tuple-element.104), channel_id=1, source_target_pairs={{0,1},{1,0},{2,3},{3,2},{4,5},{5,4},{6,7},{7,6},{8,9},{9,8},{10,11... | collective-permute-start | bytes 86024 | tf_op jit(solution)/shard_map/ppermute | solution.py:541
  19.2 1.1 %collective-permute-start.9 = (f32[56,128]{1,0:T(8,128)S(1)}, f32[56,128]{1,0:T(8,128)S(1)}, u32[]{:S(2)}, u32[]{:S(2)}) collective-permute-start(f32[56,128]{1,0:T(8,128)S(1)} %get-tuple-element.105), channel_id=1, source_target_pairs={{1,2},{2,1},{3,0},{0,3},{5,6},{6,5},{7,4},{4,7},{9,10},{10,9},{11,... | collective-permute-start | bytes 86024 | tf_op jit(solution)/shard_map/ppermute | solution.py:541
  20.3 1.1 %shard_map.103 = (f32[504,128]{1,0:T(8,128)S(1)}, f32[280,128]{1,0:T(8,128)S(1)}) custom-call(bf16[192,640]{1,0:T(8,128)(2,1)S(1)} %get-tuple-element.106.refs_0_, f32[96,640]{1,0:T(8,128)S(1)} %get-tuple-element.107.refs_1_, bf16[448,256]{1,0:T(8,128)(2,1)S(1)} %get-tuple-element.108.refs_2_, bf16[168,192]{1,0:T(8,128)(2,1)S(1)} %get-tuple-element.109.refs_3_, ...), custom_call_target="tpu_custom_call" | custom-call | flops 1073741824 | bytes 2097152 | tf_op jit(solution)/shard_map/pallas_call | solution.py:497
  21.6 1.1 %collective-permute-done.9.refs_4_ = f32[56,128]{1,0:T(8,128)S(1)} collective-permute-done((f32[56,128]{1,0:T(8,128)S(1)}, f32[56,128]{1,0:T(8,128)S(1)}, u32[]{:S(2)}, u32[]{:S(2)}) %collective-permute-start.9) | collective-permute-done | bytes 28704 | tf_op jit(solution)/shard_map/ppermute | solution.py:541
  22.8 3.9 %shard_map.104 = (f32[504,128]{1,0:T(8,128)S(1)}, f32[280,128]{1,0:T(8,128)S(1)}, f32[280,128]{1,0:T(8,128)S(1)}, bf16[192,640]{1,0:T(8,128)(2,1)S(1)}, f32[96,6...) custom-call(f32[56,128]{1,0:T(8,128)S(1)} %collective-permute-done.5, ...), custom_call_target="tpu_custom_call" | custom-call | flops 1073741824 | bytes 2097152 | tf_op jit(solution)/shard_map/pallas_call | solution.py:497
  26.7 0.5 %collective-permute-start.10 = (f32[56,128]{1,0:T(8,128)S(1)}, f32[56,128]{1,0:T(8,128)S(1)}, u32[]{:S(2)}, u32[]{:S(2)}) collective-permute-start(f32[56,128]{1,0:T(8,128)S(1)} %get-tuple-element.117), channel_id=1, source_target_pairs={{0,8},{8,0},{16,24},{24,16},{1,9},{9,1},{17,25},{25,17},{2,10},{10... | collective-permute-start | bytes 86024 | tf_op jit(solution)/shard_map/ppermute | solution.py:541
  27.2 2.0 %collective-permute-start.11 = (f32[56,128]{1,0:T(8,128)S(1)}, f32[56,128]{1,0:T(8,128)S(1)}, u32[]{:S(2)}, u32[]{:S(2)}) collective-permute-start(f32[56,128]{1,0:T(8,128)S(1)} %get-tuple-element.118), channel_id=1, source_target_pairs={{8,16},{16,8},{24,0},{0,24},{9,17},{17,9},{25,1},{1,25},{10,18},{1... | collective-permute-start | bytes 86024 | tf_op jit(solution)/shard_map/ppermute | solution.py:541
  29.3 1.2 %collective-permute-start.12 = (f32[56,128]{1,0:T(8,128)S(1)}, f32[56,128]{1,0:T(8,128)S(1)}, u32[]{:S(2)}, u32[]{:S(2)}) collective-permute-start(f32[56,128]{1,0:T(8,128)S(1)} %get-tuple-element.119), channel_id=1, source_target_pairs={{0,4},{4,0},{1,5},{5,1},{2,6},{6,2},{3,7},{7,3},{8,12},{12,8},{9,1... | collective-permute-start | bytes 86024 | tf_op jit(solution)/shard_map/ppermute | solution.py:541
  30.5 0.8 %collective-permute-start.13 = (f32[56,128]{1,0:T(8,128)S(1)}, f32[56,128]{1,0:T(8,128)S(1)}, u32[]{:S(2)}, u32[]{:S(2)}) collective-permute-start(f32[56,128]{1,0:T(8,128)S(1)} %get-tuple-element.120), channel_id=1, source_target_pairs={{0,1},{1,0},{2,3},{3,2},{4,5},{5,4},{6,7},{7,6},{8,9},{9,8},{10,11... | collective-permute-start | bytes 86024 | tf_op jit(solution)/shard_map/ppermute | solution.py:541
  31.3 0.8 %collective-permute-start.14 = (f32[56,128]{1,0:T(8,128)S(1)}, f32[56,128]{1,0:T(8,128)S(1)}, u32[]{:S(2)}, u32[]{:S(2)}) collective-permute-start(f32[56,128]{1,0:T(8,128)S(1)} %get-tuple-element.121), channel_id=1, source_target_pairs={{1,2},{2,1},{3,0},{0,3},{5,6},{6,5},{7,4},{4,7},{9,10},{10,9},{11,... | collective-permute-start | bytes 86024 | tf_op jit(solution)/shard_map/ppermute | solution.py:541
  32.1 1.0 %shard_map.105 = (f32[504,128]{1,0:T(8,128)S(1)}, f32[280,128]{1,0:T(8,128)S(1)}) custom-call(bf16[192,640]{1,0:T(8,128)(2,1)S(1)} %get-tuple-element.122.refs_0_, f32[96,640]{1,0:T(8,128)S(1)} %get-tuple-element.123.refs_1_, bf16[448,256]{1,0:T(8,128)(2,1)S(1)} %get-tuple-element.124.refs_2_, bf16[168,192]{1,0:T(8,128)(2,1)S(1)} %get-tuple-element.109.refs_3_, ...), custom_call_target="tpu_custom_call" | custom-call | flops 1073741824 | bytes 2097152 | tf_op jit(solution)/shard_map/pallas_call | solution.py:497
  33.2 1.4 %collective-permute-done.14.refs_4_ = f32[56,128]{1,0:T(8,128)S(1)} collective-permute-done((f32[56,128]{1,0:T(8,128)S(1)}, f32[56,128]{1,0:T(8,128)S(1)}, u32[]{:S(2)}, u32[]{:S(2)}) %collective-permute-start.14) | collective-permute-done | bytes 28704 | tf_op jit(solution)/shard_map/ppermute | solution.py:541
  34.6 3.9 %shard_map.106 = (f32[504,128]{1,0:T(8,128)S(1)}, f32[280,128]{1,0:T(8,128)S(1)}, f32[280,128]{1,0:T(8,128)S(1)}, bf16[192,640]{1,0:T(8,128)(2,1)S(1)}, f32[96,6...) custom-call(f32[56,128]{1,0:T(8,128)S(1)} %collective-permute-done.1, ...), custom_call_target="tpu_custom_call" | custom-call | flops 1073741824 | bytes 2097152 | tf_op jit(solution)/shard_map/pallas_call | solution.py:497
  38.5 0.5 collective-permute-start.15
  39.0 0.7 %collective-permute-start.16 = (f32[56,128]{1,0:T(8,128)S(1)}, f32[56,128]{1,0:T(8,128)S(1)}, u32[]{:S(2)}, u32[]{:S(2)}) collective-permute-start(f32[56,128]{1,0:T(8,128)S(1)} %get-tuple-element.131), channel_id=1, source_target_pairs={{8,16},{16,8},{24,0},{0,24},{9,17},{17,9},{25,1},{1,25},{10,18},{1... | collective-permute-start | bytes 86024 | tf_op jit(solution)/shard_map/ppermute | solution.py:541
  39.7 1.1 %collective-permute-start.17 = (f32[56,128]{1,0:T(8,128)S(1)}, f32[56,128]{1,0:T(8,128)S(1)}, u32[]{:S(2)}, u32[]{:S(2)}) collective-permute-start(f32[56,128]{1,0:T(8,128)S(1)} %get-tuple-element.132), channel_id=1, source_target_pairs={{0,4},{4,0},{1,5},{5,1},{2,6},{6,2},{3,7},{7,3},{8,12},{12,8},{9,1... | collective-permute-start | bytes 86024 | tf_op jit(solution)/shard_map/ppermute | solution.py:541
  40.8 0.8 %collective-permute-start.18 = (f32[56,128]{1,0:T(8,128)S(1)}, f32[56,128]{1,0:T(8,128)S(1)}, u32[]{:S(2)}, u32[]{:S(2)}) collective-permute-start(f32[56,128]{1,0:T(8,128)S(1)} %get-tuple-element.133), channel_id=1, source_target_pairs={{0,1},{1,0},{2,3},{3,2},{4,5},{5,4},{6,7},{7,6},{8,9},{9,8},{10,11... | collective-permute-start | bytes 86024 | tf_op jit(solution)/shard_map/ppermute | solution.py:541
  41.7 0.8 %collective-permute-start.19 = (f32[56,128]{1,0:T(8,128)S(1)}, f32[56,128]{1,0:T(8,128)S(1)}, u32[]{:S(2)}, u32[]{:S(2)}) collective-permute-start(f32[56,128]{1,0:T(8,128)S(1)} %get-tuple-element.134), channel_id=1, source_target_pairs={{1,2},{2,1},{3,0},{0,3},{5,6},{6,5},{7,4},{4,7},{9,10},{10,9},{11,... | collective-permute-start | bytes 86024 | tf_op jit(solution)/shard_map/ppermute | solution.py:541
  42.5 1.8 %shard_map.107 = (f32[504,128]{1,0:T(8,128)S(1)}, f32[6,504,128]{2,1,0:T(8,128)S(1)}, f32[504,128]{1,0:T(8,128)S(1)}, f32[280,128]{1,0:T(8,128)}) custom-call(bf16[192,640]{1,0:T(8,128)(2,1)S(1)} %get-tuple-element.135.refs_0_, f32[96,640]{1,0:T(8,128)S(1)} %get-tuple-element.136.refs_1_, bf16[448,256]{1,0:T(8,128)(2,1)S(1)} %get-tuple-element.137.refs_2_, ...), custom_call_target="tpu_custom_call" | custom-call | flops 1073741824 | bytes 2097152 | tf_op jit(solution)/shard_map/pallas_call | solution.py:497
  44.3 0.6 %collective-permute-done.19.refs_4_ = f32[56,128]{1,0:T(8,128)S(1)} collective-permute-done((f32[56,128]{1,0:T(8,128)S(1)}, f32[56,128]{1,0:T(8,128)S(1)}, u32[]{:S(2)}, u32[]{:S(2)}) %collective-permute-start.19) | collective-permute-done | bytes 28704 | tf_op jit(solution)/shard_map/ppermute | solution.py:541
  45.0 5.0 %shard_map.108 = f32[504,128]{1,0:T(8,128)} custom-call(f32[56,128]{1,0:T(8,128)S(1)} %collective-permute-done.15.refs_0_, f32[56,128]{1,0:T(8,128)S(1)} %collective-permute-done.16.refs_1_, f32[56,128]{1,0:T(8,128)S(1)} %collective-permute-done.17.refs_2_, f32[56,128]{1,0:T(8,128)S(1)} %collective-permute-done.18.refs_3_, ...), custom_call_target="tpu_custom_call" | custom-call | flops 1073741824 | bytes 2097152 | tf_op jit(solution)/shard_map/pallas_call | solution.py:497
  (18 shorter events, 0.5 us)
Async XLA Ops:
  2.1 10.2 %collective-permute-start = (f32[56,128]{1,0:T(8,128)S(1)}, f32[56,128]{1,0:T(8,128)S(1)}, u32[]{:S(2)}, u32[]{:S(2)}) collective-permute-start(f32[56,128]{1,0:T(8,128)S(1)} %get-tuple-element.75), channel_id=1, source_target_pairs={{0,8},{8,0},{16,24},{24,16},{1,9},{9,1},{17,25},{25,17},{2,10},{10... | collective-permute-start | bytes 86024 | tf_op jit(solution)/shard_map/ppermute | solution.py:541
  4.3 8.0 %collective-permute-start.1 = (f32[56,128]{1,0:T(8,128)S(1)}, f32[56,128]{1,0:T(8,128)S(1)}, u32[]{:S(2)}, u32[]{:S(2)}) collective-permute-start(f32[56,128]{1,0:T(8,128)S(1)} %get-tuple-element.76), channel_id=1, source_target_pairs={{8,16},{16,8},{24,0},{0,24},{9,17},{17,9},{25,1},{1,25},{10,18},{1... | collective-permute-start | bytes 86024 | tf_op jit(solution)/shard_map/ppermute | solution.py:541
  6.5 5.8 %collective-permute-start.2 = (f32[56,128]{1,0:T(8,128)S(1)}, f32[56,128]{1,0:T(8,128)S(1)}, u32[]{:S(2)}, u32[]{:S(2)}) collective-permute-start(f32[56,128]{1,0:T(8,128)S(1)} %get-tuple-element.77), channel_id=1, source_target_pairs={{0,4},{4,0},{1,5},{5,1},{2,6},{6,2},{3,7},{7,3},{8,12},{12,8},{9,1... | collective-permute-start | bytes 86024 | tf_op jit(solution)/shard_map/ppermute | solution.py:541
  7.7 4.6 %collective-permute-start.3 = (f32[56,128]{1,0:T(8,128)S(1)}, f32[56,128]{1,0:T(8,128)S(1)}, u32[]{:S(2)}, u32[]{:S(2)}) collective-permute-start(f32[56,128]{1,0:T(8,128)S(1)} %get-tuple-element.78), channel_id=1, source_target_pairs={{0,1},{1,0},{2,3},{3,2},{4,5},{5,4},{6,7},{7,6},{8,9},{9,8},{10,11... | collective-permute-start | bytes 86024 | tf_op jit(solution)/shard_map/ppermute | solution.py:541
  9.2 3.3 %collective-permute-start.4 = (f32[56,128]{1,0:T(8,128)S(1)}, f32[56,128]{1,0:T(8,128)S(1)}, u32[]{:S(2)}, u32[]{:S(2)}) collective-permute-start(f32[56,128]{1,0:T(8,128)S(1)} %get-tuple-element.79), channel_id=1, source_target_pairs={{1,2},{2,1},{3,0},{0,3},{5,6},{6,5},{7,4},{4,7},{9,10},{10,9},{11,... | collective-permute-start | bytes 86024 | tf_op jit(solution)/shard_map/ppermute | solution.py:541
  16.6 4.7 %collective-permute-start.5 = (f32[56,128]{1,0:T(8,128)S(1)}, f32[56,128]{1,0:T(8,128)S(1)}, u32[]{:S(2)}, u32[]{:S(2)}) collective-permute-start(f32[56,128]{1,0:T(8,128)S(1)} %get-tuple-element.101), channel_id=1, source_target_pairs={{0,8},{8,0},{16,24},{24,16},{1,9},{9,1},{17,25},{25,17},{2,10},{10... | collective-permute-start | bytes 86024 | tf_op jit(solution)/shard_map/ppermute | solution.py:541
  17.1 4.5 %collective-permute-start.6 = (f32[56,128]{1,0:T(8,128)S(1)}, f32[56,128]{1,0:T(8,128)S(1)}, u32[]{:S(2)}, u32[]{:S(2)}) collective-permute-start(f32[56,128]{1,0:T(8,128)S(1)} %get-tuple-element.102), channel_id=1, source_target_pairs={{8,16},{16,8},{24,0},{0,24},{9,17},{17,9},{25,1},{1,25},{10,18},{1... | collective-permute-start | bytes 86024 | tf_op jit(solution)/shard_map/ppermute | solution.py:541
  17.8 3.8 %collective-permute-start.7 = (f32[56,128]{1,0:T(8,128)S(1)}, f32[56,128]{1,0:T(8,128)S(1)}, u32[]{:S(2)}, u32[]{:S(2)}) collective-permute-start(f32[56,128]{1,0:T(8,128)S(1)} %get-tuple-element.103), channel_id=1, source_target_pairs={{0,4},{4,0},{1,5},{5,1},{2,6},{6,2},{3,7},{7,3},{8,12},{12,8},{9,1... | collective-permute-start | bytes 86024 | tf_op jit(solution)/shard_map/ppermute | solution.py:541
  18.2 3.5 %collective-permute-start.8 = (f32[56,128]{1,0:T(8,128)S(1)}, f32[56,128]{1,0:T(8,128)S(1)}, u32[]{:S(2)}, u32[]{:S(2)}) collective-permute-start(f32[56,128]{1,0:T(8,128)S(1)} %get-tuple-element.104), channel_id=1, source_target_pairs={{0,1},{1,0},{2,3},{3,2},{4,5},{5,4},{6,7},{7,6},{8,9},{9,8},{10,11... | collective-permute-start | bytes 86024 | tf_op jit(solution)/shard_map/ppermute | solution.py:541
  19.2 3.6 %collective-permute-start.9 = (f32[56,128]{1,0:T(8,128)S(1)}, f32[56,128]{1,0:T(8,128)S(1)}, u32[]{:S(2)}, u32[]{:S(2)}) collective-permute-start(f32[56,128]{1,0:T(8,128)S(1)} %get-tuple-element.105), channel_id=1, source_target_pairs={{1,2},{2,1},{3,0},{0,3},{5,6},{6,5},{7,4},{4,7},{9,10},{10,9},{11,... | collective-permute-start | bytes 86024 | tf_op jit(solution)/shard_map/ppermute | solution.py:541
  26.7 6.5 %collective-permute-start.10 = (f32[56,128]{1,0:T(8,128)S(1)}, f32[56,128]{1,0:T(8,128)S(1)}, u32[]{:S(2)}, u32[]{:S(2)}) collective-permute-start(f32[56,128]{1,0:T(8,128)S(1)} %get-tuple-element.117), channel_id=1, source_target_pairs={{0,8},{8,0},{16,24},{24,16},{1,9},{9,1},{17,25},{25,17},{2,10},{10... | collective-permute-start | bytes 86024 | tf_op jit(solution)/shard_map/ppermute | solution.py:541
  27.2 5.9 %collective-permute-start.11 = (f32[56,128]{1,0:T(8,128)S(1)}, f32[56,128]{1,0:T(8,128)S(1)}, u32[]{:S(2)}, u32[]{:S(2)}) collective-permute-start(f32[56,128]{1,0:T(8,128)S(1)} %get-tuple-element.118), channel_id=1, source_target_pairs={{8,16},{16,8},{24,0},{0,24},{9,17},{17,9},{25,1},{1,25},{10,18},{1... | collective-permute-start | bytes 86024 | tf_op jit(solution)/shard_map/ppermute | solution.py:541
  29.3 3.9 %collective-permute-start.12 = (f32[56,128]{1,0:T(8,128)S(1)}, f32[56,128]{1,0:T(8,128)S(1)}, u32[]{:S(2)}, u32[]{:S(2)}) collective-permute-start(f32[56,128]{1,0:T(8,128)S(1)} %get-tuple-element.119), channel_id=1, source_target_pairs={{0,4},{4,0},{1,5},{5,1},{2,6},{6,2},{3,7},{7,3},{8,12},{12,8},{9,1... | collective-permute-start | bytes 86024 | tf_op jit(solution)/shard_map/ppermute | solution.py:541
  30.5 2.7 %collective-permute-start.13 = (f32[56,128]{1,0:T(8,128)S(1)}, f32[56,128]{1,0:T(8,128)S(1)}, u32[]{:S(2)}, u32[]{:S(2)}) collective-permute-start(f32[56,128]{1,0:T(8,128)S(1)} %get-tuple-element.120), channel_id=1, source_target_pairs={{0,1},{1,0},{2,3},{3,2},{4,5},{5,4},{6,7},{7,6},{8,9},{9,8},{10,11... | collective-permute-start | bytes 86024 | tf_op jit(solution)/shard_map/ppermute | solution.py:541
  31.3 3.3 %collective-permute-start.14 = (f32[56,128]{1,0:T(8,128)S(1)}, f32[56,128]{1,0:T(8,128)S(1)}, u32[]{:S(2)}, u32[]{:S(2)}) collective-permute-start(f32[56,128]{1,0:T(8,128)S(1)} %get-tuple-element.121), channel_id=1, source_target_pairs={{1,2},{2,1},{3,0},{0,3},{5,6},{6,5},{7,4},{4,7},{9,10},{10,9},{11,... | collective-permute-start | bytes 86024 | tf_op jit(solution)/shard_map/ppermute | solution.py:541
  38.5 5.8 %collective-permute-start.15 = (f32[56,128]{1,0:T(8,128)S(1)}, f32[56,128]{1,0:T(8,128)S(1)}, u32[]{:S(2)}, u32[]{:S(2)}) collective-permute-start(f32[56,128]{1,0:T(8,128)S(1)} %get-tuple-element.130), channel_id=1, source_target_pairs={{0,8},{8,0},{16,24},{24,16},{1,9},{9,1},{17,25},{25,17},{2,10},{10... | collective-permute-start | bytes 86024 | tf_op jit(solution)/shard_map/ppermute | solution.py:541
  39.0 5.3 %collective-permute-start.16 = (f32[56,128]{1,0:T(8,128)S(1)}, f32[56,128]{1,0:T(8,128)S(1)}, u32[]{:S(2)}, u32[]{:S(2)}) collective-permute-start(f32[56,128]{1,0:T(8,128)S(1)} %get-tuple-element.131), channel_id=1, source_target_pairs={{8,16},{16,8},{24,0},{0,24},{9,17},{17,9},{25,1},{1,25},{10,18},{1... | collective-permute-start | bytes 86024 | tf_op jit(solution)/shard_map/ppermute | solution.py:541
  39.7 4.6 %collective-permute-start.17 = (f32[56,128]{1,0:T(8,128)S(1)}, f32[56,128]{1,0:T(8,128)S(1)}, u32[]{:S(2)}, u32[]{:S(2)}) collective-permute-start(f32[56,128]{1,0:T(8,128)S(1)} %get-tuple-element.132), channel_id=1, source_target_pairs={{0,4},{4,0},{1,5},{5,1},{2,6},{6,2},{3,7},{7,3},{8,12},{12,8},{9,1... | collective-permute-start | bytes 86024 | tf_op jit(solution)/shard_map/ppermute | solution.py:541
  40.8 3.5 %collective-permute-start.18 = (f32[56,128]{1,0:T(8,128)S(1)}, f32[56,128]{1,0:T(8,128)S(1)}, u32[]{:S(2)}, u32[]{:S(2)}) collective-permute-start(f32[56,128]{1,0:T(8,128)S(1)} %get-tuple-element.133), channel_id=1, source_target_pairs={{0,1},{1,0},{2,3},{3,2},{4,5},{5,4},{6,7},{7,6},{8,9},{9,8},{10,11... | collective-permute-start | bytes 86024 | tf_op jit(solution)/shard_map/ppermute | solution.py:541
  41.7 3.3 %collective-permute-start.19 = (f32[56,128]{1,0:T(8,128)S(1)}, f32[56,128]{1,0:T(8,128)S(1)}, u32[]{:S(2)}, u32[]{:S(2)}) collective-permute-start(f32[56,128]{1,0:T(8,128)S(1)} %get-tuple-element.134), channel_id=1, source_target_pairs={{1,2},{2,1},{3,0},{0,3},{5,6},{6,5},{7,4},{4,7},{9,10},{10,9},{11,... | collective-permute-start | bytes 86024 | tf_op jit(solution)/shard_map/ppermute | solution.py:541

commit v2 on v1

--- a/solution.py
+++ b/solution.py
@@ -19,6 +19,7 @@
 
 
 AXES = ("gx", "gy", "gz")
+ORDER = (("gx", 1), ("gx", 0), ("gz", 1), ("gy", 1), ("gy", 0), ("gz", 0))
 
 
 def matchings():
@@ -32,6 +33,7 @@
             if first == 1 and size % 2 == 0:
                 links.append((size - 1, 0))
             plan.append((axis, [q for i, j in links for q in ((i, j), (j, i))], first))
+    plan.sort(key=lambda entry: ORDER.index((entry[0], entry[2])))
     return plan
 
 
@@ -265,7 +267,7 @@
 
 
 def set_up(z, plan, deriv, volume, square, partner, cluster, ohs, star, across, local, outs, scratch):
-    s3, v3, pt, ohr, ohl, ohs_half, ohl_half, index, star_pairs, across_pairs, local_pairs = outs
+    s3, v3, pt, ohr, ohl, ohr_pairs, ohs_half, ohl_half, index, star_pairs, across_pairs, local_pairs = outs
     wide, block, picks = scratch
     wide[...] = jnp.zeros_like(wide)
     block[...] = jnp.zeros_like(block)
@@ -310,7 +312,10 @@
     index[0:1, :] = pick
     index[1:2, :] = jnp.maximum(rank, 0)
     index[2:3, :] = jnp.where(fast, 1, 0)
-    for c in range(z.C):
+    both = jnp.concatenate([chosen, chosen], axis=0)
+    for c in range(z.C):
+        pairs = lax.dot_general(ohr[:, lane(z, c)], both, (((1,), (1,)), ((), ())), preferred_element_type=F32)
+        ohr_pairs[:, lane(z, c)] = pairs.astype(BF)
         rows = slice(c * z.H, (c + 1) * z.H)
         ohs_half[rows, :] = dot(chosen, ohs[lane(z, c), :]).astype(BF)
         ohl_half[rows, :] = dot(chosen, ohl[lane(z, c), :]).astype(BF)
@@ -327,7 +332,7 @@
 
 def first_local_kernel(z, plan, *refs):
     deriv, volume, square, partner, cluster, ohs, star, across, local, y3, traces, sx = refs[:12]
-    outs, src, refs = refs[12:23], refs[23], refs[24:]
+    outs, src, half, refs = refs[12:24], refs[24], refs[25], refs[26:]
     turned, u, gathered, *scratch = refs
     set_up(z, plan, deriv, volume, square, partner, cluster, ohs, star, across, local, outs, scratch)
     v3, pt, ohl = outs[1], outs[2], outs[4]
@@ -344,6 +349,9 @@
         start = [lifted[:, lane(z, g)] for g in group]
         for g, total in zip(group, star_sum(z, start, group, turned, star, z.F)):
             src[g * z.M:(g + 1) * z.M, :] = total
+    index = outs[8]
+    for p, value in enumerate(compact(z, index[0:1, :], lambda f: src[f * z.M:(f + 1) * z.M, :])):
+        half[p * z.M:(p + 1) * z.M, :] = value
 
 
 def lift_gathered(z, gathered, u, pt):
@@ -356,16 +364,16 @@
 
 
 def local_kernel(z, last, *refs):
-    y3, traces, sx, v3, pt, star, local, ohl, index, src_in, half_in = refs[:11]
-    refs = refs[11:]
+    y3, traces, sx, v3, pt, star, local, ohl, index, src_in, half_in, stacked, ohr = refs[:13]
+    refs = refs[13:]
     if last:
         older, start, moved, refs = refs[0:2], refs[2], refs[3], refs[4:]
-        src_out, weights, base, refs = refs[0], refs[1], refs[2], refs[3:]
-        half_out = refs[0]
-        refs = refs[1:]
+        src_out, weights, base, half_out, refs = refs[0], refs[1], refs[2], refs[3], refs[4:]
     else:
-        src_out, half_out, refs = refs[0], refs[1], refs[2:]
-    turned, u, gathered, u_half, lifted = refs
+        src_full, src_out, half_out, refs = refs[0], refs[1], refs[2], refs[3:]
+    turned, u, gathered, u_half, lifted, u_far, gathered_far, landed = refs
+    gathered_far[...] = dot(stacked[...], ohr[...])
+    landed[...] = lift_gathered(z, gathered_far, u_far, pt)
     turned[...] = dot(v3[...], y3[...])
     gathered[...] = dot(sx[...], ohl[...])
     for c in range(z.C):
@@ -385,13 +393,14 @@
     fast = index[2:3, :] > 0
     for g in range(z.F):
         rows = slice(g * z.M, (g + 1) * z.M)
-        value = src_in[rows, :] + lifted[:, lane(z, g)]
+        whole = src_in[rows, :] + landed[:, lane(z, g)]
+        value = whole + lifted[:, lane(z, g)]
         if last:
             pairs = lambda p: half_out[p * z.M:(p + 1) * z.M, :]
             src_out[rows, :] = jnp.where(fast, expand(z, rank, pairs, g), value)
             pairs = lambda p: moved[p * z.M:(p + 1) * z.M, :]
             base[rows, :] = start[rows, :] + jnp.where(fast, expand(z, rank, pairs, g), 0.0)
-            sources = [x[rows, :] for x in older] + [src_in[rows, :]]
+            sources = [x[rows, :] for x in older] + [whole]
             sources = [jnp.where(fast, 0.0, x) for x in sources]
             for k in range(TERMS):
                 total = None
@@ -400,10 +409,11 @@
                     total = c * x if total is None else total + c * x
                 weights[k, rows, :] = total
         else:
+            src_full[rows, :] = whole
             src_out[rows, :] = value
 
 
-def arrive(z, arrived, ohr, pt, landed, stacked, gathered, u):
+def arrive(z, arrived, landed, stacked):
     for i, group in enumerate(groups_of(z.K, z.Q)):
         for q in range(z.Q):
             rows = min(z.R, (q + 1) * z.QR) - q * z.QR
@@ -411,45 +421,61 @@
     hi, lo = halves(landed[...])
     stacked[0:z.R, :] = hi
     stacked[z.RP:z.RP + z.R, :] = lo
-    gathered[...] = dot(stacked[...], ohr[...])
-    return lift_gathered(z, gathered, u, pt)
+
+
+def lift_pairs(z, gathered, u, pt):
+    low = low_lanes(z, z.BP)
+    for c in range(z.C):
+        for p in range(z.FP):
+            parts = []
+            for at in (0, z.RP):
+                a = gathered[at + 2 * p * z.BP:at + (2 * p + 1) * z.BP, lane(z, c)]
+                b = gathered[at + (2 * p + 1) * z.BP:at + (2 * p + 2) * z.BP, lane(z, c)] if 2 * p + 1 < z.F else 0.0
+                parts.append(filled(jnp.where(low, a, b), z.BQ).astype(BF))
+            put_face(z, u, c, lane(z, p), *parts)
+    return lift(z, pt, u)
 
 
 def step_kernel(z, first, *refs):
     arrived, refs = refs[:z.K], refs[z.K:]
-    src_in, half_in, moved_in, s3, p3, pt, star, across, ohr, ohs, index = refs[:11]
-    src_out, half, moved, y3, traces, sx = refs[11:17]
-    messages, refs = refs[17:17 + z.K], refs[17 + z.K:]
-    landed, stacked, gathered, u, lifted, turned, change, sent, picked = refs
-    lifted[...] = arrive(z, arrived, ohr, pt, landed, stacked, gathered, u)
-    for g in range(z.F):
-        rows = slice(g * z.M, (g + 1) * z.M)
-        src_out[rows, :] = src_in[rows, :] + lifted[:, lane(z, g)]
-    if first:
-        gained = compact(z, index[0:1, :], lambda f: src_out[f * z.M:(f + 1) * z.M, :])
-    else:
-        gained = compact(z, index[0:1, :], lambda f: lifted[:, lane(z, f)])
+    half_in, moved_in, s3, p3, pt, star, across, ohr, ohs = refs[:9]
+    half, moved, y3, traces, sx, stacked = refs[9:15]
+    messages, refs = refs[15:15 + z.K], refs[15 + z.K:]
+    landed, gathered, u, turned, other, change, sent, picked = refs
+    arrive(z, arrived, landed, stacked)
+    gathered[...] = dot(stacked[...], ohr[...])
+    gained = lift_pairs(z, gathered, u, pt)
     row = coefficients(0.0, 1.0 / FINE_STEPS)
     for p in range(z.FP):
         rows = slice(p * z.M, (p + 1) * z.M)
-        value = gained[p] if first else half_in[rows, :] + gained[p]
+        value = half_in[rows, :] + gained[:, lane(z, p)]
         half[rows, :] = value
         put_field(z, y3, p, row[TERMS - 1] * value)
 
-    def term(i, carry):
-        c = F32(row[TERMS - 2])
-        for k in range(TERMS - 2):
-            c = jnp.where(i == TERMS - 2 - k, F32(row[k]), c)
-        balanced(z, turned, s3, y3)
-        for p in range(z.FP):
-            rows = slice(p * z.M, (p + 1) * z.M)
-            total = c * half[rows, :] + star_pair(z, p, turned, star)
-            put_field(z, y3, p, total)
-            change[rows, :] = total
-        return carry
-
-    lax.fori_loop(0, TERMS - 1, term, 0)
+    buffers = (turned, other)
+
+    def product(out, pairs):
+        lanes = slice(pairs[0] * z.E, (pairs[-1] + 1) * z.E)
+        out[:, lanes] = dot(s3[...], y3[:, lanes])
+
+    tiles = groups_of(z.FP, 2)
+    for pairs in tiles:
+        product(turned, pairs)
+    for k in range(TERMS - 2, -1, -1):
+        now, later = buffers if k % 2 == 0 else buffers[::-1]
+        for pairs in tiles:
+            for p in pairs:
+                rows = slice(p * z.M, (p + 1) * z.M)
+                total = row[k] * half[rows, :] + star_pair(z, p, now, star)
+                if k > 0:
+                    put_field(z, y3, p, total)
+                else:
+                    change[rows, :] = total
+            if k > 0:
+                product(later, pairs)
     moved[...] = change[...] if first else moved_in[...] + change[...]
+    for p in range(z.FP):
+        put_field(z, y3, p, change[p * z.M:(p + 1) * z.M, :])
     traces[...] = dot(p3[...], y3[...])
     for pair in groups_of(z.C, 2):
         t = [face_rows(z, traces, c, z.FP) for c in pair]
@@ -463,7 +489,9 @@
     arrived, refs = refs[:z.K], refs[z.K:]
     src_in, weights, base, s3, pt, star, ohr, out = refs[:8]
     landed, stacked, gathered, u, lifted, turned, y3, src = refs[8:]
-    lifted[...] = arrive(z, arrived, ohr, pt, landed, stacked, gathered, u)
+    arrive(z, arrived, landed, stacked)
+    gathered[...] = dot(stacked[...], ohr[...])
+    lifted[...] = lift_gathered(z, gathered, u, pt)
     row = coefficients(0.0, 1.0 / FINE_STEPS)
     for g in range(z.F):
         rows = slice(g * z.M, (g + 1) * z.M)
@@ -556,35 +584,35 @@
         *args, remote=True,
     )
     arrived = trade(messages)
-    s3, v3, pt, ohr, ohl, ohs_half, ohl_half, index, star_pairs, across_pairs, local_pairs, src = call(
+    s3, v3, pt, ohr, ohl, ohr_pairs, ohs_half, ohl_half, index, star_pairs, across_pairs, local_pairs, src, half_src = call(
         functools.partial(first_local_kernel, z, plan),
         [((3 * modes, 3 * z.MP), BF), ((3 * modes, 3 * z.MP), BF), ((modes, 3 * faces * z.BQ), BF), ((z.KW, z.S), BF),
-         ((z.S, z.S), BF), ((z.S // 2, z.KW), BF), ((z.S // 2, z.S), BF), ((8, members), jnp.int32),
-         pairs(3), pairs(faces), pairs(faces), full],
+         ((z.S, z.S), BF), ((z.KW, z.S), BF), ((z.S // 2, z.KW), BF), ((z.S // 2, z.S), BF), ((8, members), jnp.int32),
+         pairs(3), pairs(faces), pairs(faces), full, half],
         [turned, u, gathered, wide, ((128, 128), F32), ((8, members), F32)],
         deriv, volume, square, partner, cluster, ohs, star, across, local, y3v, tr, sxv,
     )
-    half_src = moved = jnp.zeros((8, members), F32)
+    moved = jnp.zeros((8, members), F32)
     sources = []
     for step in range(FINE_STEPS - 1, 0, -1):
-        src, half_src, moved, y3v, tr, sxv, *messages = call(
+        half_src, moved, y3v, tr, sxv, stack, *messages = call(
             functools.partial(step_kernel, z, step == FINE_STEPS - 1),
-            [full, half, half, y3_half, traces_half, sx_half] + messages_out,
-            [landed, stacked, gathered, u, lifted, turned_half, half, sent_half, picked],
-            *arrived, src, half_src, moved, s3, p3, pt, star_pairs, across_pairs, ohr, ohs_half, index,
+            [half, half, y3_half, traces_half, sx_half, stacked] + messages_out,
+            [landed, gathered, u_half, turned_half, turned_half, half, sent_half, picked],
+            *arrived, half_src, moved, s3, p3, pt, star_pairs, across_pairs, ohr_pairs, ohs_half,
         )
         arrived = trade(messages)
-        sources.append(src)
         last = step == 1
-        local_args = [y3v, tr, sxv, v3, pt, star_pairs, local_pairs, ohl_half, index, src, half_src]
-        local_scratch = [turned_half, u, gathered, u_half, lifted]
+        local_args = [y3v, tr, sxv, v3, pt, star_pairs, local_pairs, ohl_half, index, src, half_src, stack, ohr]
+        local_scratch = [turned_half, u, gathered, u_half, lifted, u, gathered, lifted]
         if last:
             src, weights, base, _ = call(
                 functools.partial(local_kernel, z, True), [full, ((TERMS,) + full[0], F32), full, half], local_scratch,
-                *local_args, *sources[:2], start, moved,
+                *local_args, *sources, start, moved,
             )
         else:
-            src, half_src = call(functools.partial(local_kernel, z, False), [full, half], local_scratch, *local_args)
+            whole, src, half_src = call(functools.partial(local_kernel, z, False), [full, full, half], local_scratch, *local_args)
+            sources.append(whole)
     (out,) = call(
         functools.partial(last_kernel, z), [full],
         [landed, stacked, gathered, u, lifted, marked(turned), y3, full],

time: 50.1 us -> 48.2 us (0.962); the launches traced: 50 us -> 47.5 us
  waiting for transfers between devices: 3.64 us -> 0.82 us
    ppermute x20, waiting for transfers between devices: 3.64 us -> 0.82 us  [trade(): lax.ppermute(m, axis, links)]
  transfers between devices with their start and end apart: 20 -> 20, of which waited for: 5 -> 4; matrix products, arithmetic and copies ran while one was open for 0% -> 0% of each run, Pallas kernels for 12% -> 15%
where the time goes in v2:
time: 48.2 us; the launch traced here: 47.5 us
  Pallas kernels  25.4 us (53%)
  starting transfers between devices  21.2 us (44%)
  waiting for transfers between devices  0.82 us (2%)
    pallas_call x9, Pallas kernels, call(): pl.pallas_call(kernel, out_shape=[jax.ShapeDtypeStruct(*o) for o in outs]...  25.4 us
    ppermute x20, starting transfers between devices, trade(): lax.ppermute(m, axis, links)  21.2 us
  transfers between devices with their start and end apart: 20, of which 4 were waited for; matrix products, arithmetic and copies ran while one was open for 0% of the time, Pallas kernels for 15%

profile of v2, /device:TPU:1, one launch (start us, length us, event | category | flops | bytes accessed | tf_op | source)
XLA Modules:
  0.0 47.5 jit_solution(16980984454438045949)
XLA Ops:
  0.0 2.0 %shard_map.100 = (f32[504,128]{1,0:T(8,128)S(1)}, f32[9,9,3,128]{3,2,1,0:T(4,128)S(1)}, f32[9,9,4,128]{3,2,1,0:T(4,128)S(1)}, f32[9,9,4,128]{3,2,1,0:T(4,128)S(1...) custom-call(f32[504,128]{1,0:T(8,128)} %bitcast.7, ...), custom_call_target="tpu_custom_call" | custom-call | flops 1073741824 | bytes 2097152 | tf_op jit(solution)/shard_map/pallas_call | solution.py:525
  2.1 4.2 %collective-permute-start = (f32[56,128]{1,0:T(8,128)S(1)}, f32[56,128]{1,0:T(8,128)S(1)}, u32[]{:S(2)}, u32[]{:S(2)}) collective-permute-start(f32[56,128]{1,0:T(8,128)S(1)} %get-tuple-element.79), channel_id=1, source_target_pairs={{8,16},{16,8},{24,0},{0,24},{9,17},{17,9},{25,1},{1,25},{10,18},{1... | collective-permute-start | bytes 86024 | tf_op jit(solution)/shard_map/ppermute | solution.py:569
  6.3 0.0 collective-permute-start.1
  6.3 2.1 %collective-permute-start.2 = (f32[56,128]{1,0:T(8,128)S(1)}, f32[56,128]{1,0:T(8,128)S(1)}, u32[]{:S(2)}, u32[]{:S(2)}) collective-permute-start(f32[56,128]{1,0:T(8,128)S(1)} %get-tuple-element.81), channel_id=1, source_target_pairs={{1,2},{2,1},{3,0},{0,3},{5,6},{6,5},{7,4},{4,7},{9,10},{10,9},{11,... | collective-permute-start | bytes 86024 | tf_op jit(solution)/shard_map/ppermute | solution.py:569
  8.3 1.2 %collective-permute-start.3 = (f32[56,128]{1,0:T(8,128)S(1)}, f32[56,128]{1,0:T(8,128)S(1)}, u32[]{:S(2)}, u32[]{:S(2)}) collective-permute-start(f32[56,128]{1,0:T(8,128)S(1)} %get-tuple-element.82), channel_id=1, source_target_pairs={{0,4},{4,0},{1,5},{5,1},{2,6},{6,2},{3,7},{7,3},{8,12},{12,8},{9,1... | collective-permute-start | bytes 86024 | tf_op jit(solution)/shard_map/ppermute | solution.py:569
  9.6 0.0 collective-permute-start.4
  9.6 2.1 %shard_map.101 = (bf16[168,192]{1,0:T(8,128)(2,1)S(1)}, bf16[168,192]{1,0:T(8,128)(2,1)S(1)}, bf16[56,384]{1,0:T(8,128)(2,1)S(1)}, bf16[256,512]{1,0:T(8,128)(2,...) custom-call(f32[3,56,56]{2,1,0:T(8,128)S(1)} %get-tuple-element.84.r, ...), custom_call_target="tpu_custom_call" | custom-call | flops 1073741824 | bytes 2097152 | tf_op jit(solution)/shard_map/pallas_call | solution.py:525
  11.7 0.0 collective-permute-done.1.refs_1_
  11.7 0.0 collective-permute-done.2.refs_2_
  11.7 0.0 collective-permute-done.4.refs_4_
  11.7 3.7 %shard_map.102 = (f32[280,128]{1,0:T(8,128)S(1)}, f32[280,128]{1,0:T(8,128)S(1)}, bf16[192,640]{1,0:T(8,128)(2,1)S(1)}, f32[96,640]{1,0:T(8,128)S(1)}, bf16[448,...) custom-call(f32[56,128]{1,0:T(8,128)S(1)} %collective-permute-done.r, ...), custom_call_target="tpu_custom_call" | custom-call | flops 1073741824 | bytes 2097152 | tf_op jit(solution)/shard_map/pallas_call | solution.py:525
  15.4 0.7 %collective-permute-start.5 = (f32[56,128]{1,0:T(8,128)S(1)}, f32[56,128]{1,0:T(8,128)S(1)}, u32[]{:S(2)}, u32[]{:S(2)}) collective-permute-start(f32[56,128]{1,0:T(8,128)S(1)} %get-tuple-element.104), channel_id=1, source_target_pairs={{8,16},{16,8},{24,0},{0,24},{9,17},{17,9},{25,1},{1,25},{10,18},{1... | collective-permute-start | bytes 86024 | tf_op jit(solution)/shard_map/ppermute | solution.py:569
  16.1 1.2 %collective-permute-start.6 = (f32[56,128]{1,0:T(8,128)S(1)}, f32[56,128]{1,0:T(8,128)S(1)}, u32[]{:S(2)}, u32[]{:S(2)}) collective-permute-start(f32[56,128]{1,0:T(8,128)S(1)} %get-tuple-element.105), channel_id=1, source_target_pairs={{0,8},{8,0},{16,24},{24,16},{1,9},{9,1},{17,25},{25,17},{2,10},{10... | collective-permute-start | bytes 86024 | tf_op jit(solution)/shard_map/ppermute | solution.py:569
  17.3 0.9 %collective-permute-start.7 = (f32[56,128]{1,0:T(8,128)S(1)}, f32[56,128]{1,0:T(8,128)S(1)}, u32[]{:S(2)}, u32[]{:S(2)}) collective-permute-start(f32[56,128]{1,0:T(8,128)S(1)} %get-tuple-element.106), channel_id=1, source_target_pairs={{1,2},{2,1},{3,0},{0,3},{5,6},{6,5},{7,4},{4,7},{9,10},{10,9},{11,... | collective-permute-start | bytes 86024 | tf_op jit(solution)/shard_map/ppermute | solution.py:569
  18.2 1.1 %collective-permute-start.8 = (f32[56,128]{1,0:T(8,128)S(1)}, f32[56,128]{1,0:T(8,128)S(1)}, u32[]{:S(2)}, u32[]{:S(2)}) collective-permute-start(f32[56,128]{1,0:T(8,128)S(1)} %get-tuple-element.107), channel_id=1, source_target_pairs={{0,4},{4,0},{1,5},{5,1},{2,6},{6,2},{3,7},{7,3},{8,12},{12,8},{9,1... | collective-permute-start | bytes 86024 | tf_op jit(solution)/shard_map/ppermute | solution.py:569
  19.3 1.4 %shard_map.103 = (f32[504,128]{1,0:T(8,128)S(1)}, f32[504,128]{1,0:T(8,128)S(1)}, f32[280,128]{1,0:T(8,128)S(1)}) custom-call(bf16[192,640]{1,0:T(8,128)(2,1)S(1)} %get-tuple-element.109.refs_0_, f32[96,640]{1,0:T(8,128)S(1)} %get-tuple-element.110.refs_1_, bf16[448,256]{1,0:T(8,128)(2,1)S(1)} %get-tuple-element.111.refs_2_, ...), custom_call_target="tpu_custom_call" | custom-call | flops 1073741824 | bytes 2097152 | tf_op jit(solution)/shard_map/pallas_call | solution.py:525
  20.7 0.4 collective-permute-done.7.refs_2_
  21.1 0.1 collective-permute-done.8.refs_3_
  21.2 3.7 %shard_map.104 = (f32[280,128]{1,0:T(8,128)S(1)}, f32[280,128]{1,0:T(8,128)S(1)}, bf16[192,640]{1,0:T(8,128)(2,1)S(1)}, f32[96,640]{1,0:T(8,128)S(1)}, bf16[448,...) custom-call(f32[56,128]{1,0:T(8,128)S(1)} %collective-permute-done.5, ...), custom_call_target="tpu_custom_call" | custom-call | flops 1073741824 | bytes 2097152 | tf_op jit(solution)/shard_map/pallas_call | solution.py:525
  24.9 2.4 %collective-permute-start.10 = (f32[56,128]{1,0:T(8,128)S(1)}, f32[56,128]{1,0:T(8,128)S(1)}, u32[]{:S(2)}, u32[]{:S(2)}) collective-permute-start(f32[56,128]{1,0:T(8,128)S(1)} %get-tuple-element.122), channel_id=1, source_target_pairs={{8,16},{16,8},{24,0},{0,24},{9,17},{17,9},{25,1},{1,25},{10,18},{1... | collective-permute-start | bytes 86024 | tf_op jit(solution)/shard_map/ppermute | solution.py:569
  27.3 2.2 %collective-permute-start.12 = (f32[56,128]{1,0:T(8,128)S(1)}, f32[56,128]{1,0:T(8,128)S(1)}, u32[]{:S(2)}, u32[]{:S(2)}) collective-permute-start(f32[56,128]{1,0:T(8,128)S(1)} %get-tuple-element.124), channel_id=1, source_target_pairs={{1,2},{2,1},{3,0},{0,3},{5,6},{6,5},{7,4},{4,7},{9,10},{10,9},{11,... | collective-permute-start | bytes 86024 | tf_op jit(solution)/shard_map/ppermute | solution.py:569
  29.4 1.2 %collective-permute-start.13 = (f32[56,128]{1,0:T(8,128)S(1)}, f32[56,128]{1,0:T(8,128)S(1)}, u32[]{:S(2)}, u32[]{:S(2)}) collective-permute-start(f32[56,128]{1,0:T(8,128)S(1)} %get-tuple-element.125), channel_id=1, source_target_pairs={{0,4},{4,0},{1,5},{5,1},{2,6},{6,2},{3,7},{7,3},{8,12},{12,8},{9,1... | collective-permute-start | bytes 86024 | tf_op jit(solution)/shard_map/ppermute | solution.py:569
  30.7 1.6 %shard_map.105 = (f32[504,128]{1,0:T(8,128)S(1)}, f32[504,128]{1,0:T(8,128)S(1)}, f32[280,128]{1,0:T(8,128)S(1)}) custom-call(bf16[192,640]{1,0:T(8,128)(2,1)S(1)} %get-tuple-element.127.refs_0_, f32[96,640]{1,0:T(8,128)S(1)} %get-tuple-element.128.refs_1_, bf16[448,256]{1,0:T(8,128)(2,1)S(1)} %get-tuple-element.129.refs_2_, ...), custom_call_target="tpu_custom_call" | custom-call | flops 1073741824 | bytes 2097152 | tf_op jit(solution)/shard_map/pallas_call | solution.py:525
  32.3 0.2 collective-permute-done.13.refs_3_
  32.5 3.7 %shard_map.106 = (f32[280,128]{1,0:T(8,128)S(1)}, f32[280,128]{1,0:T(8,128)S(1)}, bf16[192,640]{1,0:T(8,128)(2,1)S(1)}, f32[96,640]{1,0:T(8,128)S(1)}, bf16[448,...) custom-call(f32[56,128]{1,0:T(8,128)S(1)} %collective-permute-done.1, ...), custom_call_target="tpu_custom_call" | custom-call | flops 1073741824 | bytes 2097152 | tf_op jit(solution)/shard_map/pallas_call | solution.py:525
  36.2 1.1 %collective-permute-start.15 = (f32[56,128]{1,0:T(8,128)S(1)}, f32[56,128]{1,0:T(8,128)S(1)}, u32[]{:S(2)}, u32[]{:S(2)}) collective-permute-start(f32[56,128]{1,0:T(8,128)S(1)} %get-tuple-element.135), channel_id=1, source_target_pairs={{8,16},{16,8},{24,0},{0,24},{9,17},{17,9},{25,1},{1,25},{10,18},{1... | collective-permute-start | bytes 86024 | tf_op jit(solution)/shard_map/ppermute | solution.py:569
  37.3 1.0 %collective-permute-start.16 = (f32[56,128]{1,0:T(8,128)S(1)}, f32[56,128]{1,0:T(8,128)S(1)}, u32[]{:S(2)}, u32[]{:S(2)}) collective-permute-start(f32[56,128]{1,0:T(8,128)S(1)} %get-tuple-element.136), channel_id=1, source_target_pairs={{0,8},{8,0},{16,24},{24,16},{1,9},{9,1},{17,25},{25,17},{2,10},{10... | collective-permute-start | bytes 86024 | tf_op jit(solution)/shard_map/ppermute | solution.py:569
  38.3 1.0 %collective-permute-start.17 = (f32[56,128]{1,0:T(8,128)S(1)}, f32[56,128]{1,0:T(8,128)S(1)}, u32[]{:S(2)}, u32[]{:S(2)}) collective-permute-start(f32[56,128]{1,0:T(8,128)S(1)} %get-tuple-element.137), channel_id=1, source_target_pairs={{1,2},{2,1},{3,0},{0,3},{5,6},{6,5},{7,4},{4,7},{9,10},{10,9},{11,... | collective-permute-start | bytes 86024 | tf_op jit(solution)/shard_map/ppermute | solution.py:569
  39.4 0.8 %collective-permute-start.18 = (f32[56,128]{1,0:T(8,128)S(1)}, f32[56,128]{1,0:T(8,128)S(1)}, u32[]{:S(2)}, u32[]{:S(2)}) collective-permute-start(f32[56,128]{1,0:T(8,128)S(1)} %get-tuple-element.138), channel_id=1, source_target_pairs={{0,4},{4,0},{1,5},{5,1},{2,6},{6,2},{3,7},{7,3},{8,12},{12,8},{9,1... | collective-permute-start | bytes 86024 | tf_op jit(solution)/shard_map/ppermute | solution.py:569
  40.1 2.2 %shard_map.107 = (f32[504,128]{1,0:T(8,128)S(1)}, f32[6,504,128]{2,1,0:T(8,128)S(1)}, f32[504,128]{1,0:T(8,128)S(1)}, f32[280,128]{1,0:T(8,128)}) custom-call(bf16[192,640]{1,0:T(8,128)(2,1)S(1)} %get-tuple-element.140.refs_0_, f32[96,640]{1,0:T(8,128)S(1)} %get-tuple-element.141.refs_1_, bf16[448,256]{1,0:T(8,128)(2,1)S(1)} %get-tuple-element.142.refs_2_, ...), custom_call_target="tpu_custom_call" | custom-call | flops 1073741824 | bytes 2097152 | tf_op jit(solution)/shard_map/pallas_call | solution.py:525
  42.4 0.1 collective-permute-done.18.refs_3_
  42.5 5.0 %shard_map.108 = f32[504,128]{1,0:T(8,128)} custom-call(f32[56,128]{1,0:T(8,128)S(1)} %collective-permute-done.15.refs_0_, f32[56,128]{1,0:T(8,128)S(1)} %collective-permute-done.16.refs_1_, f32[56,128]{1,0:T(8,128)S(1)} %collective-permute-done.17.refs_2_, f32[56,128]{1,0:T(8,128)S(1)} %collective-permute-done.18.refs_3_, ...), custom_call_target="tpu_custom_call" | custom-call | flops 1073741824 | bytes 2097152 | tf_op jit(solution)/shard_map/pallas_call | solution.py:525
  (18 shorter events, 0.0 us)
Async XLA Ops:
  2.1 9.6 %collective-permute-start = (f32[56,128]{1,0:T(8,128)S(1)}, f32[56,128]{1,0:T(8,128)S(1)}, u32[]{:S(2)}, u32[]{:S(2)}) collective-permute-start(f32[56,128]{1,0:T(8,128)S(1)} %get-tuple-element.79), channel_id=1, source_target_pairs={{8,16},{16,8},{24,0},{0,24},{9,17},{17,9},{25,1},{1,25},{10,18},{1... | collective-permute-start | bytes 86024 | tf_op jit(solution)/shard_map/ppermute | solution.py:569
  6.3 5.4 %collective-permute-start.1 = (f32[56,128]{1,0:T(8,128)S(1)}, f32[56,128]{1,0:T(8,128)S(1)}, u32[]{:S(2)}, u32[]{:S(2)}) collective-permute-start(f32[56,128]{1,0:T(8,128)S(1)} %get-tuple-element.80), channel_id=1, source_target_pairs={{0,8},{8,0},{16,24},{24,16},{1,9},{9,1},{17,25},{25,17},{2,10},{10... | collective-permute-start | bytes 86024 | tf_op jit(solution)/shard_map/ppermute | solution.py:569
  6.3 5.4 %collective-permute-start.2 = (f32[56,128]{1,0:T(8,128)S(1)}, f32[56,128]{1,0:T(8,128)S(1)}, u32[]{:S(2)}, u32[]{:S(2)}) collective-permute-start(f32[56,128]{1,0:T(8,128)S(1)} %get-tuple-element.81), channel_id=1, source_target_pairs={{1,2},{2,1},{3,0},{0,3},{5,6},{6,5},{7,4},{4,7},{9,10},{10,9},{11,... | collective-permute-start | bytes 86024 | tf_op jit(solution)/shard_map/ppermute | solution.py:569
  8.3 3.3 %collective-permute-start.3 = (f32[56,128]{1,0:T(8,128)S(1)}, f32[56,128]{1,0:T(8,128)S(1)}, u32[]{:S(2)}, u32[]{:S(2)}) collective-permute-start(f32[56,128]{1,0:T(8,128)S(1)} %get-tuple-element.82), channel_id=1, source_target_pairs={{0,4},{4,0},{1,5},{5,1},{2,6},{6,2},{3,7},{7,3},{8,12},{12,8},{9,1... | collective-permute-start | bytes 86024 | tf_op jit(solution)/shard_map/ppermute | solution.py:569
  9.6 2.1 %collective-permute-start.4 = (f32[56,128]{1,0:T(8,128)S(1)}, f32[56,128]{1,0:T(8,128)S(1)}, u32[]{:S(2)}, u32[]{:S(2)}) collective-permute-start(f32[56,128]{1,0:T(8,128)S(1)} %get-tuple-element.83), channel_id=1, source_target_pairs={{0,1},{1,0},{2,3},{3,2},{4,5},{5,4},{6,7},{7,6},{8,9},{9,8},{10,11... | collective-permute-start | bytes 86024 | tf_op jit(solution)/shard_map/ppermute | solution.py:569
  15.4 5.3 %collective-permute-start.5 = (f32[56,128]{1,0:T(8,128)S(1)}, f32[56,128]{1,0:T(8,128)S(1)}, u32[]{:S(2)}, u32[]{:S(2)}) collective-permute-start(f32[56,128]{1,0:T(8,128)S(1)} %get-tuple-element.104), channel_id=1, source_target_pairs={{8,16},{16,8},{24,0},{0,24},{9,17},{17,9},{25,1},{1,25},{10,18},{1... | collective-permute-start | bytes 86024 | tf_op jit(solution)/shard_map/ppermute | solution.py:569
  16.1 4.6 %collective-permute-start.6 = (f32[56,128]{1,0:T(8,128)S(1)}, f32[56,128]{1,0:T(8,128)S(1)}, u32[]{:S(2)}, u32[]{:S(2)}) collective-permute-start(f32[56,128]{1,0:T(8,128)S(1)} %get-tuple-element.105), channel_id=1, source_target_pairs={{0,8},{8,0},{16,24},{24,16},{1,9},{9,1},{17,25},{25,17},{2,10},{10... | collective-permute-start | bytes 86024 | tf_op jit(solution)/shard_map/ppermute | solution.py:569
  17.3 3.8 %collective-permute-start.7 = (f32[56,128]{1,0:T(8,128)S(1)}, f32[56,128]{1,0:T(8,128)S(1)}, u32[]{:S(2)}, u32[]{:S(2)}) collective-permute-start(f32[56,128]{1,0:T(8,128)S(1)} %get-tuple-element.106), channel_id=1, source_target_pairs={{1,2},{2,1},{3,0},{0,3},{5,6},{6,5},{7,4},{4,7},{9,10},{10,9},{11,... | collective-permute-start | bytes 86024 | tf_op jit(solution)/shard_map/ppermute | solution.py:569
  18.2 3.0 %collective-permute-start.8 = (f32[56,128]{1,0:T(8,128)S(1)}, f32[56,128]{1,0:T(8,128)S(1)}, u32[]{:S(2)}, u32[]{:S(2)}) collective-permute-start(f32[56,128]{1,0:T(8,128)S(1)} %get-tuple-element.107), channel_id=1, source_target_pairs={{0,4},{4,0},{1,5},{5,1},{2,6},{6,2},{3,7},{7,3},{8,12},{12,8},{9,1... | collective-permute-start | bytes 86024 | tf_op jit(solution)/shard_map/ppermute | solution.py:569
  19.3 1.9 %collective-permute-start.9 = (f32[56,128]{1,0:T(8,128)S(1)}, f32[56,128]{1,0:T(8,128)S(1)}, u32[]{:S(2)}, u32[]{:S(2)}) collective-permute-start(f32[56,128]{1,0:T(8,128)S(1)} %get-tuple-element.108), channel_id=1, source_target_pairs={{0,1},{1,0},{2,3},{3,2},{4,5},{5,4},{6,7},{7,6},{8,9},{9,8},{10,11... | collective-permute-start | bytes 86024 | tf_op jit(solution)/shard_map/ppermute | solution.py:569
  24.9 7.4 %collective-permute-start.10 = (f32[56,128]{1,0:T(8,128)S(1)}, f32[56,128]{1,0:T(8,128)S(1)}, u32[]{:S(2)}, u32[]{:S(2)}) collective-permute-start(f32[56,128]{1,0:T(8,128)S(1)} %get-tuple-element.122), channel_id=1, source_target_pairs={{8,16},{16,8},{24,0},{0,24},{9,17},{17,9},{25,1},{1,25},{10,18},{1... | collective-permute-start | bytes 86024 | tf_op jit(solution)/shard_map/ppermute | solution.py:569
  27.3 5.0 %collective-permute-start.11 = (f32[56,128]{1,0:T(8,128)S(1)}, f32[56,128]{1,0:T(8,128)S(1)}, u32[]{:S(2)}, u32[]{:S(2)}) collective-permute-start(f32[56,128]{1,0:T(8,128)S(1)} %get-tuple-element.123), channel_id=1, source_target_pairs={{0,8},{8,0},{16,24},{24,16},{1,9},{9,1},{17,25},{25,17},{2,10},{10... | collective-permute-start | bytes 86024 | tf_op jit(solution)/shard_map/ppermute | solution.py:569
  27.3 5.0 %collective-permute-start.12 = (f32[56,128]{1,0:T(8,128)S(1)}, f32[56,128]{1,0:T(8,128)S(1)}, u32[]{:S(2)}, u32[]{:S(2)}) collective-permute-start(f32[56,128]{1,0:T(8,128)S(1)} %get-tuple-element.124), channel_id=1, source_target_pairs={{1,2},{2,1},{3,0},{0,3},{5,6},{6,5},{7,4},{4,7},{9,10},{10,9},{11,... | collective-permute-start | bytes 86024 | tf_op jit(solution)/shard_map/ppermute | solution.py:569
  29.4 3.0 %collective-permute-start.13 = (f32[56,128]{1,0:T(8,128)S(1)}, f32[56,128]{1,0:T(8,128)S(1)}, u32[]{:S(2)}, u32[]{:S(2)}) collective-permute-start(f32[56,128]{1,0:T(8,128)S(1)} %get-tuple-element.125), channel_id=1, source_target_pairs={{0,4},{4,0},{1,5},{5,1},{2,6},{6,2},{3,7},{7,3},{8,12},{12,8},{9,1... | collective-permute-start | bytes 86024 | tf_op jit(solution)/shard_map/ppermute | solution.py:569
  30.7 1.8 %collective-permute-start.14 = (f32[56,128]{1,0:T(8,128)S(1)}, f32[56,128]{1,0:T(8,128)S(1)}, u32[]{:S(2)}, u32[]{:S(2)}) collective-permute-start(f32[56,128]{1,0:T(8,128)S(1)} %get-tuple-element.126), channel_id=1, source_target_pairs={{0,1},{1,0},{2,3},{3,2},{4,5},{5,4},{6,7},{7,6},{8,9},{9,8},{10,11... | collective-permute-start | bytes 86024 | tf_op jit(solution)/shard_map/ppermute | solution.py:569
  36.2 6.2 %collective-permute-start.15 = (f32[56,128]{1,0:T(8,128)S(1)}, f32[56,128]{1,0:T(8,128)S(1)}, u32[]{:S(2)}, u32[]{:S(2)}) collective-permute-start(f32[56,128]{1,0:T(8,128)S(1)} %get-tuple-element.135), channel_id=1, source_target_pairs={{8,16},{16,8},{24,0},{0,24},{9,17},{17,9},{25,1},{1,25},{10,18},{1... | collective-permute-start | bytes 86024 | tf_op jit(solution)/shard_map/ppermute | solution.py:569
  37.3 5.1 %collective-permute-start.16 = (f32[56,128]{1,0:T(8,128)S(1)}, f32[56,128]{1,0:T(8,128)S(1)}, u32[]{:S(2)}, u32[]{:S(2)}) collective-permute-start(f32[56,128]{1,0:T(8,128)S(1)} %get-tuple-element.136), channel_id=1, source_target_pairs={{0,8},{8,0},{16,24},{24,16},{1,9},{9,1},{17,25},{25,17},{2,10},{10... | collective-permute-start | bytes 86024 | tf_op jit(solution)/shard_map/ppermute | solution.py:569
  38.3 4.1 %collective-permute-start.17 = (f32[56,128]{1,0:T(8,128)S(1)}, f32[56,128]{1,0:T(8,128)S(1)}, u32[]{:S(2)}, u32[]{:S(2)}) collective-permute-start(f32[56,128]{1,0:T(8,128)S(1)} %get-tuple-element.137), channel_id=1, source_target_pairs={{1,2},{2,1},{3,0},{0,3},{5,6},{6,5},{7,4},{4,7},{9,10},{10,9},{11,... | collective-permute-start | bytes 86024 | tf_op jit(solution)/shard_map/ppermute | solution.py:569
  39.4 3.2 %collective-permute-start.18 = (f32[56,128]{1,0:T(8,128)S(1)}, f32[56,128]{1,0:T(8,128)S(1)}, u32[]{:S(2)}, u32[]{:S(2)}) collective-permute-start(f32[56,128]{1,0:T(8,128)S(1)} %get-tuple-element.138), channel_id=1, source_target_pairs={{0,4},{4,0},{1,5},{5,1},{2,6},{6,2},{3,7},{7,3},{8,12},{12,8},{9,1... | collective-permute-start | bytes 86024 | tf_op jit(solution)/shard_map/ppermute | solution.py:569
  40.1 2.4 %collective-permute-start.19 = (f32[56,128]{1,0:T(8,128)S(1)}, f32[56,128]{1,0:T(8,128)S(1)}, u32[]{:S(2)}, u32[]{:S(2)}) collective-permute-start(f32[56,128]{1,0:T(8,128)S(1)} %get-tuple-element.139), channel_id=1, source_target_pairs={{0,1},{1,0},{2,3},{3,2},{4,5},{5,4},{6,7},{7,6},{8,9},{9,8},{10,11... | collective-permute-start | bytes 86024 | tf_op jit(solution)/shard_map/ppermute | solution.py:569

commit v3 on v2

--- a/solution.py
+++ b/solution.py
@@ -19,7 +19,7 @@
 
 
 AXES = ("gx", "gy", "gz")
-ORDER = (("gx", 1), ("gx", 0), ("gz", 1), ("gy", 1), ("gy", 0), ("gz", 0))
+ORDER = (("gx", 1), ("gz", 1), ("gx", 0), ("gy", 1), ("gy", 0), ("gz", 0))
 
 
 def matchings():
@@ -239,24 +239,24 @@
     square[...] = jnp.zeros_like(square)
     wide[...] = jnp.zeros_like(wide)
     picks[...] = jnp.full_like(picks, -1)
+    copies[1].wait()
+    for c in range(z.C):
+        for b in range(z.B):
+            square[c * z.BQ + b:c * z.BQ + b + 1, 0:z.M] = projection[b, c:c + 1, :]
+    for c in range(z.C):
+        rows = slice(c * z.BP, (c + 1) * z.BP)
+        triple(rows, z.MP, p3, wide, square[c * z.BQ:c * z.BQ + z.BP, 0:z.MP])
+    copies[0].wait()
+    for f in range(z.F):
+        put_field(z, y3, f, y[f * z.M:(f + 1) * z.M, :])
+    copies[3].wait()
     upward, _ = bearings(plan)
     copies[2].wait()
     for m, (a, rises) in enumerate(upward):
         picks[0:1, m * z.W:(m + 1) * z.W] = jnp.where(rises, slots[2 * a + 1:2 * a + 2, :], slots[2 * a:2 * a + 1, :])
     ids = lax.broadcasted_iota(jnp.int32, (z.S, z.KW), 0)
     ohs[...] = jnp.where(ids == picks[0:1, :], 1.0, 0.0).astype(BF)
-    copies[1].wait()
-    for c in range(z.C):
-        for b in range(z.B):
-            square[c * z.BQ + b:c * z.BQ + b + 1, 0:z.M] = projection[b, c:c + 1, :]
-    for c in range(z.C):
-        rows = slice(c * z.BP, (c + 1) * z.BP)
-        triple(rows, z.MP, p3, wide, square[c * z.BQ:c * z.BQ + z.BP, 0:z.MP])
-    copies[0].wait()
-    for f in range(z.F):
-        put_field(z, y3, f, y[f * z.M:(f + 1) * z.M, :])
     traces[...] = dot(p3[...], y3[...])
-    copies[3].wait()
     for c in range(z.C):
         t = face_rows(z, traces, c, z.F)
         for g in range(z.F):

time: 48.2 us -> 48 us (level)
  no operation moved by 1% of the time
where the time goes in v3:
time: 48 us; the launch traced here: 47.4 us
  Pallas kernels  25.4 us (53%)
  starting transfers between devices  20.8 us (43%)
  waiting for transfers between devices  1.1 us (2%)
    pallas_call x9, Pallas kernels, call(): pl.pallas_call(kernel, out_shape=[jax.ShapeDtypeStruct(*o) for o in outs]...  25.4 us
    ppermute x20, starting transfers between devices, trade(): lax.ppermute(m, axis, links)  20.8 us
    ppermute x20, waiting for transfers between devices, trade(): lax.ppermute(m, axis, links)  1.1 us
  transfers between devices with their start and end apart: 20, of which 4 were waited for; matrix products, arithmetic and copies ran while one was open for 0% of the time, Pallas kernels for 15%

profile of v3, /device:TPU:1, one launch (start us, length us, event | category | flops | bytes accessed | tf_op | source)
XLA Modules:
  0.0 47.4 jit_solution(3309781618085541948)
XLA Ops:
  0.0 2.0 %shard_map.100 = (f32[504,128]{1,0:T(8,128)S(1)}, f32[9,9,3,128]{3,2,1,0:T(4,128)S(1)}, f32[9,9,4,128]{3,2,1,0:T(4,128)S(1)}, f32[9,9,4,128]{3,2,1,0:T(4,128)S(1...) custom-call(f32[504,128]{1,0:T(8,128)} %bitcast.7, ...), custom_call_target="tpu_custom_call" | custom-call | flops 1073741824 | bytes 2097152 | tf_op jit(solution)/shard_map/pallas_call | solution.py:525
  2.1 4.2 %collective-permute-start = (f32[56,128]{1,0:T(8,128)S(1)}, f32[56,128]{1,0:T(8,128)S(1)}, u32[]{:S(2)}, u32[]{:S(2)}) collective-permute-start(f32[56,128]{1,0:T(8,128)S(1)} %get-tuple-element.79), channel_id=1, source_target_pairs={{8,16},{16,8},{24,0},{0,24},{9,17},{17,9},{25,1},{1,25},{10,18},{1... | collective-permute-start | bytes 86024 | tf_op jit(solution)/shard_map/ppermute | solution.py:569
  6.3 2.1 %collective-permute-start.1 = (f32[56,128]{1,0:T(8,128)S(1)}, f32[56,128]{1,0:T(8,128)S(1)}, u32[]{:S(2)}, u32[]{:S(2)}) collective-permute-start(f32[56,128]{1,0:T(8,128)S(1)} %get-tuple-element.80), channel_id=1, source_target_pairs={{1,2},{2,1},{3,0},{0,3},{5,6},{6,5},{7,4},{4,7},{9,10},{10,9},{11,... | collective-permute-start | bytes 86024 | tf_op jit(solution)/shard_map/ppermute | solution.py:569
  8.3 1.2 %collective-permute-start.3 = (f32[56,128]{1,0:T(8,128)S(1)}, f32[56,128]{1,0:T(8,128)S(1)}, u32[]{:S(2)}, u32[]{:S(2)}) collective-permute-start(f32[56,128]{1,0:T(8,128)S(1)} %get-tuple-element.82), channel_id=1, source_target_pairs={{0,4},{4,0},{1,5},{5,1},{2,6},{6,2},{3,7},{7,3},{8,12},{12,8},{9,1... | collective-permute-start | bytes 86024 | tf_op jit(solution)/shard_map/ppermute | solution.py:569
  9.6 0.0 collective-permute-start.4
  9.6 2.1 %shard_map.101 = (bf16[168,192]{1,0:T(8,128)(2,1)S(1)}, bf16[168,192]{1,0:T(8,128)(2,1)S(1)}, bf16[56,384]{1,0:T(8,128)(2,1)S(1)}, bf16[256,512]{1,0:T(8,128)(2,...) custom-call(f32[3,56,56]{2,1,0:T(8,128)S(1)} %get-tuple-element.84.r, ...), custom_call_target="tpu_custom_call" | custom-call | flops 1073741824 | bytes 2097152 | tf_op jit(solution)/shard_map/pallas_call | solution.py:525
  11.6 0.0 collective-permute-done.1.refs_1_
  11.7 0.0 collective-permute-done.4.refs_4_
  11.7 3.7 %shard_map.102 = (f32[280,128]{1,0:T(8,128)S(1)}, f32[280,128]{1,0:T(8,128)S(1)}, bf16[192,640]{1,0:T(8,128)(2,1)S(1)}, f32[96,640]{1,0:T(8,128)S(1)}, bf16[448,...) custom-call(f32[56,128]{1,0:T(8,128)S(1)} %collective-permute-done.r, ...), custom_call_target="tpu_custom_call" | custom-call | flops 1073741824 | bytes 2097152 | tf_op jit(solution)/shard_map/pallas_call | solution.py:525
  15.4 0.5 %collective-permute-start.5 = (f32[56,128]{1,0:T(8,128)S(1)}, f32[56,128]{1,0:T(8,128)S(1)}, u32[]{:S(2)}, u32[]{:S(2)}) collective-permute-start(f32[56,128]{1,0:T(8,128)S(1)} %get-tuple-element.104), channel_id=1, source_target_pairs={{8,16},{16,8},{24,0},{0,24},{9,17},{17,9},{25,1},{1,25},{10,18},{1... | collective-permute-start | bytes 86024 | tf_op jit(solution)/shard_map/ppermute | solution.py:569
  15.9 2.1 %collective-permute-start.6 = (f32[56,128]{1,0:T(8,128)S(1)}, f32[56,128]{1,0:T(8,128)S(1)}, u32[]{:S(2)}, u32[]{:S(2)}) collective-permute-start(f32[56,128]{1,0:T(8,128)S(1)} %get-tuple-element.105), channel_id=1, source_target_pairs={{1,2},{2,1},{3,0},{0,3},{5,6},{6,5},{7,4},{4,7},{9,10},{10,9},{11,... | collective-permute-start | bytes 86024 | tf_op jit(solution)/shard_map/ppermute | solution.py:569
  18.0 0.0 collective-permute-start.7
  18.0 1.2 %collective-permute-start.8 = (f32[56,128]{1,0:T(8,128)S(1)}, f32[56,128]{1,0:T(8,128)S(1)}, u32[]{:S(2)}, u32[]{:S(2)}) collective-permute-start(f32[56,128]{1,0:T(8,128)S(1)} %get-tuple-element.107), channel_id=1, source_target_pairs={{0,4},{4,0},{1,5},{5,1},{2,6},{6,2},{3,7},{7,3},{8,12},{12,8},{9,1... | collective-permute-start | bytes 86024 | tf_op jit(solution)/shard_map/ppermute | solution.py:569
  19.3 1.4 %shard_map.103 = (f32[504,128]{1,0:T(8,128)S(1)}, f32[504,128]{1,0:T(8,128)S(1)}, f32[280,128]{1,0:T(8,128)S(1)}) custom-call(bf16[192,640]{1,0:T(8,128)(2,1)S(1)} %get-tuple-element.109.refs_0_, f32[96,640]{1,0:T(8,128)S(1)} %get-tuple-element.110.refs_1_, bf16[448,256]{1,0:T(8,128)(2,1)S(1)} %get-tuple-element.111.refs_2_, ...), custom_call_target="tpu_custom_call" | custom-call | flops 1073741824 | bytes 2097152 | tf_op jit(solution)/shard_map/pallas_call | solution.py:525
  20.7 0.0 collective-permute-done.5.refs_0_
  20.7 0.6 %collective-permute-done.7.refs_2_ = f32[56,128]{1,0:T(8,128)S(1)} collective-permute-done((f32[56,128]{1,0:T(8,128)S(1)}, f32[56,128]{1,0:T(8,128)S(1)}, u32[]{:S(2)}, u32[]{:S(2)}) %collective-permute-start.7) | collective-permute-done | bytes 28704 | tf_op jit(solution)/shard_map/ppermute | solution.py:569
  21.2 3.7 %shard_map.104 = (f32[280,128]{1,0:T(8,128)S(1)}, f32[280,128]{1,0:T(8,128)S(1)}, bf16[192,640]{1,0:T(8,128)(2,1)S(1)}, f32[96,640]{1,0:T(8,128)S(1)}, bf16[448,...) custom-call(f32[56,128]{1,0:T(8,128)S(1)} %collective-permute-done.5, ...), custom_call_target="tpu_custom_call" | custom-call | flops 1073741824 | bytes 2097152 | tf_op jit(solution)/shard_map/pallas_call | solution.py:525
  24.9 2.0 %collective-permute-start.10 = (f32[56,128]{1,0:T(8,128)S(1)}, f32[56,128]{1,0:T(8,128)S(1)}, u32[]{:S(2)}, u32[]{:S(2)}) collective-permute-start(f32[56,128]{1,0:T(8,128)S(1)} %get-tuple-element.122), channel_id=1, source_target_pairs={{8,16},{16,8},{24,0},{0,24},{9,17},{17,9},{25,1},{1,25},{10,18},{1... | collective-permute-start | bytes 86024 | tf_op jit(solution)/shard_map/ppermute | solution.py:569
  26.9 2.4 %collective-permute-start.11 = (f32[56,128]{1,0:T(8,128)S(1)}, f32[56,128]{1,0:T(8,128)S(1)}, u32[]{:S(2)}, u32[]{:S(2)}) collective-permute-start(f32[56,128]{1,0:T(8,128)S(1)} %get-tuple-element.123), channel_id=1, source_target_pairs={{1,2},{2,1},{3,0},{0,3},{5,6},{6,5},{7,4},{4,7},{9,10},{10,9},{11,... | collective-permute-start | bytes 86024 | tf_op jit(solution)/shard_map/ppermute | solution.py:569
  29.3 1.1 %collective-permute-start.13 = (f32[56,128]{1,0:T(8,128)S(1)}, f32[56,128]{1,0:T(8,128)S(1)}, u32[]{:S(2)}, u32[]{:S(2)}) collective-permute-start(f32[56,128]{1,0:T(8,128)S(1)} %get-tuple-element.125), channel_id=1, source_target_pairs={{0,4},{4,0},{1,5},{5,1},{2,6},{6,2},{3,7},{7,3},{8,12},{12,8},{9,1... | collective-permute-start | bytes 86024 | tf_op jit(solution)/shard_map/ppermute | solution.py:569
  30.4 0.0 collective-permute-start.14
  30.4 1.6 %shard_map.105 = (f32[504,128]{1,0:T(8,128)S(1)}, f32[504,128]{1,0:T(8,128)S(1)}, f32[280,128]{1,0:T(8,128)S(1)}) custom-call(bf16[192,640]{1,0:T(8,128)(2,1)S(1)} %get-tuple-element.127.refs_0_, f32[96,640]{1,0:T(8,128)S(1)} %get-tuple-element.128.refs_1_, bf16[448,256]{1,0:T(8,128)(2,1)S(1)} %get-tuple-element.129.refs_2_, ...), custom_call_target="tpu_custom_call" | custom-call | flops 1073741824 | bytes 2097152 | tf_op jit(solution)/shard_map/pallas_call | solution.py:525
  32.0 0.3 collective-permute-done.12.refs_2_
  32.3 0.1 collective-permute-done.13.refs_3_
  32.5 3.7 %shard_map.106 = (f32[280,128]{1,0:T(8,128)S(1)}, f32[280,128]{1,0:T(8,128)S(1)}, bf16[192,640]{1,0:T(8,128)(2,1)S(1)}, f32[96,640]{1,0:T(8,128)S(1)}, bf16[448,...) custom-call(f32[56,128]{1,0:T(8,128)S(1)} %collective-permute-done.1, ...), custom_call_target="tpu_custom_call" | custom-call | flops 1073741824 | bytes 2097152 | tf_op jit(solution)/shard_map/pallas_call | solution.py:525
  36.1 1.1 %collective-permute-start.15 = (f32[56,128]{1,0:T(8,128)S(1)}, f32[56,128]{1,0:T(8,128)S(1)}, u32[]{:S(2)}, u32[]{:S(2)}) collective-permute-start(f32[56,128]{1,0:T(8,128)S(1)} %get-tuple-element.135), channel_id=1, source_target_pairs={{8,16},{16,8},{24,0},{0,24},{9,17},{17,9},{25,1},{1,25},{10,18},{1... | collective-permute-start | bytes 86024 | tf_op jit(solution)/shard_map/ppermute | solution.py:569
  37.3 1.6 %collective-permute-start.16 = (f32[56,128]{1,0:T(8,128)S(1)}, f32[56,128]{1,0:T(8,128)S(1)}, u32[]{:S(2)}, u32[]{:S(2)}) collective-permute-start(f32[56,128]{1,0:T(8,128)S(1)} %get-tuple-element.136), channel_id=1, source_target_pairs={{1,2},{2,1},{3,0},{0,3},{5,6},{6,5},{7,4},{4,7},{9,10},{10,9},{11,... | collective-permute-start | bytes 86024 | tf_op jit(solution)/shard_map/ppermute | solution.py:569
  38.8 0.2 collective-permute-start.17
  39.1 1.0 %collective-permute-start.18 = (f32[56,128]{1,0:T(8,128)S(1)}, f32[56,128]{1,0:T(8,128)S(1)}, u32[]{:S(2)}, u32[]{:S(2)}) collective-permute-start(f32[56,128]{1,0:T(8,128)S(1)} %get-tuple-element.138), channel_id=1, source_target_pairs={{0,4},{4,0},{1,5},{5,1},{2,6},{6,2},{3,7},{7,3},{8,12},{12,8},{9,1... | collective-permute-start | bytes 86024 | tf_op jit(solution)/shard_map/ppermute | solution.py:569
  40.1 2.2 %shard_map.107 = (f32[504,128]{1,0:T(8,128)S(1)}, f32[6,504,128]{2,1,0:T(8,128)S(1)}, f32[504,128]{1,0:T(8,128)S(1)}, f32[280,128]{1,0:T(8,128)}) custom-call(bf16[192,640]{1,0:T(8,128)(2,1)S(1)} %get-tuple-element.140.refs_0_, f32[96,640]{1,0:T(8,128)S(1)} %get-tuple-element.141.refs_1_, bf16[448,256]{1,0:T(8,128)(2,1)S(1)} %get-tuple-element.142.refs_2_, ...), custom_call_target="tpu_custom_call" | custom-call | flops 1073741824 | bytes 2097152 | tf_op jit(solution)/shard_map/pallas_call | solution.py:525
  42.3 0.1 collective-permute-done.17.refs_2_
  42.4 5.0 %shard_map.108 = f32[504,128]{1,0:T(8,128)} custom-call(f32[56,128]{1,0:T(8,128)S(1)} %collective-permute-done.15.refs_0_, f32[56,128]{1,0:T(8,128)S(1)} %collective-permute-done.16.refs_1_, f32[56,128]{1,0:T(8,128)S(1)} %collective-permute-done.17.refs_2_, f32[56,128]{1,0:T(8,128)S(1)} %collective-permute-done.18.refs_3_, ...), custom_call_target="tpu_custom_call" | custom-call | flops 1073741824 | bytes 2097152 | tf_op jit(solution)/shard_map/pallas_call | solution.py:525
  (18 shorter events, 0.0 us)
Async XLA Ops:
  2.1 9.6 %collective-permute-start = (f32[56,128]{1,0:T(8,128)S(1)}, f32[56,128]{1,0:T(8,128)S(1)}, u32[]{:S(2)}, u32[]{:S(2)}) collective-permute-start(f32[56,128]{1,0:T(8,128)S(1)} %get-tuple-element.79), channel_id=1, source_target_pairs={{8,16},{16,8},{24,0},{0,24},{9,17},{17,9},{25,1},{1,25},{10,18},{1... | collective-permute-start | bytes 86024 | tf_op jit(solution)/shard_map/ppermute | solution.py:569
  6.3 5.4 %collective-permute-start.1 = (f32[56,128]{1,0:T(8,128)S(1)}, f32[56,128]{1,0:T(8,128)S(1)}, u32[]{:S(2)}, u32[]{:S(2)}) collective-permute-start(f32[56,128]{1,0:T(8,128)S(1)} %get-tuple-element.80), channel_id=1, source_target_pairs={{1,2},{2,1},{3,0},{0,3},{5,6},{6,5},{7,4},{4,7},{9,10},{10,9},{11,... | collective-permute-start | bytes 86024 | tf_op jit(solution)/shard_map/ppermute | solution.py:569
  8.3 3.3 %collective-permute-start.2 = (f32[56,128]{1,0:T(8,128)S(1)}, f32[56,128]{1,0:T(8,128)S(1)}, u32[]{:S(2)}, u32[]{:S(2)}) collective-permute-start(f32[56,128]{1,0:T(8,128)S(1)} %get-tuple-element.81), channel_id=1, source_target_pairs={{0,8},{8,0},{16,24},{24,16},{1,9},{9,1},{17,25},{25,17},{2,10},{10... | collective-permute-start | bytes 86024 | tf_op jit(solution)/shard_map/ppermute | solution.py:569
  8.3 3.3 %collective-permute-start.3 = (f32[56,128]{1,0:T(8,128)S(1)}, f32[56,128]{1,0:T(8,128)S(1)}, u32[]{:S(2)}, u32[]{:S(2)}) collective-permute-start(f32[56,128]{1,0:T(8,128)S(1)} %get-tuple-element.82), channel_id=1, source_target_pairs={{0,4},{4,0},{1,5},{5,1},{2,6},{6,2},{3,7},{7,3},{8,12},{12,8},{9,1... | collective-permute-start | bytes 86024 | tf_op jit(solution)/shard_map/ppermute | solution.py:569
  9.6 2.1 %collective-permute-start.4 = (f32[56,128]{1,0:T(8,128)S(1)}, f32[56,128]{1,0:T(8,128)S(1)}, u32[]{:S(2)}, u32[]{:S(2)}) collective-permute-start(f32[56,128]{1,0:T(8,128)S(1)} %get-tuple-element.83), channel_id=1, source_target_pairs={{0,1},{1,0},{2,3},{3,2},{4,5},{5,4},{6,7},{7,6},{8,9},{9,8},{10,11... | collective-permute-start | bytes 86024 | tf_op jit(solution)/shard_map/ppermute | solution.py:569
  15.4 5.3 %collective-permute-start.5 = (f32[56,128]{1,0:T(8,128)S(1)}, f32[56,128]{1,0:T(8,128)S(1)}, u32[]{:S(2)}, u32[]{:S(2)}) collective-permute-start(f32[56,128]{1,0:T(8,128)S(1)} %get-tuple-element.104), channel_id=1, source_target_pairs={{8,16},{16,8},{24,0},{0,24},{9,17},{17,9},{25,1},{1,25},{10,18},{1... | collective-permute-start | bytes 86024 | tf_op jit(solution)/shard_map/ppermute | solution.py:569
  15.9 4.8 %collective-permute-start.6 = (f32[56,128]{1,0:T(8,128)S(1)}, f32[56,128]{1,0:T(8,128)S(1)}, u32[]{:S(2)}, u32[]{:S(2)}) collective-permute-start(f32[56,128]{1,0:T(8,128)S(1)} %get-tuple-element.105), channel_id=1, source_target_pairs={{1,2},{2,1},{3,0},{0,3},{5,6},{6,5},{7,4},{4,7},{9,10},{10,9},{11,... | collective-permute-start | bytes 86024 | tf_op jit(solution)/shard_map/ppermute | solution.py:569
  18.0 3.2 %collective-permute-start.7 = (f32[56,128]{1,0:T(8,128)S(1)}, f32[56,128]{1,0:T(8,128)S(1)}, u32[]{:S(2)}, u32[]{:S(2)}) collective-permute-start(f32[56,128]{1,0:T(8,128)S(1)} %get-tuple-element.106), channel_id=1, source_target_pairs={{0,8},{8,0},{16,24},{24,16},{1,9},{9,1},{17,25},{25,17},{2,10},{10... | collective-permute-start | bytes 86024 | tf_op jit(solution)/shard_map/ppermute | solution.py:569
  18.0 3.2 %collective-permute-start.8 = (f32[56,128]{1,0:T(8,128)S(1)}, f32[56,128]{1,0:T(8,128)S(1)}, u32[]{:S(2)}, u32[]{:S(2)}) collective-permute-start(f32[56,128]{1,0:T(8,128)S(1)} %get-tuple-element.107), channel_id=1, source_target_pairs={{0,4},{4,0},{1,5},{5,1},{2,6},{6,2},{3,7},{7,3},{8,12},{12,8},{9,1... | collective-permute-start | bytes 86024 | tf_op jit(solution)/shard_map/ppermute | solution.py:569
  19.3 2.0 %collective-permute-start.9 = (f32[56,128]{1,0:T(8,128)S(1)}, f32[56,128]{1,0:T(8,128)S(1)}, u32[]{:S(2)}, u32[]{:S(2)}) collective-permute-start(f32[56,128]{1,0:T(8,128)S(1)} %get-tuple-element.108), channel_id=1, source_target_pairs={{0,1},{1,0},{2,3},{3,2},{4,5},{5,4},{6,7},{7,6},{8,9},{9,8},{10,11... | collective-permute-start | bytes 86024 | tf_op jit(solution)/shard_map/ppermute | solution.py:569
  24.9 7.1 %collective-permute-start.10 = (f32[56,128]{1,0:T(8,128)S(1)}, f32[56,128]{1,0:T(8,128)S(1)}, u32[]{:S(2)}, u32[]{:S(2)}) collective-permute-start(f32[56,128]{1,0:T(8,128)S(1)} %get-tuple-element.122), channel_id=1, source_target_pairs={{8,16},{16,8},{24,0},{0,24},{9,17},{17,9},{25,1},{1,25},{10,18},{1... | collective-permute-start | bytes 86024 | tf_op jit(solution)/shard_map/ppermute | solution.py:569
  26.9 5.1 %collective-permute-start.11 = (f32[56,128]{1,0:T(8,128)S(1)}, f32[56,128]{1,0:T(8,128)S(1)}, u32[]{:S(2)}, u32[]{:S(2)}) collective-permute-start(f32[56,128]{1,0:T(8,128)S(1)} %get-tuple-element.123), channel_id=1, source_target_pairs={{1,2},{2,1},{3,0},{0,3},{5,6},{6,5},{7,4},{4,7},{9,10},{10,9},{11,... | collective-permute-start | bytes 86024 | tf_op jit(solution)/shard_map/ppermute | solution.py:569
  29.3 3.0 %collective-permute-start.12 = (f32[56,128]{1,0:T(8,128)S(1)}, f32[56,128]{1,0:T(8,128)S(1)}, u32[]{:S(2)}, u32[]{:S(2)}) collective-permute-start(f32[56,128]{1,0:T(8,128)S(1)} %get-tuple-element.124), channel_id=1, source_target_pairs={{0,8},{8,0},{16,24},{24,16},{1,9},{9,1},{17,25},{25,17},{2,10},{10... | collective-permute-start | bytes 86024 | tf_op jit(solution)/shard_map/ppermute | solution.py:569
  29.3 3.1 %collective-permute-start.13 = (f32[56,128]{1,0:T(8,128)S(1)}, f32[56,128]{1,0:T(8,128)S(1)}, u32[]{:S(2)}, u32[]{:S(2)}) collective-permute-start(f32[56,128]{1,0:T(8,128)S(1)} %get-tuple-element.125), channel_id=1, source_target_pairs={{0,4},{4,0},{1,5},{5,1},{2,6},{6,2},{3,7},{7,3},{8,12},{12,8},{9,1... | collective-permute-start | bytes 86024 | tf_op jit(solution)/shard_map/ppermute | solution.py:569
  30.4 2.1 %collective-permute-start.14 = (f32[56,128]{1,0:T(8,128)S(1)}, f32[56,128]{1,0:T(8,128)S(1)}, u32[]{:S(2)}, u32[]{:S(2)}) collective-permute-start(f32[56,128]{1,0:T(8,128)S(1)} %get-tuple-element.126), channel_id=1, source_target_pairs={{0,1},{1,0},{2,3},{3,2},{4,5},{5,4},{6,7},{7,6},{8,9},{9,8},{10,11... | collective-permute-start | bytes 86024 | tf_op jit(solution)/shard_map/ppermute | solution.py:569
  36.1 6.2 %collective-permute-start.15 = (f32[56,128]{1,0:T(8,128)S(1)}, f32[56,128]{1,0:T(8,128)S(1)}, u32[]{:S(2)}, u32[]{:S(2)}) collective-permute-start(f32[56,128]{1,0:T(8,128)S(1)} %get-tuple-element.135), channel_id=1, source_target_pairs={{8,16},{16,8},{24,0},{0,24},{9,17},{17,9},{25,1},{1,25},{10,18},{1... | collective-permute-start | bytes 86024 | tf_op jit(solution)/shard_map/ppermute | solution.py:569
  37.3 5.0 %collective-permute-start.16 = (f32[56,128]{1,0:T(8,128)S(1)}, f32[56,128]{1,0:T(8,128)S(1)}, u32[]{:S(2)}, u32[]{:S(2)}) collective-permute-start(f32[56,128]{1,0:T(8,128)S(1)} %get-tuple-element.136), channel_id=1, source_target_pairs={{1,2},{2,1},{3,0},{0,3},{5,6},{6,5},{7,4},{4,7},{9,10},{10,9},{11,... | collective-permute-start | bytes 86024 | tf_op jit(solution)/shard_map/ppermute | solution.py:569
  38.8 3.6 %collective-permute-start.17 = (f32[56,128]{1,0:T(8,128)S(1)}, f32[56,128]{1,0:T(8,128)S(1)}, u32[]{:S(2)}, u32[]{:S(2)}) collective-permute-start(f32[56,128]{1,0:T(8,128)S(1)} %get-tuple-element.137), channel_id=1, source_target_pairs={{0,8},{8,0},{16,24},{24,16},{1,9},{9,1},{17,25},{25,17},{2,10},{10... | collective-permute-start | bytes 86024 | tf_op jit(solution)/shard_map/ppermute | solution.py:569
  39.1 3.3 %collective-permute-start.18 = (f32[56,128]{1,0:T(8,128)S(1)}, f32[56,128]{1,0:T(8,128)S(1)}, u32[]{:S(2)}, u32[]{:S(2)}) collective-permute-start(f32[56,128]{1,0:T(8,128)S(1)} %get-tuple-element.138), channel_id=1, source_target_pairs={{0,4},{4,0},{1,5},{5,1},{2,6},{6,2},{3,7},{7,3},{8,12},{12,8},{9,1... | collective-permute-start | bytes 86024 | tf_op jit(solution)/shard_map/ppermute | solution.py:569
  40.1 2.3 %collective-permute-start.19 = (f32[56,128]{1,0:T(8,128)S(1)}, f32[56,128]{1,0:T(8,128)S(1)}, u32[]{:S(2)}, u32[]{:S(2)}) collective-permute-start(f32[56,128]{1,0:T(8,128)S(1)} %get-tuple-element.139), channel_id=1, source_target_pairs={{0,1},{1,0},{2,3},{3,2},{4,5},{5,4},{6,7},{7,6},{8,9},{9,8},{10,11... | collective-permute-start | bytes 86024 | tf_op jit(solution)/shard_map/ppermute | solution.py:569

commit v4 on v3

--- a/solution.py
+++ b/solution.py
@@ -363,14 +363,20 @@
     return lift(z, pt, u)
 
 
-def local_kernel(z, last, *refs):
+def local_kernel(z, step, *refs):
     y3, traces, sx, v3, pt, star, local, ohl, index, src_in, half_in, stacked, ohr = refs[:13]
     refs = refs[13:]
+    last = step == 1
     if last:
-        older, start, moved, refs = refs[0:2], refs[2], refs[3], refs[4:]
-        src_out, weights, base, half_out, refs = refs[0], refs[1], refs[2], refs[3], refs[4:]
+        partial, start, moved, src_out, weights, base, half_out = refs[:7]
+        refs = refs[7:]
+    elif step == 2:
+        older, partial, src_out, half_out = refs[:4]
+        refs = refs[4:]
     else:
-        src_full, src_out, half_out, refs = refs[0], refs[1], refs[2], refs[3:]
+        src_full, src_out, half_out = refs[:3]
+        refs = refs[3:]
+    shares = [coefficients(i / FINE_STEPS, (i + 1) / FINE_STEPS) for i in range(FINE_STEPS)]
     turned, u, gathered, u_half, lifted, u_far, gathered_far, landed = refs
     gathered_far[...] = dot(stacked[...], ohr[...])
     landed[...] = lift_gathered(z, gathered_far, u_far, pt)
@@ -400,14 +406,15 @@
             src_out[rows, :] = jnp.where(fast, expand(z, rank, pairs, g), value)
             pairs = lambda p: moved[p * z.M:(p + 1) * z.M, :]
             base[rows, :] = start[rows, :] + jnp.where(fast, expand(z, rank, pairs, g), 0.0)
-            sources = [x[rows, :] for x in older] + [whole]
-            sources = [jnp.where(fast, 0.0, x) for x in sources]
+            slow = jnp.where(fast, 0.0, whole)
             for k in range(TERMS):
-                total = None
-                for step, x in zip(range(FINE_STEPS - 1, 0, -1), sources):
-                    c = coefficients(step / FINE_STEPS, (step + 1) / FINE_STEPS)[k]
-                    total = c * x if total is None else total + c * x
-                weights[k, rows, :] = total
+                weights[k, rows, :] = partial[k, rows, :] + shares[1][k] * slow
+        elif step == 2:
+            src_out[rows, :] = value
+            before = jnp.where(fast, 0.0, older[rows, :])
+            slow = jnp.where(fast, 0.0, whole)
+            for k in range(TERMS):
+                partial[k, rows, :] = shares[3][k] * before + shares[2][k] * slow
         else:
             src_full[rows, :] = whole
             src_out[rows, :] = value
@@ -593,7 +600,6 @@
         deriv, volume, square, partner, cluster, ohs, star, across, local, y3v, tr, sxv,
     )
     moved = jnp.zeros((8, members), F32)
-    sources = []
     for step in range(FINE_STEPS - 1, 0, -1):
         half_src, moved, y3v, tr, sxv, stack, *messages = call(
             functools.partial(step_kernel, z, step == FINE_STEPS - 1),
@@ -607,12 +613,16 @@
         local_scratch = [turned_half, u, gathered, u_half, lifted, u, gathered, lifted]
         if last:
             src, weights, base, _ = call(
-                functools.partial(local_kernel, z, True), [full, ((TERMS,) + full[0], F32), full, half], local_scratch,
-                *local_args, *sources, start, moved,
+                functools.partial(local_kernel, z, step), [full, ((TERMS,) + full[0], F32), full, half], local_scratch,
+                *local_args, partial, start, moved,
+            )
+        elif step == 2:
+            partial, src, half_src = call(
+                functools.partial(local_kernel, z, step), [((TERMS,) + full[0], F32), full, half], local_scratch,
+                *local_args, whole,
             )
         else:
-            whole, src, half_src = call(functools.partial(local_kernel, z, False), [full, full, half], local_scratch, *local_args)
-            sources.append(whole)
+            whole, src, half_src = call(functools.partial(local_kernel, z, step), [full, full, half], local_scratch, *local_args)
     (out,) = call(
         functools.partial(last_kernel, z), [full],
         [landed, stacked, gathered, u, lifted, marked(turned), y3, full],

time: 48 us -> 47.9 us (level)
  no operation moved by 1% of the time
where the time goes in v4:
time: 47.9 us; the launch traced here: 47.3 us
  Pallas kernels  25.3 us (53%)
  starting transfers between devices  20.8 us (43%)
  waiting for transfers between devices  1.12 us (2%)
    pallas_call x9, Pallas kernels, call(): pl.pallas_call(kernel, out_shape=[jax.ShapeDtypeStruct(*o) for o in outs]...  25.3 us
    ppermute x20, starting transfers between devices, trade(): lax.ppermute(m, axis, links)  20.8 us
    ppermute x20, waiting for transfers between devices, trade(): lax.ppermute(m, axis, links)  1.12 us
  transfers between devices with their start and end apart: 20, of which 4 were waited for; matrix products, arithmetic and copies ran while one was open for 0% of the time, Pallas kernels for 15%

profile of v4, /device:TPU:1, one launch (start us, length us, event | category | flops | bytes accessed | tf_op | source)
XLA Modules:
  0.0 47.3 jit_solution(2527482116688492086)
XLA Ops:
  0.0 2.0 %shard_map.100 = (f32[504,128]{1,0:T(8,128)S(1)}, f32[9,9,3,128]{3,2,1,0:T(4,128)S(1)}, f32[9,9,4,128]{3,2,1,0:T(4,128)S(1)}, f32[9,9,4,128]{3,2,1,0:T(4,128)S(1...) custom-call(f32[504,128]{1,0:T(8,128)} %bitcast.7, ...), custom_call_target="tpu_custom_call" | custom-call | flops 1073741824 | bytes 2097152 | tf_op jit(solution)/shard_map/pallas_call | solution.py:532
  2.0 4.2 %collective-permute-start = (f32[56,128]{1,0:T(8,128)S(1)}, f32[56,128]{1,0:T(8,128)S(1)}, u32[]{:S(2)}, u32[]{:S(2)}) collective-permute-start(f32[56,128]{1,0:T(8,128)S(1)} %get-tuple-element.79), channel_id=1, source_target_pairs={{8,16},{16,8},{24,0},{0,24},{9,17},{17,9},{25,1},{1,25},{10,18},{1... | collective-permute-start | bytes 86024 | tf_op jit(solution)/shard_map/ppermute | solution.py:576
  6.2 2.1 %collective-permute-start.1 = (f32[56,128]{1,0:T(8,128)S(1)}, f32[56,128]{1,0:T(8,128)S(1)}, u32[]{:S(2)}, u32[]{:S(2)}) collective-permute-start(f32[56,128]{1,0:T(8,128)S(1)} %get-tuple-element.80), channel_id=1, source_target_pairs={{1,2},{2,1},{3,0},{0,3},{5,6},{6,5},{7,4},{4,7},{9,10},{10,9},{11,... | collective-permute-start | bytes 86024 | tf_op jit(solution)/shard_map/ppermute | solution.py:576
  8.3 1.2 %collective-permute-start.3 = (f32[56,128]{1,0:T(8,128)S(1)}, f32[56,128]{1,0:T(8,128)S(1)}, u32[]{:S(2)}, u32[]{:S(2)}) collective-permute-start(f32[56,128]{1,0:T(8,128)S(1)} %get-tuple-element.82), channel_id=1, source_target_pairs={{0,4},{4,0},{1,5},{5,1},{2,6},{6,2},{3,7},{7,3},{8,12},{12,8},{9,1... | collective-permute-start | bytes 86024 | tf_op jit(solution)/shard_map/ppermute | solution.py:576
  9.6 2.1 %shard_map.101 = (bf16[168,192]{1,0:T(8,128)(2,1)S(1)}, bf16[168,192]{1,0:T(8,128)(2,1)S(1)}, bf16[56,384]{1,0:T(8,128)(2,1)S(1)}, bf16[256,512]{1,0:T(8,128)(2,...) custom-call(f32[3,56,56]{2,1,0:T(8,128)S(1)} %get-tuple-element.84.r, ...), custom_call_target="tpu_custom_call" | custom-call | flops 1073741824 | bytes 2097152 | tf_op jit(solution)/shard_map/pallas_call | solution.py:532
  11.6 0.0 collective-permute-done.refs_0_
  11.6 0.0 collective-permute-done.1.refs_1_
  11.7 0.0 collective-permute-done.3.refs_3_
  11.7 0.0 collective-permute-done.4.refs_4_
  11.7 3.7 %shard_map.102 = (f32[280,128]{1,0:T(8,128)S(1)}, f32[280,128]{1,0:T(8,128)S(1)}, bf16[192,640]{1,0:T(8,128)(2,1)S(1)}, f32[96,640]{1,0:T(8,128)S(1)}, bf16[448,...) custom-call(f32[56,128]{1,0:T(8,128)S(1)} %collective-permute-done.r, ...), custom_call_target="tpu_custom_call" | custom-call | flops 1073741824 | bytes 2097152 | tf_op jit(solution)/shard_map/pallas_call | solution.py:532
  15.4 0.5 %collective-permute-start.5 = (f32[56,128]{1,0:T(8,128)S(1)}, f32[56,128]{1,0:T(8,128)S(1)}, u32[]{:S(2)}, u32[]{:S(2)}) collective-permute-start(f32[56,128]{1,0:T(8,128)S(1)} %get-tuple-element.104), channel_id=1, source_target_pairs={{8,16},{16,8},{24,0},{0,24},{9,17},{17,9},{25,1},{1,25},{10,18},{1... | collective-permute-start | bytes 86024 | tf_op jit(solution)/shard_map/ppermute | solution.py:576
  15.9 2.1 %collective-permute-start.6 = (f32[56,128]{1,0:T(8,128)S(1)}, f32[56,128]{1,0:T(8,128)S(1)}, u32[]{:S(2)}, u32[]{:S(2)}) collective-permute-start(f32[56,128]{1,0:T(8,128)S(1)} %get-tuple-element.105), channel_id=1, source_target_pairs={{1,2},{2,1},{3,0},{0,3},{5,6},{6,5},{7,4},{4,7},{9,10},{10,9},{11,... | collective-permute-start | bytes 86024 | tf_op jit(solution)/shard_map/ppermute | solution.py:576
  18.0 1.2 %collective-permute-start.8 = (f32[56,128]{1,0:T(8,128)S(1)}, f32[56,128]{1,0:T(8,128)S(1)}, u32[]{:S(2)}, u32[]{:S(2)}) collective-permute-start(f32[56,128]{1,0:T(8,128)S(1)} %get-tuple-element.107), channel_id=1, source_target_pairs={{0,4},{4,0},{1,5},{5,1},{2,6},{6,2},{3,7},{7,3},{8,12},{12,8},{9,1... | collective-permute-start | bytes 86024 | tf_op jit(solution)/shard_map/ppermute | solution.py:576
  19.2 1.4 %shard_map.103 = (f32[504,128]{1,0:T(8,128)S(1)}, f32[504,128]{1,0:T(8,128)S(1)}, f32[280,128]{1,0:T(8,128)S(1)}) custom-call(bf16[192,640]{1,0:T(8,128)(2,1)S(1)} %get-tuple-element.109.refs_0_, f32[96,640]{1,0:T(8,128)S(1)} %get-tuple-element.110.refs_1_, bf16[448,256]{1,0:T(8,128)(2,1)S(1)} %get-tuple-element.111.refs_2_, ...), custom_call_target="tpu_custom_call" | custom-call | flops 1073741824 | bytes 2097152 | tf_op jit(solution)/shard_map/pallas_call | solution.py:532
  20.6 0.0 collective-permute-done.5.refs_0_
  20.6 0.6 %collective-permute-done.7.refs_2_ = f32[56,128]{1,0:T(8,128)S(1)} collective-permute-done((f32[56,128]{1,0:T(8,128)S(1)}, f32[56,128]{1,0:T(8,128)S(1)}, u32[]{:S(2)}, u32[]{:S(2)}) %collective-permute-start.7) | collective-permute-done | bytes 28704 | tf_op jit(solution)/shard_map/ppermute | solution.py:576
  21.2 0.0 collective-permute-done.8.refs_3_
  21.2 3.6 %shard_map.104 = (f32[280,128]{1,0:T(8,128)S(1)}, f32[280,128]{1,0:T(8,128)S(1)}, bf16[192,640]{1,0:T(8,128)(2,1)S(1)}, f32[96,640]{1,0:T(8,128)S(1)}, bf16[448,...) custom-call(f32[56,128]{1,0:T(8,128)S(1)} %collective-permute-done.5, ...), custom_call_target="tpu_custom_call" | custom-call | flops 1073741824 | bytes 2097152 | tf_op jit(solution)/shard_map/pallas_call | solution.py:532
  24.9 2.0 %collective-permute-start.10 = (f32[56,128]{1,0:T(8,128)S(1)}, f32[56,128]{1,0:T(8,128)S(1)}, u32[]{:S(2)}, u32[]{:S(2)}) collective-permute-start(f32[56,128]{1,0:T(8,128)S(1)} %get-tuple-element.122), channel_id=1, source_target_pairs={{8,16},{16,8},{24,0},{0,24},{9,17},{17,9},{25,1},{1,25},{10,18},{1... | collective-permute-start | bytes 86024 | tf_op jit(solution)/shard_map/ppermute | solution.py:576
  26.8 2.4 %collective-permute-start.11 = (f32[56,128]{1,0:T(8,128)S(1)}, f32[56,128]{1,0:T(8,128)S(1)}, u32[]{:S(2)}, u32[]{:S(2)}) collective-permute-start(f32[56,128]{1,0:T(8,128)S(1)} %get-tuple-element.123), channel_id=1, source_target_pairs={{1,2},{2,1},{3,0},{0,3},{5,6},{6,5},{7,4},{4,7},{9,10},{10,9},{11,... | collective-permute-start | bytes 86024 | tf_op jit(solution)/shard_map/ppermute | solution.py:576
  29.3 1.1 %collective-permute-start.13 = (f32[56,128]{1,0:T(8,128)S(1)}, f32[56,128]{1,0:T(8,128)S(1)}, u32[]{:S(2)}, u32[]{:S(2)}) collective-permute-start(f32[56,128]{1,0:T(8,128)S(1)} %get-tuple-element.125), channel_id=1, source_target_pairs={{0,4},{4,0},{1,5},{5,1},{2,6},{6,2},{3,7},{7,3},{8,12},{12,8},{9,1... | collective-permute-start | bytes 86024 | tf_op jit(solution)/shard_map/ppermute | solution.py:576
  30.3 1.6 %shard_map.105 = (f32[6,504,128]{2,1,0:T(8,128)S(1)}, f32[504,128]{1,0:T(8,128)S(1)}, f32[280,128]{1,0:T(8,128)S(1)}) custom-call(bf16[192,640]{1,0:T(8,128)(2,1)S(1)} %get-tuple-element.127.refs_0_, f32[96,640]{1,0:T(8,128)S(1)} %get-tuple-element.128.refs_1_, bf16[448,256]{1,0:T(8,128)(2,1)S(1)} %get-tuple-element.129.refs_2_, ...), custom_call_target="tpu_custom_call" | custom-call | flops 1073741824 | bytes 2097152 | tf_op jit(solution)/shard_map/pallas_call | solution.py:532
  32.0 0.3 collective-permute-done.12.refs_2_
  32.3 0.1 collective-permute-done.13.refs_3_
  32.4 3.7 %shard_map.106 = (f32[280,128]{1,0:T(8,128)S(1)}, f32[280,128]{1,0:T(8,128)S(1)}, bf16[192,640]{1,0:T(8,128)(2,1)S(1)}, f32[96,640]{1,0:T(8,128)S(1)}, bf16[448,...) custom-call(f32[56,128]{1,0:T(8,128)S(1)} %collective-permute-done.1, ...), custom_call_target="tpu_custom_call" | custom-call | flops 1073741824 | bytes 2097152 | tf_op jit(solution)/shard_map/pallas_call | solution.py:532
  36.1 1.1 %collective-permute-start.15 = (f32[56,128]{1,0:T(8,128)S(1)}, f32[56,128]{1,0:T(8,128)S(1)}, u32[]{:S(2)}, u32[]{:S(2)}) collective-permute-start(f32[56,128]{1,0:T(8,128)S(1)} %get-tuple-element.136), channel_id=1, source_target_pairs={{8,16},{16,8},{24,0},{0,24},{9,17},{17,9},{25,1},{1,25},{10,18},{1... | collective-permute-start | bytes 86024 | tf_op jit(solution)/shard_map/ppermute | solution.py:576
  37.2 1.6 %collective-permute-start.16 = (f32[56,128]{1,0:T(8,128)S(1)}, f32[56,128]{1,0:T(8,128)S(1)}, u32[]{:S(2)}, u32[]{:S(2)}) collective-permute-start(f32[56,128]{1,0:T(8,128)S(1)} %get-tuple-element.137), channel_id=1, source_target_pairs={{1,2},{2,1},{3,0},{0,3},{5,6},{6,5},{7,4},{4,7},{9,10},{10,9},{11,... | collective-permute-start | bytes 86024 | tf_op jit(solution)/shard_map/ppermute | solution.py:576
  38.8 0.2 collective-permute-start.17
  39.0 1.0 %collective-permute-start.18 = (f32[56,128]{1,0:T(8,128)S(1)}, f32[56,128]{1,0:T(8,128)S(1)}, u32[]{:S(2)}, u32[]{:S(2)}) collective-permute-start(f32[56,128]{1,0:T(8,128)S(1)} %get-tuple-element.139), channel_id=1, source_target_pairs={{0,4},{4,0},{1,5},{5,1},{2,6},{6,2},{3,7},{7,3},{8,12},{12,8},{9,1... | collective-permute-start | bytes 86024 | tf_op jit(solution)/shard_map/ppermute | solution.py:576
  40.0 2.2 %shard_map.107 = (f32[504,128]{1,0:T(8,128)S(1)}, f32[6,504,128]{2,1,0:T(8,128)S(1)}, f32[504,128]{1,0:T(8,128)S(1)}, f32[280,128]{1,0:T(8,128)}) custom-call(bf16[192,640]{1,0:T(8,128)(2,1)S(1)} %get-tuple-element.141.refs_0_, f32[96,640]{1,0:T(8,128)S(1)} %get-tuple-element.142.refs_1_, bf16[448,256]{1,0:T(8,128)(2,1)S(1)} %get-tuple-element.143.refs_2_, ...), custom_call_target="tpu_custom_call" | custom-call | flops 1073741824 | bytes 2097152 | tf_op jit(solution)/shard_map/pallas_call | solution.py:532
  42.2 0.1 collective-permute-done.17.refs_2_
  42.3 5.0 %shard_map.108 = f32[504,128]{1,0:T(8,128)} custom-call(f32[56,128]{1,0:T(8,128)S(1)} %collective-permute-done.15.refs_0_, f32[56,128]{1,0:T(8,128)S(1)} %collective-permute-done.16.refs_1_, f32[56,128]{1,0:T(8,128)S(1)} %collective-permute-done.17.refs_2_, f32[56,128]{1,0:T(8,128)S(1)} %collective-permute-done.18.refs_3_, ...), custom_call_target="tpu_custom_call" | custom-call | flops 1073741824 | bytes 2097152 | tf_op jit(solution)/shard_map/pallas_call | solution.py:532
  (18 shorter events, 0.0 us)
Async XLA Ops:
  2.0 9.6 %collective-permute-start = (f32[56,128]{1,0:T(8,128)S(1)}, f32[56,128]{1,0:T(8,128)S(1)}, u32[]{:S(2)}, u32[]{:S(2)}) collective-permute-start(f32[56,128]{1,0:T(8,128)S(1)} %get-tuple-element.79), channel_id=1, source_target_pairs={{8,16},{16,8},{24,0},{0,24},{9,17},{17,9},{25,1},{1,25},{10,18},{1... | collective-permute-start | bytes 86024 | tf_op jit(solution)/shard_map/ppermute | solution.py:576
  6.2 5.4 %collective-permute-start.1 = (f32[56,128]{1,0:T(8,128)S(1)}, f32[56,128]{1,0:T(8,128)S(1)}, u32[]{:S(2)}, u32[]{:S(2)}) collective-permute-start(f32[56,128]{1,0:T(8,128)S(1)} %get-tuple-element.80), channel_id=1, source_target_pairs={{1,2},{2,1},{3,0},{0,3},{5,6},{6,5},{7,4},{4,7},{9,10},{10,9},{11,... | collective-permute-start | bytes 86024 | tf_op jit(solution)/shard_map/ppermute | solution.py:576
  8.3 3.3 %collective-permute-start.2 = (f32[56,128]{1,0:T(8,128)S(1)}, f32[56,128]{1,0:T(8,128)S(1)}, u32[]{:S(2)}, u32[]{:S(2)}) collective-permute-start(f32[56,128]{1,0:T(8,128)S(1)} %get-tuple-element.81), channel_id=1, source_target_pairs={{0,8},{8,0},{16,24},{24,16},{1,9},{9,1},{17,25},{25,17},{2,10},{10... | collective-permute-start | bytes 86024 | tf_op jit(solution)/shard_map/ppermute | solution.py:576
  8.3 3.3 %collective-permute-start.3 = (f32[56,128]{1,0:T(8,128)S(1)}, f32[56,128]{1,0:T(8,128)S(1)}, u32[]{:S(2)}, u32[]{:S(2)}) collective-permute-start(f32[56,128]{1,0:T(8,128)S(1)} %get-tuple-element.82), channel_id=1, source_target_pairs={{0,4},{4,0},{1,5},{5,1},{2,6},{6,2},{3,7},{7,3},{8,12},{12,8},{9,1... | collective-permute-start | bytes 86024 | tf_op jit(solution)/shard_map/ppermute | solution.py:576
  9.5 2.1 %collective-permute-start.4 = (f32[56,128]{1,0:T(8,128)S(1)}, f32[56,128]{1,0:T(8,128)S(1)}, u32[]{:S(2)}, u32[]{:S(2)}) collective-permute-start(f32[56,128]{1,0:T(8,128)S(1)} %get-tuple-element.83), channel_id=1, source_target_pairs={{0,1},{1,0},{2,3},{3,2},{4,5},{5,4},{6,7},{7,6},{8,9},{9,8},{10,11... | collective-permute-start | bytes 86024 | tf_op jit(solution)/shard_map/ppermute | solution.py:576
  15.4 5.3 %collective-permute-start.5 = (f32[56,128]{1,0:T(8,128)S(1)}, f32[56,128]{1,0:T(8,128)S(1)}, u32[]{:S(2)}, u32[]{:S(2)}) collective-permute-start(f32[56,128]{1,0:T(8,128)S(1)} %get-tuple-element.104), channel_id=1, source_target_pairs={{8,16},{16,8},{24,0},{0,24},{9,17},{17,9},{25,1},{1,25},{10,18},{1... | collective-permute-start | bytes 86024 | tf_op jit(solution)/shard_map/ppermute | solution.py:576
  15.9 4.8 %collective-permute-start.6 = (f32[56,128]{1,0:T(8,128)S(1)}, f32[56,128]{1,0:T(8,128)S(1)}, u32[]{:S(2)}, u32[]{:S(2)}) collective-permute-start(f32[56,128]{1,0:T(8,128)S(1)} %get-tuple-element.105), channel_id=1, source_target_pairs={{1,2},{2,1},{3,0},{0,3},{5,6},{6,5},{7,4},{4,7},{9,10},{10,9},{11,... | collective-permute-start | bytes 86024 | tf_op jit(solution)/shard_map/ppermute | solution.py:576
  18.0 3.2 %collective-permute-start.7 = (f32[56,128]{1,0:T(8,128)S(1)}, f32[56,128]{1,0:T(8,128)S(1)}, u32[]{:S(2)}, u32[]{:S(2)}) collective-permute-start(f32[56,128]{1,0:T(8,128)S(1)} %get-tuple-element.106), channel_id=1, source_target_pairs={{0,8},{8,0},{16,24},{24,16},{1,9},{9,1},{17,25},{25,17},{2,10},{10... | collective-permute-start | bytes 86024 | tf_op jit(solution)/shard_map/ppermute | solution.py:576
  18.0 3.2 %collective-permute-start.8 = (f32[56,128]{1,0:T(8,128)S(1)}, f32[56,128]{1,0:T(8,128)S(1)}, u32[]{:S(2)}, u32[]{:S(2)}) collective-permute-start(f32[56,128]{1,0:T(8,128)S(1)} %get-tuple-element.107), channel_id=1, source_target_pairs={{0,4},{4,0},{1,5},{5,1},{2,6},{6,2},{3,7},{7,3},{8,12},{12,8},{9,1... | collective-permute-start | bytes 86024 | tf_op jit(solution)/shard_map/ppermute | solution.py:576
  19.2 2.0 %collective-permute-start.9 = (f32[56,128]{1,0:T(8,128)S(1)}, f32[56,128]{1,0:T(8,128)S(1)}, u32[]{:S(2)}, u32[]{:S(2)}) collective-permute-start(f32[56,128]{1,0:T(8,128)S(1)} %get-tuple-element.108), channel_id=1, source_target_pairs={{0,1},{1,0},{2,3},{3,2},{4,5},{5,4},{6,7},{7,6},{8,9},{9,8},{10,11... | collective-permute-start | bytes 86024 | tf_op jit(solution)/shard_map/ppermute | solution.py:576
  24.9 7.1 %collective-permute-start.10 = (f32[56,128]{1,0:T(8,128)S(1)}, f32[56,128]{1,0:T(8,128)S(1)}, u32[]{:S(2)}, u32[]{:S(2)}) collective-permute-start(f32[56,128]{1,0:T(8,128)S(1)} %get-tuple-element.122), channel_id=1, source_target_pairs={{8,16},{16,8},{24,0},{0,24},{9,17},{17,9},{25,1},{1,25},{10,18},{1... | collective-permute-start | bytes 86024 | tf_op jit(solution)/shard_map/ppermute | solution.py:576
  26.8 5.1 %collective-permute-start.11 = (f32[56,128]{1,0:T(8,128)S(1)}, f32[56,128]{1,0:T(8,128)S(1)}, u32[]{:S(2)}, u32[]{:S(2)}) collective-permute-start(f32[56,128]{1,0:T(8,128)S(1)} %get-tuple-element.123), channel_id=1, source_target_pairs={{1,2},{2,1},{3,0},{0,3},{5,6},{6,5},{7,4},{4,7},{9,10},{10,9},{11,... | collective-permute-start | bytes 86024 | tf_op jit(solution)/shard_map/ppermute | solution.py:576
  29.3 3.0 %collective-permute-start.12 = (f32[56,128]{1,0:T(8,128)S(1)}, f32[56,128]{1,0:T(8,128)S(1)}, u32[]{:S(2)}, u32[]{:S(2)}) collective-permute-start(f32[56,128]{1,0:T(8,128)S(1)} %get-tuple-element.124), channel_id=1, source_target_pairs={{0,8},{8,0},{16,24},{24,16},{1,9},{9,1},{17,25},{25,17},{2,10},{10... | collective-permute-start | bytes 86024 | tf_op jit(solution)/shard_map/ppermute | solution.py:576
  29.3 3.1 %collective-permute-start.13 = (f32[56,128]{1,0:T(8,128)S(1)}, f32[56,128]{1,0:T(8,128)S(1)}, u32[]{:S(2)}, u32[]{:S(2)}) collective-permute-start(f32[56,128]{1,0:T(8,128)S(1)} %get-tuple-element.125), channel_id=1, source_target_pairs={{0,4},{4,0},{1,5},{5,1},{2,6},{6,2},{3,7},{7,3},{8,12},{12,8},{9,1... | collective-permute-start | bytes 86024 | tf_op jit(solution)/shard_map/ppermute | solution.py:576
  30.3 2.1 %collective-permute-start.14 = (f32[56,128]{1,0:T(8,128)S(1)}, f32[56,128]{1,0:T(8,128)S(1)}, u32[]{:S(2)}, u32[]{:S(2)}) collective-permute-start(f32[56,128]{1,0:T(8,128)S(1)} %get-tuple-element.126), channel_id=1, source_target_pairs={{0,1},{1,0},{2,3},{3,2},{4,5},{5,4},{6,7},{7,6},{8,9},{9,8},{10,11... | collective-permute-start | bytes 86024 | tf_op jit(solution)/shard_map/ppermute | solution.py:576
  36.1 6.1 %collective-permute-start.15 = (f32[56,128]{1,0:T(8,128)S(1)}, f32[56,128]{1,0:T(8,128)S(1)}, u32[]{:S(2)}, u32[]{:S(2)}) collective-permute-start(f32[56,128]{1,0:T(8,128)S(1)} %get-tuple-element.136), channel_id=1, source_target_pairs={{8,16},{16,8},{24,0},{0,24},{9,17},{17,9},{25,1},{1,25},{10,18},{1... | collective-permute-start | bytes 86024 | tf_op jit(solution)/shard_map/ppermute | solution.py:576
  37.2 5.0 %collective-permute-start.16 = (f32[56,128]{1,0:T(8,128)S(1)}, f32[56,128]{1,0:T(8,128)S(1)}, u32[]{:S(2)}, u32[]{:S(2)}) collective-permute-start(f32[56,128]{1,0:T(8,128)S(1)} %get-tuple-element.137), channel_id=1, source_target_pairs={{1,2},{2,1},{3,0},{0,3},{5,6},{6,5},{7,4},{4,7},{9,10},{10,9},{11,... | collective-permute-start | bytes 86024 | tf_op jit(solution)/shard_map/ppermute | solution.py:576
  38.8 3.6 %collective-permute-start.17 = (f32[56,128]{1,0:T(8,128)S(1)}, f32[56,128]{1,0:T(8,128)S(1)}, u32[]{:S(2)}, u32[]{:S(2)}) collective-permute-start(f32[56,128]{1,0:T(8,128)S(1)} %get-tuple-element.138), channel_id=1, source_target_pairs={{0,8},{8,0},{16,24},{24,16},{1,9},{9,1},{17,25},{25,17},{2,10},{10... | collective-permute-start | bytes 86024 | tf_op jit(solution)/shard_map/ppermute | solution.py:576
  39.0 3.3 %collective-permute-start.18 = (f32[56,128]{1,0:T(8,128)S(1)}, f32[56,128]{1,0:T(8,128)S(1)}, u32[]{:S(2)}, u32[]{:S(2)}) collective-permute-start(f32[56,128]{1,0:T(8,128)S(1)} %get-tuple-element.139), channel_id=1, source_target_pairs={{0,4},{4,0},{1,5},{5,1},{2,6},{6,2},{3,7},{7,3},{8,12},{12,8},{9,1... | collective-permute-start | bytes 86024 | tf_op jit(solution)/shard_map/ppermute | solution.py:576
  40.0 2.3 %collective-permute-start.19 = (f32[56,128]{1,0:T(8,128)S(1)}, f32[56,128]{1,0:T(8,128)S(1)}, u32[]{:S(2)}, u32[]{:S(2)}) collective-permute-start(f32[56,128]{1,0:T(8,128)S(1)} %get-tuple-element.140), channel_id=1, source_target_pairs={{0,1},{1,0},{2,3},{3,2},{4,5},{5,4},{6,7},{7,6},{8,9},{9,8},{10,11... | collective-permute-start | bytes 86024 | tf_op jit(solution)/shard_map/ppermute | solution.py:576
